TPU v7x, 512 devices: a whole 4x8x8 slice. The times are simulated.
512 devices in a mesh: sims: 32 (over z_lo, y, core), sites: 16 (over x, z_hi).
Axes of the slice: x: 4, y: 8, z: 8 (z_hi: 4, z_lo: 2; z = z_hi * 2 + z_lo), core: 2. Of those that a mesh axis runs over, the one named last changes fastest.
Arguments:
- genotypes: int32 [32, 64, 8192], P('sims', None, 'sites'), may hold values from 0 to 1
- key_prior: bfloat16 [32, 2048], P('sims', 'sites'), may hold values from -300 to 300
- band_reach: int32 [32], P('sims'), may hold values from 128 to 512, as said below
- cotangent: bfloat16 [32, 2048, 512], P('sims', 'sites'), may hold values from -0.09375 to 0.09375
- conv_weight: float32 [4, 64], replicated, may hold values from -3 to 3
- conv_bias: float32 [64], replicated, may hold values from -3 to 3
- mix_weight: float32 [3, 64, 64], replicated, may hold values from -0.4375 to 0.4375
- embed_weight: float32 [64, 512], replicated, may hold values from -0.75 to 0.75
- norm_gain: float32 [512], replicated, may hold values from 0.5 to 1.5
- attn_weight: bfloat16 [4, 512, 512], replicated, may hold values from -0.25 to 0.25
Outputs:
- grad_attention: float32 [1048576], P(('sims', 'sites'))
- grad_conv: float32 [4, 64], replicated
- grad_bias: float32 [64], replicated
- grad_mix: float32 [3, 64, 64], replicated
- grad_embed: float32 [64, 512], replicated
- grad_gain: float32 [512], replicated
Inputs may be any that keep to these rules, and one draw needn't show every extreme that they name: `band_reach`: some evolution has reach exactly 512 in every draw.
All inputs are finite; a program needn't handle non-finite values.
Results may differ from a plain program's by a relative error of at most 0.017.
Values may be sent and summed in bfloat16 or wider, within the bound.
A program may use at most 64 MiB of HBM per device.

v0:
```python
import jax
import jax.numpy as jnp
from jax import lax
from jax.sharding import PartitionSpec as P

HEADS = 8
HEAD_DIM = 64
BAND = 512


HIGH = lax.Precision.HIGHEST
EPS = 1e-06


def extended(cells, sides, width):
    for axis, dim in sides:
        count = lax.axis_size(axis)
        head = lax.slice_in_dim(cells, 0, width, axis=dim)
        tail = lax.slice_in_dim(cells, cells.shape[dim] - width, cells.shape[dim], axis=dim)
        cells = jnp.concatenate(
            [
                lax.ppermute(tail, axis, [(i, (i + 1) % count) for i in range(count)]),
                cells,
                lax.ppermute(head, axis, [((i + 1) % count, i) for i in range(count)]),
            ],
            axis=dim,
        )
    return cells


def from_behind(value, axis, steps):
    count = lax.axis_size(axis)
    pairs = [(source, (source + steps) % count) for source in range(count)]
    return lax.ppermute(value, axis, pairs)


def silu_slope(value):
    sigma = jax.nn.sigmoid(value)
    return sigma * (1.0 + value * (1.0 - sigma))


def block_offsets(count, reach_blocks):
    chosen = []
    taken = []
    for distance in range(reach_blocks + 1):
        for offset in (distance, -distance):
            if offset % count not in taken:
                taken.append(offset % count)
                chosen.append(offset)
    return chosen


def split_heads(array, heads):
    return array.reshape(array.shape[0], array.shape[1], heads, array.shape[2] // heads)


def band_scores(query, keys, prior, query_places, key_places, limit, cycle_tokens, factor):
    scores = jnp.einsum("sqhe,skhe->shqk", query, keys, preferred_element_type=jnp.float32) * factor
    scores = scores + prior.astype(jnp.float32)[:, None, None, :]
    apart = (key_places[None, :] - query_places[:, None]) % cycle_tokens
    apart = jnp.minimum(apart, cycle_tokens - apart)
    inside = apart[None, None] <= limit[:, None, None, None]
    return (scores, inside)


def per_device(
    genotypes,
    key_prior,
    band_reach,
    cotangent,
    conv_weight,
    conv_bias,
    mix_weight,
    embed_weight,
    norm_gain,
    attn_weight,
):
    sims, haps, sites = genotypes.shape
    patch = conv_weight.shape[0]
    local = sites // patch
    width = attn_weight.shape[1]
    heads = HEADS
    factor = HEAD_DIM ** (-0.5)
    count = lax.axis_size("sites")
    cycle_tokens = local * count
    place = lax.axis_index("sites")
    ordinal = jnp.arange(local, dtype=jnp.int32)
    patches = genotypes.astype(jnp.float32).reshape(sims, haps, local, patch)
    pre = (
        jnp.einsum("shtk,kc->shct", patches, conv_weight, precision=HIGH)
        + conv_bias[None, None, :, None]
    )
    pooled = jnp.mean(jax.nn.silu(pre), axis=1)
    pooled_wide = extended(pooled, (("sites", 2),), 1)
    mixed = jnp.zeros((sims, mix_weight.shape[2], local), jnp.float32)
    for shift_by in (-1, 0, 1):
        mixed = mixed + jnp.einsum(
            "co,sct->sot",
            mix_weight[shift_by + 1],
            pooled_wide[:, :, 1 + shift_by : 1 + shift_by + local],
            precision=HIGH,
        )
    activated = jax.nn.silu(mixed)
    embedded = jnp.einsum("sct,cd->std", activated, embed_weight, precision=HIGH).astype(
        jnp.bfloat16
    )
    wide = embedded.astype(jnp.float32)
    inverse = lax.rsqrt(jnp.mean(wide * wide, axis=2, keepdims=True) + EPS)
    normed = (wide * inverse * norm_gain).astype(jnp.bfloat16)
    query = jnp.einsum(
        "std,de->ste", normed, attn_weight[0], preferred_element_type=jnp.float32
    ).astype(jnp.bfloat16)
    keys = jnp.einsum(
        "std,de->ste", normed, attn_weight[1], preferred_element_type=jnp.float32
    ).astype(jnp.bfloat16)
    values = jnp.einsum(
        "std,de->ste", normed, attn_weight[2], preferred_element_type=jnp.float32
    ).astype(jnp.bfloat16)
    query_heads = split_heads(query, heads)
    key_heads = split_heads(keys, heads)
    value_heads = split_heads(values, heads)
    reach_blocks = -(-BAND // local)
    offsets = block_offsets(count, reach_blocks)
    blocks = {0: (key_heads, value_heads, key_prior)}
    for offset in offsets[1:]:
        blocks[offset] = from_behind((key_heads, value_heads, key_prior), "sites", -offset)
    key_cat = jnp.concatenate([blocks[offset][0] for offset in offsets], axis=1)
    value_cat = jnp.concatenate([blocks[offset][1] for offset in offsets], axis=1)
    prior_cat = jnp.concatenate([blocks[offset][2] for offset in offsets], axis=1)
    key_places = jnp.concatenate([(place + offset) % count * local + ordinal for offset in offsets])
    query_places = place * local + ordinal
    scores, inside = band_scores(
        query_heads, key_cat, prior_cat, query_places, key_places, band_reach, cycle_tokens, factor
    )
    row_top = jnp.max(jnp.where(inside, scores, -jnp.inf), axis=-1, keepdims=True)
    lifted = jnp.where(inside, jnp.exp(scores - row_top), 0.0)
    row_total = jnp.sum(lifted, axis=-1, keepdims=True)
    prob = lifted / row_total
    prob_half = prob.astype(jnp.bfloat16)
    attended_full = jnp.einsum(
        "shqk,skhe->sqhe", prob_half, value_cat, preferred_element_type=jnp.float32
    )
    attended = attended_full.astype(jnp.bfloat16).reshape(sims, local, width)
    grad_attended = jnp.einsum(
        "std,ed->ste", cotangent, attn_weight[3], preferred_element_type=jnp.float32
    ).astype(jnp.bfloat16)
    grad_heads = split_heads(grad_attended, heads)
    delta = jnp.einsum("sqhe,sqhe->shq", grad_heads.astype(jnp.float32), attended_full)
    grad_prob = jnp.einsum(
        "sqhe,skhe->shqk", grad_heads, value_cat, preferred_element_type=jnp.float32
    )
    grad_scores = (prob * (grad_prob - delta[..., None]) * factor).astype(jnp.bfloat16)
    grad_query = jnp.einsum(
        "shqk,skhe->sqhe", grad_scores, key_cat, preferred_element_type=jnp.float32
    ).astype(jnp.bfloat16)
    grad_query = grad_query.reshape(sims, local, width)
    key_part = jnp.einsum(
        "shqk,sqhe->skhe", grad_scores, query_heads, preferred_element_type=jnp.float32
    )
    value_part = jnp.einsum(
        "shqk,sqhe->skhe", prob_half, grad_heads, preferred_element_type=jnp.float32
    )
    key_sum = key_part[:, 0:local]
    value_sum = value_part[:, 0:local]
    for position, offset in enumerate(offsets[1:], start=1):
        lower = position * local
        back_keys, back_values = (
            from_behind(
                key_part[:, lower : lower + local].astype(jnp.bfloat16), "sites", offset
            ).astype(jnp.float32),
            from_behind(
                value_part[:, lower : lower + local].astype(jnp.bfloat16), "sites", offset
            ).astype(jnp.float32),
        )
        key_sum = key_sum + back_keys
        value_sum = value_sum + back_values
    grad_keys = key_sum.astype(jnp.bfloat16).reshape(sims, local, width)
    grad_values = value_sum.astype(jnp.bfloat16).reshape(sims, local, width)
    term_query = jnp.einsum("std,ste->de", normed, grad_query, preferred_element_type=jnp.float32)
    term_keys = jnp.einsum("std,ste->de", normed, grad_keys, preferred_element_type=jnp.float32)
    term_values = jnp.einsum("std,ste->de", normed, grad_values, preferred_element_type=jnp.float32)
    term_output = jnp.einsum("std,ste->de", attended, cotangent, preferred_element_type=jnp.float32)
    flat_terms = jnp.stack([term_query, term_keys, term_values, term_output]).reshape(-1)
    grad_attention = lax.psum_scatter(
        flat_terms, ("sims", "sites"), scatter_dimension=0, tiled=True
    )
    grad_normed = jnp.einsum(
        "ste,de->std", grad_query, attn_weight[0], preferred_element_type=jnp.float32
    )
    grad_normed = grad_normed + jnp.einsum(
        "ste,de->std", grad_keys, attn_weight[1], preferred_element_type=jnp.float32
    )
    grad_normed = grad_normed + jnp.einsum(
        "ste,de->std", grad_values, attn_weight[2], preferred_element_type=jnp.float32
    )
    term_gain = jnp.sum(grad_normed * wide * inverse, axis=(0, 1))
    scaled = grad_normed * norm_gain
    grad_embedded = (
        inverse * scaled - wide * inverse**3 * jnp.sum(scaled * wide, axis=2, keepdims=True) / width
    )
    grad_embedded = grad_embedded + cotangent.astype(jnp.float32)
    term_embed = jnp.einsum("sct,std->cd", activated, grad_embedded, precision=HIGH)
    grad_mixed = jnp.einsum(
        "std,od->sot", grad_embedded, embed_weight, precision=HIGH
    ) * silu_slope(mixed)
    mixed_wide = extended(grad_mixed.astype(jnp.bfloat16), (("sites", 2),), 1).astype(
        grad_mixed.dtype
    )
    mix_terms = []
    grad_pooled = jnp.zeros(pooled.shape, jnp.float32)
    for shift_by in (-1, 0, 1):
        mix_terms.append(
            jnp.einsum(
                "sct,sot->co",
                pooled_wide[:, :, 1 + shift_by : 1 + shift_by + local],
                grad_mixed,
                precision=HIGH,
            )
        )
        grad_pooled = grad_pooled + jnp.einsum(
            "co,sot->sct",
            mix_weight[shift_by + 1],
            mixed_wide[:, :, 1 - shift_by : 1 - shift_by + local],
            precision=HIGH,
        )
    grad_pre = (grad_pooled / haps)[:, None] * silu_slope(pre)
    term_conv = jnp.einsum("shtk,shct->kc", patches, grad_pre, precision=HIGH)
    term_bias = jnp.sum(grad_pre, axis=(0, 1, 3))
    grad_conv, grad_bias, grad_mix, grad_embed, grad_gain = lax.psum(
        (term_conv, term_bias, jnp.stack(mix_terms), term_embed, term_gain), ("sims", "sites")
    )
    return (grad_attention, grad_conv, grad_bias, grad_mix, grad_embed, grad_gain)


def solution(mesh):
    placed = (
        P("sims", None, "sites"),
        P("sims", "sites"),
        P("sims"),
        P("sims", "sites", None),
        P(),
        P(),
        P(),
        P(),
        P(),
        P(),
    )
    return jax.shard_map(
        per_device,
        mesh=mesh,
        in_specs=placed,
        out_specs=(P(("sims", "sites")), P(), P(), P(), P(), P()),
        check_vma=False,
    )
```

profile of v0, /device:TPU:6, one launch (start us, length us, event | category | flops | bytes accessed | tf_op | source)
XLA Modules:
  0.0 572.1 jit_solution(4122395832519361176)
XLA Ops:
  7.2 11.2 %collective-permute-start.10 = (bf16[1,128]{1,0:T(2,128)(2,1)}, bf16[1,128]{1,0:T(2,128)(2,1)S(1)}, u32[]{:S(2)}, u32[]{:S(2)}) collective-permute-start(bf16[1,128]{1,0:T(2,128)(2,1)} %param.11), channel_id=1, source_target_pairs={{0,15},{1,0},{2,1},{3,2},{4,3},{5,4},{6,5},{7,6},{8,7},{9,8},{10,9... | collective-permute-start | bytes 776 | tf_op jit(solution)/shard_map/ppermute | solution.py:34
  18.4 1.9 collective-permute-start.11
  20.4 4.8 collective-permute-start.12
  25.2 5.0 collective-permute-start.13
  31.4 4.5 fusion.16
  35.9 7.8 %collective-permute-start.1 = (f32[1,64,1]{2,1,0:T(8,128)S(1)}, f32[1,64,1]{2,1,0:T(8,128)S(1)}, u32[]{:S(2)}, u32[]{:S(2)}) collective-permute-start(f32[1,64,1]{2,1,0:T(8,128)S(1)} %get-tuple-element.31), channel_id=1, source_target_pairs={{1,0},{2,1},{3,2},{4,3},{5,4},{6,5},{7,6},{8,7},{9,8},{10,9},{11,1... | collective-permute-start | bytes 776 | tf_op jit(solution)/shard_map/ppermute | solution.py:24
  45.9 1.4 dynamic-update-slice.9
  47.4 1.9 collective-permute-start
  49.6 6.6 %collective-permute-done = f32[1,64,1]{2,1,0:T(8,128)S(1)} collective-permute-done((f32[1,64,1]{2,1,0:T(8,128)S(1)}, f32[1,64,1]{2,1,0:T(8,128)S(1)}, u32[]{:S(2)}, u32[]{:S(2)}) %collective-permute-start) | collective-permute-done | bytes 288 | tf_op jit(solution)/shard_map/ppermute | solution.py:22
  56.2 1.9 collective-permute-start.14
  63.8 6.4 %collective-permute-start.15 = (bf16[1,128]{1,0:T(2,128)(2,1)S(1)}, bf16[1,128]{1,0:T(2,128)(2,1)S(1)}, u32[]{:S(2)}, u32[]{:S(2)}) collective-permute-start(bf16[1,128]{1,0:T(2,128)(2,1)S(1)} %copy-done.16), channel_id=1, source_target_pairs={{0,3},{1,4},{2,5},{3,6},{4,7},{5,8},{6,9},{7,10},{8,11},{9,12},{10... | collective-permute-start | bytes 776 | tf_op jit(solution)/shard_map/ppermute | solution.py:34
  70.2 1.4 dynamic-update-slice.10
  71.7 2.0 collective-permute-start.16
  73.7 1.4 dynamic-update-slice.11
  75.2 7.4 %collective-permute-start.17 = (bf16[1,128]{1,0:T(2,128)(2,1)S(1)}, bf16[1,128]{1,0:T(2,128)(2,1)S(1)}, u32[]{:S(2)}, u32[]{:S(2)}) collective-permute-start(bf16[1,128]{1,0:T(2,128)(2,1)S(1)} %copy-done.16), channel_id=1, source_target_pairs={{0,4},{1,5},{2,6},{3,7},{4,8},{5,9},{6,10},{7,11},{8,12},{9,13},{1... | collective-permute-start | bytes 776 | tf_op jit(solution)/shard_map/ppermute | solution.py:34
  82.6 1.4 dynamic-update-slice.12
  84.0 2.8 collective-permute-start.18
  88.2 4.0 collective-permute-start.19
  92.2 1.4 dynamic-update-slice.14
  93.7 3.1 collective-permute-start.20
  96.7 1.4 dynamic-update-slice.15
  98.2 5.2 collective-permute-start.2
  104.8 2.8 collective-permute-start.3
  110.8 4.9 collective-permute-start.4
  116.7 1.6 collective-permute-done.3
  118.3 5.0 collective-permute-start.5
  124.2 6.3 %collective-permute-start.6 = (bf16[1,128,8,64]{1,3,2,0:T(8,128)(2,1)}, bf16[1,128,8,64]{1,3,2,0:T(8,128)(2,1)S(1)}, u32[]{:S(2)}, u32[]{:S(2)}) collective-permute-start(bf16[1,128,8,64]{1,3,2,0:T(8,128)(2,1)} %bitcast.17), channel_id=1, source_target_pairs={{0,13},{1,14},{2,15},{3,0},{4,1},{5,2},{6,3},{7,4},{8,5},{9,6},{10... | collective-permute-start | bytes 393224 | tf_op jit(solution)/shard_map/ppermute | solution.py:34
  130.6 4.0 collective-permute-done.5
  134.5 3.5 collective-permute-start.7
  138.1 1.8 collective-permute-done.6
  139.8 1.9 collective-permute-start.8
  141.8 2.9 collective-permute-done.7
  144.7 5.0 collective-permute-start.9
  149.8 7.1 %collective-permute-start.21 = (bf16[1,128,8,64]{1,3,2,0:T(8,128)(2,1)}, bf16[1,128,8,64]{1,3,2,0:T(8,128)(2,1)S(1)}, u32[]{:S(2)}, u32[]{:S(2)}) collective-permute-start(bf16[1,128,8,64]{1,3,2,0:T(8,128)(2,1)} %bitcast.35), channel_id=1, source_target_pairs={{0,2},{1,3},{2,4},{3,5},{4,6},{5,7},{6,8},{7,9},{8,10},{9,11},{10,... | collective-permute-start | bytes 393224 | tf_op jit(solution)/shard_map/ppermute | solution.py:34
  157.0 1.9 collective-permute-start.22
  159.8 1.8 fusion.140
  162.1 6.0 %collective-permute-start.23 = (bf16[1,128,8,64]{1,3,2,0:T(8,128)(2,1)}, bf16[1,128,8,64]{1,3,2,0:T(8,128)(2,1)S(1)}, u32[]{:S(2)}, u32[]{:S(2)}) collective-permute-start(bf16[1,128,8,64]{1,3,2,0:T(8,128)(2,1)} %bitcast.35), channel_id=1, source_target_pairs={{0,3},{1,4},{2,5},{3,6},{4,7},{5,8},{6,9},{7,10},{8,11},{9,12},{10... | collective-permute-start | bytes 393224 | tf_op jit(solution)/shard_map/ppermute | solution.py:34
  169.1 2.8 collective-permute-start.24
  172.9 4.4 collective-permute-start.25
  178.5 1.5 collective-permute-done.25
  184.6 3.7 collective-permute-start.26
  188.4 5.2 collective-permute-start.27
  193.6 4.2 collective-permute-start.28
  197.9 6.4 %collective-permute-start.29 = (bf16[1,128,8,64]{1,3,2,0:T(8,128)(2,1)S(1)}, bf16[1,128,8,64]{1,3,2,0:T(8,128)(2,1)S(1)}, u32[]{:S(2)}, u32[]{:S(2)}) collective-permute-start(bf16[1,128,8,64]{1,3,2,0:T(8,128)(2,1)S(1)} %get-tuple-element.19), channel_id=1, source_target_pairs={{0,14},{1,15},{2,0},{3,1},{4,2},{5,3},{6,4},{7,5},{8,6},{9,7},{10,... | collective-permute-start | bytes 393224 | tf_op jit(solution)/shard_map/ppermute | solution.py:34
  204.3 3.1 collective-permute-start.30
  208.0 4.5 collective-permute-start.31
  212.5 9.1 %collective-permute-start.32 = (bf16[1,128,8,64]{1,3,2,0:T(8,128)(2,1)S(1)}, bf16[1,128,8,64]{1,3,2,0:T(8,128)(2,1)S(1)}, u32[]{:S(2)}, u32[]{:S(2)}) collective-permute-start(bf16[1,128,8,64]{1,3,2,0:T(8,128)(2,1)S(1)} %get-tuple-element.16), channel_id=1, source_target_pairs={{0,4},{1,5},{2,6},{3,7},{4,8},{5,9},{6,10},{7,11},{8,12},{9,13},{1... | collective-permute-start | bytes 393224 | tf_op jit(solution)/shard_map/ppermute | solution.py:34
  221.6 1.9 collective-permute-start.33
  224.2 1.9 collective-permute-start.34
  226.1 6.9 %collective-permute-start.35 = (bf16[1,128,8,64]{1,3,2,0:T(8,128)(2,1)S(1)}, bf16[1,128,8,64]{1,3,2,0:T(8,128)(2,1)S(1)}, u32[]{:S(2)}, u32[]{:S(2)}) collective-permute-start(bf16[1,128,8,64]{1,3,2,0:T(8,128)(2,1)S(1)} %get-tuple-element.29), channel_id=1, source_target_pairs={{0,15},{1,0},{2,1},{3,2},{4,3},{5,4},{6,5},{7,6},{8,7},{9,8},{10,9... | collective-permute-start | bytes 393224 | tf_op jit(solution)/shard_map/ppermute | solution.py:34
  233.1 1.9 collective-permute-start.36
  235.0 8.7 %collective-permute-start.37 = (bf16[1,128,8,64]{1,3,2,0:T(8,128)(2,1)S(1)}, bf16[1,128,8,64]{1,3,2,0:T(8,128)(2,1)S(1)}, u32[]{:S(2)}, u32[]{:S(2)}) collective-permute-start(bf16[1,128,8,64]{1,3,2,0:T(8,128)(2,1)S(1)} %get-tuple-element.27), channel_id=1, source_target_pairs={{0,14},{1,15},{2,0},{3,1},{4,2},{5,3},{6,4},{7,5},{8,6},{9,7},{10,... | collective-permute-start | bytes 393224 | tf_op jit(solution)/shard_map/ppermute | solution.py:34
  243.8 2.8 collective-permute-start.38
  246.8 4.9 collective-permute-start.39
  251.6 8.8 %collective-permute-start.40 = (bf16[1,128,8,64]{1,3,2,0:T(8,128)(2,1)S(1)}, bf16[1,128,8,64]{1,3,2,0:T(8,128)(2,1)S(1)}, u32[]{:S(2)}, u32[]{:S(2)}) collective-permute-start(bf16[1,128,8,64]{1,3,2,0:T(8,128)(2,1)S(1)} %get-tuple-element.24), channel_id=1, source_target_pairs={{0,4},{1,5},{2,6},{3,7},{4,8},{5,9},{6,10},{7,11},{8,12},{9,13},{1... | collective-permute-start | bytes 393224 | tf_op jit(solution)/shard_map/ppermute | solution.py:34
  260.4 1.9 collective-permute-start.41
  262.9 5.6 collective-permute-done.41
  271.7 3.1 copy.63
  275.0 2.0 collective-permute-start.43
  277.0 6.9 %collective-permute-start.42 = (bf16[1,64,1]{2,1,0:T(8,128)(2,1)S(1)}, bf16[1,64,1]{2,1,0:T(8,128)(2,1)S(1)}, u32[]{:S(2)}, u32[]{:S(2)}) collective-permute-start(bf16[1,64,1]{2,1,0:T(8,128)(2,1)S(1)} %get-tuple-element.32), channel_id=1, source_target_pairs={{1,0},{2,1},{3,2},{4,3},{5,4},{6,5},{7,6},{8,7},{9,8},{10,9},{11,1... | collective-permute-start | bytes 392 | tf_op jit(solution)/shard_map/ppermute | solution.py:24
  285.6 2.4 fusion.37
  289.0 104.3 %all-reduce.1 = (f32[4,64]{1,0:T(4,128)}, f32[64]{0:T(128)}, f32[3,64,64]{2,1,0:T(8,128)}, f32[512]{0:T(512)}) all-reduce(f32[4,64]{1,0:T(4,128)S(1)} %fusion.37, f32[64]{0:T(128)S(1)} %fusion.40, f32[3,64,64]{2,1,0:T(8,128)S(1)} %pad_maximum_fusion.1, f32[512]{0:T(512)S(1)} %get-tuple-element.6), channel_id=1, replica_groups=mesh['sims'=32,'sites'=16] {'sims','sites'}, use_global_device_ids=true, to_apply=%region_6.7 | all-reduce | flops 13120 | bytes 104960 | tf_op jit(solution)/shard_map/psum | solution.py:229
  393.3 169.0 %all-reduce.5.cloned.1.call-done = (f32[1048576]{0:T(1024)}, f32[64,512]{1,0:T(8,128)}) async-done(((f32[1048576]{0:T(1024)}, f32[64,512]{1,0:T(8,128)}), (f32[1048576]{0:T(1024)}, f32[64,512]{1,0:T(8,128)})) %all-reduce.5.cloned.1.call-update) | async-done | bytes 4325392
  563.7 1.6 copy.101
  (161 shorter events, 34.6 us)
Async XLA Ops:
  7.2 51.3 %copy-start = (f32[64,512]{1,0:T(8,128)S(1)}, f32[64,512]{1,0:T(8,128)}, u32[]{:S(2)}) copy-start(f32[64,512]{1,0:T(8,128)} %param.17) | copy-start | bytes 393220
  7.2 555.2 %all-reduce.5.cloned.1.call-start = ((), (), s32[]{:S(2)}) async-start(), calls=%async_computation | async-start | bytes 8650752
  7.2 56.6 %collective-permute-start.10 = (bf16[1,128]{1,0:T(2,128)(2,1)}, bf16[1,128]{1,0:T(2,128)(2,1)S(1)}, u32[]{:S(2)}, u32[]{:S(2)}) collective-permute-start(bf16[1,128]{1,0:T(2,128)(2,1)} %param.11), channel_id=1, source_target_pairs={{0,15},{1,0},{2,1},{3,2},{4,3},{5,4},{6,5},{7,6},{8,7},{9,8},{10,9... | collective-permute-start | bytes 776 | tf_op jit(solution)/shard_map/ppermute | solution.py:34
  18.4 53.2 %collective-permute-start.11 = (bf16[1,128]{1,0:T(2,128)(2,1)}, bf16[1,128]{1,0:T(2,128)(2,1)S(1)}, u32[]{:S(2)}, u32[]{:S(2)}) collective-permute-start(bf16[1,128]{1,0:T(2,128)(2,1)} %param.11), channel_id=1, source_target_pairs={{0,1},{1,2},{2,3},{3,4},{4,5},{5,6},{6,7},{7,8},{8,9},{9,10},{10,1... | collective-permute-start | bytes 776 | tf_op jit(solution)/shard_map/ppermute | solution.py:34
  20.4 54.8 %collective-permute-start.12 = (bf16[1,128]{1,0:T(2,128)(2,1)}, bf16[1,128]{1,0:T(2,128)(2,1)S(1)}, u32[]{:S(2)}, u32[]{:S(2)}) collective-permute-start(bf16[1,128]{1,0:T(2,128)(2,1)} %param.11), channel_id=1, source_target_pairs={{0,14},{1,15},{2,0},{3,1},{4,2},{5,3},{6,4},{7,5},{8,6},{9,7},{10,... | collective-permute-start | bytes 776 | tf_op jit(solution)/shard_map/ppermute | solution.py:34
  25.2 58.8 %collective-permute-start.13 = (bf16[1,128]{1,0:T(2,128)(2,1)}, bf16[1,128]{1,0:T(2,128)(2,1)S(1)}, u32[]{:S(2)}, u32[]{:S(2)}) collective-permute-start(bf16[1,128]{1,0:T(2,128)(2,1)} %param.11), channel_id=1, source_target_pairs={{0,2},{1,3},{2,4},{3,5},{4,6},{5,7},{6,8},{7,9},{8,10},{9,11},{10,... | collective-permute-start | bytes 776 | tf_op jit(solution)/shard_map/ppermute | solution.py:34
  31.3 4.5 copy-start.7
  31.3 12.6 %copy-start.5 = (f32[3,64,64]{2,1,0:T(8,128)S(1)}, f32[3,64,64]{2,1,0:T(8,128)}, u32[]{:S(2)}) copy-start(f32[3,64,64]{2,1,0:T(8,128)} %param.16) | copy-start | bytes 147460
  31.4 13.5 %copy-start.2 = (bf16[4,512,512]{2,1,0:T(8,128)(2,1)S(1)}, bf16[4,512,512]{2,1,0:T(8,128)(2,1)}, u32[]{:S(2)}) copy-start(bf16[4,512,512]{2,1,0:T(8,128)(2,1)} %param.19) | copy-start | bytes 6291460
  31.4 13.5 %copy-start.4 = (bf16[1,128,512]{2,1,0:T(8,128)(2,1)S(1)}, bf16[1,128,512]{2,1,0:T(8,128)(2,1)}, u32[]{:S(2)}) copy-start(bf16[1,128,512]{2,1,0:T(8,128)(2,1)} %param.13) | copy-start | bytes 393220
  31.4 14.6 %copy-start.16 = (bf16[1,128]{1,0:T(2,128)(2,1)S(1)}, bf16[1,128]{1,0:T(2,128)(2,1)}, u32[]{:S(2)}) copy-start(bf16[1,128]{1,0:T(2,128)(2,1)} %param.11) | copy-start | bytes 772
  35.9 23.6 %copy-start.11 = (f32[512]{0:T(512)S(1)}, f32[512]{0:T(512)}, u32[]{:S(2)}) copy-start(f32[512]{0:T(512)} %param.18) | copy-start | bytes 6148
  35.9 11.4 %collective-permute-start.1 = (f32[1,64,1]{2,1,0:T(8,128)S(1)}, f32[1,64,1]{2,1,0:T(8,128)S(1)}, u32[]{:S(2)}, u32[]{:S(2)}) collective-permute-start(f32[1,64,1]{2,1,0:T(8,128)S(1)} %get-tuple-element.31), channel_id=1, source_target_pairs={{1,0},{2,1},{3,2},{4,3},{5,4},{6,5},{7,6},{8,7},{9,8},{10,9},{11,1... | collective-permute-start | bytes 776 | tf_op jit(solution)/shard_map/ppermute | solution.py:24
  47.4 8.8 %collective-permute-start = (f32[1,64,1]{2,1,0:T(8,128)S(1)}, f32[1,64,1]{2,1,0:T(8,128)S(1)}, u32[]{:S(2)}, u32[]{:S(2)}) collective-permute-start(f32[1,64,1]{2,1,0:T(8,128)S(1)} %get-tuple-element.30), channel_id=1, source_target_pairs={{0,1},{1,2},{2,3},{3,4},{4,5},{5,6},{6,7},{7,8},{8,9},{9,10},{10,1... | collective-permute-start | bytes 776 | tf_op jit(solution)/shard_map/ppermute | solution.py:22
  56.2 1.9 copy-start.9
  56.2 32.0 %collective-permute-start.14 = (bf16[1,128]{1,0:T(2,128)(2,1)S(1)}, bf16[1,128]{1,0:T(2,128)(2,1)S(1)}, u32[]{:S(2)}, u32[]{:S(2)}) collective-permute-start(bf16[1,128]{1,0:T(2,128)(2,1)S(1)} %copy-done.16), channel_id=1, source_target_pairs={{0,13},{1,14},{2,15},{3,0},{4,1},{5,2},{6,3},{7,4},{8,5},{9,6},{10... | collective-permute-start | bytes 776 | tf_op jit(solution)/shard_map/ppermute | solution.py:34
  59.5 0.5 copy-start.13
  63.8 29.9 %collective-permute-start.15 = (bf16[1,128]{1,0:T(2,128)(2,1)S(1)}, bf16[1,128]{1,0:T(2,128)(2,1)S(1)}, u32[]{:S(2)}, u32[]{:S(2)}) collective-permute-start(bf16[1,128]{1,0:T(2,128)(2,1)S(1)} %copy-done.16), channel_id=1, source_target_pairs={{0,3},{1,4},{2,5},{3,6},{4,7},{5,8},{6,9},{7,10},{8,11},{9,12},{10... | collective-permute-start | bytes 776 | tf_op jit(solution)/shard_map/ppermute | solution.py:34
  71.7 26.5 %collective-permute-start.16 = (bf16[1,128]{1,0:T(2,128)(2,1)S(1)}, bf16[1,128]{1,0:T(2,128)(2,1)S(1)}, u32[]{:S(2)}, u32[]{:S(2)}) collective-permute-start(bf16[1,128]{1,0:T(2,128)(2,1)S(1)} %copy-done.16), channel_id=1, source_target_pairs={{0,12},{1,13},{2,14},{3,15},{4,0},{5,1},{6,2},{7,3},{8,4},{9,5},{1... | collective-permute-start | bytes 776 | tf_op jit(solution)/shard_map/ppermute | solution.py:34
  75.2 29.7 %collective-permute-start.17 = (bf16[1,128]{1,0:T(2,128)(2,1)S(1)}, bf16[1,128]{1,0:T(2,128)(2,1)S(1)}, u32[]{:S(2)}, u32[]{:S(2)}) collective-permute-start(bf16[1,128]{1,0:T(2,128)(2,1)S(1)} %copy-done.16), channel_id=1, source_target_pairs={{0,4},{1,5},{2,6},{3,7},{4,8},{5,9},{6,10},{7,11},{8,12},{9,13},{1... | collective-permute-start | bytes 776 | tf_op jit(solution)/shard_map/ppermute | solution.py:34
  84.0 78.1 %collective-permute-start.18 = (bf16[1,128,8,64]{1,3,2,0:T(8,128)(2,1)}, bf16[1,128,8,64]{1,3,2,0:T(8,128)(2,1)}, u32[]{:S(2)}, u32[]{:S(2)}) collective-permute-start(bf16[1,128,8,64]{1,3,2,0:T(8,128)(2,1)} %bitcast.35), channel_id=1, source_target_pairs={{0,15},{1,0},{2,1},{3,2},{4,3},{5,4},{6,5},{7,6},{8,7},{9,8},{10,9... | collective-permute-start | bytes 393224 | tf_op jit(solution)/shard_map/ppermute | solution.py:34
  88.2 80.9 %collective-permute-start.19 = (bf16[1,128,8,64]{1,3,2,0:T(8,128)(2,1)}, bf16[1,128,8,64]{1,3,2,0:T(8,128)(2,1)}, u32[]{:S(2)}, u32[]{:S(2)}) collective-permute-start(bf16[1,128,8,64]{1,3,2,0:T(8,128)(2,1)} %bitcast.35), channel_id=1, source_target_pairs={{0,1},{1,2},{2,3},{3,4},{4,5},{5,6},{6,7},{7,8},{8,9},{9,10},{10,1... | collective-permute-start | bytes 393224 | tf_op jit(solution)/shard_map/ppermute | solution.py:34
  93.7 79.3 %collective-permute-start.20 = (bf16[1,128,8,64]{1,3,2,0:T(8,128)(2,1)}, bf16[1,128,8,64]{1,3,2,0:T(8,128)(2,1)}, u32[]{:S(2)}, u32[]{:S(2)}) collective-permute-start(bf16[1,128,8,64]{1,3,2,0:T(8,128)(2,1)} %bitcast.35), channel_id=1, source_target_pairs={{0,14},{1,15},{2,0},{3,1},{4,2},{5,3},{6,4},{7,5},{8,6},{9,7},{10,... | collective-permute-start | bytes 393224 | tf_op jit(solution)/shard_map/ppermute | solution.py:34
  98.2 12.7 %collective-permute-start.2 = (bf16[1,128,8,64]{1,3,2,0:T(8,128)(2,1)}, bf16[1,128,8,64]{1,3,2,0:T(8,128)(2,1)}, u32[]{:S(2)}, u32[]{:S(2)}) collective-permute-start(bf16[1,128,8,64]{1,3,2,0:T(8,128)(2,1)} %bitcast.17), channel_id=1, source_target_pairs={{0,15},{1,0},{2,1},{3,2},{4,3},{5,4},{6,5},{7,6},{8,7},{9,8},{10,9... | collective-permute-start | bytes 393224 | tf_op jit(solution)/shard_map/ppermute | solution.py:34
  104.8 13.4 %collective-permute-start.3 = (bf16[1,128,8,64]{1,3,2,0:T(8,128)(2,1)}, bf16[1,128,8,64]{1,3,2,0:T(8,128)(2,1)}, u32[]{:S(2)}, u32[]{:S(2)}) collective-permute-start(bf16[1,128,8,64]{1,3,2,0:T(8,128)(2,1)} %bitcast.17), channel_id=1, source_target_pairs={{0,1},{1,2},{2,3},{3,4},{4,5},{5,6},{6,7},{7,8},{8,9},{9,10},{10,1... | collective-permute-start | bytes 393224 | tf_op jit(solution)/shard_map/ppermute | solution.py:34
  110.8 13.4 %collective-permute-start.4 = (bf16[1,128,8,64]{1,3,2,0:T(8,128)(2,1)}, bf16[1,128,8,64]{1,3,2,0:T(8,128)(2,1)S(1)}, u32[]{:S(2)}, u32[]{:S(2)}) collective-permute-start(bf16[1,128,8,64]{1,3,2,0:T(8,128)(2,1)} %bitcast.17), channel_id=1, source_target_pairs={{0,14},{1,15},{2,0},{3,1},{4,2},{5,3},{6,4},{7,5},{8,6},{9,7},{10,... | collective-permute-start | bytes 393224 | tf_op jit(solution)/shard_map/ppermute | solution.py:34
  118.3 16.3 %collective-permute-start.5 = (bf16[1,128,8,64]{1,3,2,0:T(8,128)(2,1)}, bf16[1,128,8,64]{1,3,2,0:T(8,128)(2,1)S(1)}, u32[]{:S(2)}, u32[]{:S(2)}) collective-permute-start(bf16[1,128,8,64]{1,3,2,0:T(8,128)(2,1)} %bitcast.17), channel_id=1, source_target_pairs={{0,2},{1,3},{2,4},{3,5},{4,6},{5,7},{6,8},{7,9},{8,10},{9,11},{10,... | collective-permute-start | bytes 393224 | tf_op jit(solution)/shard_map/ppermute | solution.py:34
  124.2 15.6 %collective-permute-start.6 = (bf16[1,128,8,64]{1,3,2,0:T(8,128)(2,1)}, bf16[1,128,8,64]{1,3,2,0:T(8,128)(2,1)S(1)}, u32[]{:S(2)}, u32[]{:S(2)}) collective-permute-start(bf16[1,128,8,64]{1,3,2,0:T(8,128)(2,1)} %bitcast.17), channel_id=1, source_target_pairs={{0,13},{1,14},{2,15},{3,0},{4,1},{5,2},{6,3},{7,4},{8,5},{9,6},{10... | collective-permute-start | bytes 393224 | tf_op jit(solution)/shard_map/ppermute | solution.py:34
  134.5 10.2 %collective-permute-start.7 = (bf16[1,128,8,64]{1,3,2,0:T(8,128)(2,1)}, bf16[1,128,8,64]{1,3,2,0:T(8,128)(2,1)S(1)}, u32[]{:S(2)}, u32[]{:S(2)}) collective-permute-start(bf16[1,128,8,64]{1,3,2,0:T(8,128)(2,1)} %bitcast.17), channel_id=1, source_target_pairs={{0,3},{1,4},{2,5},{3,6},{4,7},{5,8},{6,9},{7,10},{8,11},{9,12},{10... | collective-permute-start | bytes 393224 | tf_op jit(solution)/shard_map/ppermute | solution.py:34
  139.8 10.0 %collective-permute-start.8 = (bf16[1,128,8,64]{1,3,2,0:T(8,128)(2,1)}, bf16[1,128,8,64]{1,3,2,0:T(8,128)(2,1)S(1)}, u32[]{:S(2)}, u32[]{:S(2)}) collective-permute-start(bf16[1,128,8,64]{1,3,2,0:T(8,128)(2,1)} %bitcast.17), channel_id=1, source_target_pairs={{0,12},{1,13},{2,14},{3,15},{4,0},{5,1},{6,2},{7,3},{8,4},{9,5},{1... | collective-permute-start | bytes 393224 | tf_op jit(solution)/shard_map/ppermute | solution.py:34
  144.7 12.2 %collective-permute-start.9 = (bf16[1,128,8,64]{1,3,2,0:T(8,128)(2,1)}, bf16[1,128,8,64]{1,3,2,0:T(8,128)(2,1)S(1)}, u32[]{:S(2)}, u32[]{:S(2)}) collective-permute-start(bf16[1,128,8,64]{1,3,2,0:T(8,128)(2,1)} %bitcast.17), channel_id=1, source_target_pairs={{0,4},{1,5},{2,6},{3,7},{4,8},{5,9},{6,10},{7,11},{8,12},{9,13},{1... | collective-permute-start | bytes 393224 | tf_op jit(solution)/shard_map/ppermute | solution.py:34
  149.8 28.4 %collective-permute-start.21 = (bf16[1,128,8,64]{1,3,2,0:T(8,128)(2,1)}, bf16[1,128,8,64]{1,3,2,0:T(8,128)(2,1)S(1)}, u32[]{:S(2)}, u32[]{:S(2)}) collective-permute-start(bf16[1,128,8,64]{1,3,2,0:T(8,128)(2,1)} %bitcast.35), channel_id=1, source_target_pairs={{0,2},{1,3},{2,4},{3,5},{4,6},{5,7},{6,8},{7,9},{8,10},{9,11},{10,... | collective-permute-start | bytes 393224 | tf_op jit(solution)/shard_map/ppermute | solution.py:34
  157.0 21.4 %collective-permute-start.22 = (bf16[1,128,8,64]{1,3,2,0:T(8,128)(2,1)}, bf16[1,128,8,64]{1,3,2,0:T(8,128)(2,1)S(1)}, u32[]{:S(2)}, u32[]{:S(2)}) collective-permute-start(bf16[1,128,8,64]{1,3,2,0:T(8,128)(2,1)} %bitcast.35), channel_id=1, source_target_pairs={{0,13},{1,14},{2,15},{3,0},{4,1},{5,2},{6,3},{7,4},{8,5},{9,6},{10... | collective-permute-start | bytes 393224 | tf_op jit(solution)/shard_map/ppermute | solution.py:34
  162.1 16.2 %collective-permute-start.23 = (bf16[1,128,8,64]{1,3,2,0:T(8,128)(2,1)}, bf16[1,128,8,64]{1,3,2,0:T(8,128)(2,1)S(1)}, u32[]{:S(2)}, u32[]{:S(2)}) collective-permute-start(bf16[1,128,8,64]{1,3,2,0:T(8,128)(2,1)} %bitcast.35), channel_id=1, source_target_pairs={{0,3},{1,4},{2,5},{3,6},{4,7},{5,8},{6,9},{7,10},{8,11},{9,12},{10... | collective-permute-start | bytes 393224 | tf_op jit(solution)/shard_map/ppermute | solution.py:34
  169.1 9.3 %collective-permute-start.24 = (bf16[1,128,8,64]{1,3,2,0:T(8,128)(2,1)}, bf16[1,128,8,64]{1,3,2,0:T(8,128)(2,1)S(1)}, u32[]{:S(2)}, u32[]{:S(2)}) collective-permute-start(bf16[1,128,8,64]{1,3,2,0:T(8,128)(2,1)} %bitcast.35), channel_id=1, source_target_pairs={{0,12},{1,13},{2,14},{3,15},{4,0},{5,1},{6,2},{7,3},{8,4},{9,5},{1... | collective-permute-start | bytes 393224 | tf_op jit(solution)/shard_map/ppermute | solution.py:34
  172.9 7.1 %collective-permute-start.25 = (bf16[1,128,8,64]{1,3,2,0:T(8,128)(2,1)}, bf16[1,128,8,64]{1,3,2,0:T(8,128)(2,1)S(1)}, u32[]{:S(2)}, u32[]{:S(2)}) collective-permute-start(bf16[1,128,8,64]{1,3,2,0:T(8,128)(2,1)} %bitcast.35), channel_id=1, source_target_pairs={{0,4},{1,5},{2,6},{3,7},{4,8},{5,9},{6,10},{7,11},{8,12},{9,13},{1... | collective-permute-start | bytes 393224 | tf_op jit(solution)/shard_map/ppermute | solution.py:34
  184.4 23.3 %copy-start.3 = (bf16[4,512,512]{2,1,0:T(8,128)(2,1)S(1)}, bf16[4,512,512]{2,1,0:T(8,128)(2,1)}, u32[]{:S(2)}) copy-start(bf16[4,512,512]{2,1,0:T(8,128)(2,1)} %param.19) | copy-start | bytes 6291460
  184.6 23.3 %collective-permute-start.26 = (bf16[1,128,8,64]{1,3,2,0:T(8,128)(2,1)S(1)}, bf16[1,128,8,64]{1,3,2,0:T(8,128)(2,1)S(1)}, u32[]{:S(2)}, u32[]{:S(2)}) collective-permute-start(bf16[1,128,8,64]{1,3,2,0:T(8,128)(2,1)S(1)} %get-tuple-element.14), channel_id=1, source_target_pairs={{0,1},{1,2},{2,3},{3,4},{4,5},{5,6},{6,7},{7,8},{8,9},{9,10},{10,1... | collective-permute-start | bytes 393224 | tf_op jit(solution)/shard_map/ppermute | solution.py:34
  188.4 24.1 %collective-permute-start.27 = (bf16[1,128,8,64]{1,3,2,0:T(8,128)(2,1)S(1)}, bf16[1,128,8,64]{1,3,2,0:T(8,128)(2,1)S(1)}, u32[]{:S(2)}, u32[]{:S(2)}) collective-permute-start(bf16[1,128,8,64]{1,3,2,0:T(8,128)(2,1)S(1)} %get-tuple-element.21), channel_id=1, source_target_pairs={{0,15},{1,0},{2,1},{3,2},{4,3},{5,4},{6,5},{7,6},{8,7},{9,8},{10,9... | collective-permute-start | bytes 393224 | tf_op jit(solution)/shard_map/ppermute | solution.py:34
  193.6 28.0 %collective-permute-start.28 = (bf16[1,128,8,64]{1,3,2,0:T(8,128)(2,1)S(1)}, bf16[1,128,8,64]{1,3,2,0:T(8,128)(2,1)S(1)}, u32[]{:S(2)}, u32[]{:S(2)}) collective-permute-start(bf16[1,128,8,64]{1,3,2,0:T(8,128)(2,1)S(1)} %get-tuple-element.20), channel_id=1, source_target_pairs={{0,2},{1,3},{2,4},{3,5},{4,6},{5,7},{6,8},{7,9},{8,10},{9,11},{10,... | collective-permute-start | bytes 393224 | tf_op jit(solution)/shard_map/ppermute | solution.py:34
  197.9 26.3 %collective-permute-start.29 = (bf16[1,128,8,64]{1,3,2,0:T(8,128)(2,1)S(1)}, bf16[1,128,8,64]{1,3,2,0:T(8,128)(2,1)S(1)}, u32[]{:S(2)}, u32[]{:S(2)}) collective-permute-start(bf16[1,128,8,64]{1,3,2,0:T(8,128)(2,1)S(1)} %get-tuple-element.19), channel_id=1, source_target_pairs={{0,14},{1,15},{2,0},{3,1},{4,2},{5,3},{6,4},{7,5},{8,6},{9,7},{10,... | collective-permute-start | bytes 393224 | tf_op jit(solution)/shard_map/ppermute | solution.py:34
  204.3 21.8 %collective-permute-start.30 = (bf16[1,128,8,64]{1,3,2,0:T(8,128)(2,1)S(1)}, bf16[1,128,8,64]{1,3,2,0:T(8,128)(2,1)S(1)}, u32[]{:S(2)}, u32[]{:S(2)}) collective-permute-start(bf16[1,128,8,64]{1,3,2,0:T(8,128)(2,1)S(1)} %get-tuple-element.18), channel_id=1, source_target_pairs={{0,3},{1,4},{2,5},{3,6},{4,7},{5,8},{6,9},{7,10},{8,11},{9,12},{10... | collective-permute-start | bytes 393224 | tf_op jit(solution)/shard_map/ppermute | solution.py:34
  208.0 25.1 %collective-permute-start.31 = (bf16[1,128,8,64]{1,3,2,0:T(8,128)(2,1)S(1)}, bf16[1,128,8,64]{1,3,2,0:T(8,128)(2,1)S(1)}, u32[]{:S(2)}, u32[]{:S(2)}) collective-permute-start(bf16[1,128,8,64]{1,3,2,0:T(8,128)(2,1)S(1)} %get-tuple-element.17), channel_id=1, source_target_pairs={{0,13},{1,14},{2,15},{3,0},{4,1},{5,2},{6,3},{7,4},{8,5},{9,6},{10... | collective-permute-start | bytes 393224 | tf_op jit(solution)/shard_map/ppermute | solution.py:34
  212.5 22.5 %collective-permute-start.32 = (bf16[1,128,8,64]{1,3,2,0:T(8,128)(2,1)S(1)}, bf16[1,128,8,64]{1,3,2,0:T(8,128)(2,1)S(1)}, u32[]{:S(2)}, u32[]{:S(2)}) collective-permute-start(bf16[1,128,8,64]{1,3,2,0:T(8,128)(2,1)S(1)} %get-tuple-element.16), channel_id=1, source_target_pairs={{0,4},{1,5},{2,6},{3,7},{4,8},{5,9},{6,10},{7,11},{8,12},{9,13},{1... | collective-permute-start | bytes 393224 | tf_op jit(solution)/shard_map/ppermute | solution.py:34
  221.6 22.1 %collective-permute-start.33 = (bf16[1,128,8,64]{1,3,2,0:T(8,128)(2,1)S(1)}, bf16[1,128,8,64]{1,3,2,0:T(8,128)(2,1)S(1)}, u32[]{:S(2)}, u32[]{:S(2)}) collective-permute-start(bf16[1,128,8,64]{1,3,2,0:T(8,128)(2,1)S(1)} %get-tuple-element.15), channel_id=1, source_target_pairs={{0,12},{1,13},{2,14},{3,15},{4,0},{5,1},{6,2},{7,3},{8,4},{9,5},{1... | collective-permute-start | bytes 393224 | tf_op jit(solution)/shard_map/ppermute | solution.py:34
  224.1 44.5 %copy-start.12 = (f32[512]{0:T(512)S(1)}, f32[512]{0:T(512)}, u32[]{:S(2)}) copy-start(f32[512]{0:T(512)} %param.18) | copy-start | bytes 6148
  224.2 44.5 %copy-start.14 = (f32[128]{0:T(128)S(1)}, f32[128]{0:T(128)}, u32[]{:S(2)}) copy-start(f32[128]{0:T(128)} %copy-done.13) | copy-start | bytes 1540
  224.2 22.6 %collective-permute-start.34 = (bf16[1,128,8,64]{1,3,2,0:T(8,128)(2,1)S(1)}, bf16[1,128,8,64]{1,3,2,0:T(8,128)(2,1)S(1)}, u32[]{:S(2)}, u32[]{:S(2)}) collective-permute-start(bf16[1,128,8,64]{1,3,2,0:T(8,128)(2,1)S(1)} %get-tuple-element.22), channel_id=1, source_target_pairs={{0,1},{1,2},{2,3},{3,4},{4,5},{5,6},{6,7},{7,8},{8,9},{9,10},{10,1... | collective-permute-start | bytes 393224 | tf_op jit(solution)/shard_map/ppermute | solution.py:34
  226.1 25.5 %collective-permute-start.35 = (bf16[1,128,8,64]{1,3,2,0:T(8,128)(2,1)S(1)}, bf16[1,128,8,64]{1,3,2,0:T(8,128)(2,1)S(1)}, u32[]{:S(2)}, u32[]{:S(2)}) collective-permute-start(bf16[1,128,8,64]{1,3,2,0:T(8,128)(2,1)S(1)} %get-tuple-element.29), channel_id=1, source_target_pairs={{0,15},{1,0},{2,1},{3,2},{4,3},{5,4},{6,5},{7,6},{8,7},{9,8},{10,9... | collective-permute-start | bytes 393224 | tf_op jit(solution)/shard_map/ppermute | solution.py:34
  233.1 27.3 %collective-permute-start.36 = (bf16[1,128,8,64]{1,3,2,0:T(8,128)(2,1)S(1)}, bf16[1,128,8,64]{1,3,2,0:T(8,128)(2,1)S(1)}, u32[]{:S(2)}, u32[]{:S(2)}) collective-permute-start(bf16[1,128,8,64]{1,3,2,0:T(8,128)(2,1)S(1)} %get-tuple-element.28), channel_id=1, source_target_pairs={{0,2},{1,3},{2,4},{3,5},{4,6},{5,7},{6,8},{7,9},{8,10},{9,11},{10,... | collective-permute-start | bytes 393224 | tf_op jit(solution)/shard_map/ppermute | solution.py:34
  235.0 27.7 %collective-permute-start.37 = (bf16[1,128,8,64]{1,3,2,0:T(8,128)(2,1)S(1)}, bf16[1,128,8,64]{1,3,2,0:T(8,128)(2,1)S(1)}, u32[]{:S(2)}, u32[]{:S(2)}) collective-permute-start(bf16[1,128,8,64]{1,3,2,0:T(8,128)(2,1)S(1)} %get-tuple-element.27), channel_id=1, source_target_pairs={{0,14},{1,15},{2,0},{3,1},{4,2},{5,3},{6,4},{7,5},{8,6},{9,7},{10,... | collective-permute-start | bytes 393224 | tf_op jit(solution)/shard_map/ppermute | solution.py:34
  243.8 18.9 %collective-permute-start.38 = (bf16[1,128,8,64]{1,3,2,0:T(8,128)(2,1)S(1)}, bf16[1,128,8,64]{1,3,2,0:T(8,128)(2,1)S(1)}, u32[]{:S(2)}, u32[]{:S(2)}) collective-permute-start(bf16[1,128,8,64]{1,3,2,0:T(8,128)(2,1)S(1)} %get-tuple-element.26), channel_id=1, source_target_pairs={{0,3},{1,4},{2,5},{3,6},{4,7},{5,8},{6,9},{7,10},{8,11},{9,12},{10... | collective-permute-start | bytes 393224 | tf_op jit(solution)/shard_map/ppermute | solution.py:34
  246.7 22.4 %copy-start.15 = (f32[128]{0:T(128)S(1)}, f32[128]{0:T(128)}, u32[]{:S(2)}) copy-start(f32[128]{0:T(128)} %get-tuple-element.34) | copy-start | bytes 1540
  246.8 15.9 %collective-permute-start.39 = (bf16[1,128,8,64]{1,3,2,0:T(8,128)(2,1)S(1)}, bf16[1,128,8,64]{1,3,2,0:T(8,128)(2,1)S(1)}, u32[]{:S(2)}, u32[]{:S(2)}) collective-permute-start(bf16[1,128,8,64]{1,3,2,0:T(8,128)(2,1)S(1)} %get-tuple-element.25), channel_id=1, source_target_pairs={{0,13},{1,14},{2,15},{3,0},{4,1},{5,2},{6,3},{7,4},{8,5},{9,6},{10... | collective-permute-start | bytes 393224 | tf_op jit(solution)/shard_map/ppermute | solution.py:34
  251.6 11.3 %collective-permute-start.40 = (bf16[1,128,8,64]{1,3,2,0:T(8,128)(2,1)S(1)}, bf16[1,128,8,64]{1,3,2,0:T(8,128)(2,1)S(1)}, u32[]{:S(2)}, u32[]{:S(2)}) collective-permute-start(bf16[1,128,8,64]{1,3,2,0:T(8,128)(2,1)S(1)} %get-tuple-element.24), channel_id=1, source_target_pairs={{0,4},{1,5},{2,6},{3,7},{4,8},{5,9},{6,10},{7,11},{8,12},{9,13},{1... | collective-permute-start | bytes 393224 | tf_op jit(solution)/shard_map/ppermute | solution.py:34
  260.4 8.1 %collective-permute-start.41 = (bf16[1,128,8,64]{1,3,2,0:T(8,128)(2,1)S(1)}, bf16[1,128,8,64]{1,3,2,0:T(8,128)(2,1)S(1)}, u32[]{:S(2)}, u32[]{:S(2)}) collective-permute-start(bf16[1,128,8,64]{1,3,2,0:T(8,128)(2,1)S(1)} %get-tuple-element.23), channel_id=1, source_target_pairs={{0,12},{1,13},{2,14},{3,15},{4,0},{5,1},{6,2},{7,3},{8,4},{9,5},{1... | collective-permute-start | bytes 393224 | tf_op jit(solution)/shard_map/ppermute | solution.py:34
  274.8 9.1 %copy-start.10 = (f32[1,64,1]{2,1,0:T(8,128)S(1)}, f32[1,64,1]{2,1,0:T(8,128)}, u32[]{:S(2)}) copy-start(f32[1,64,1]{2,1,0:T(8,128)} %copy-done.9) | copy-start | bytes 772
  274.8 9.8 %copy-start.6 = (f32[3,64,64]{2,1,0:T(8,128)S(1)}, f32[3,64,64]{2,1,0:T(8,128)}, u32[]{:S(2)}) copy-start(f32[3,64,64]{2,1,0:T(8,128)} %param.16) | copy-start | bytes 147460
  274.8 10.8 %copy-start.1 = (f32[64,64,128]{2,0,1:T(8,128)S(1)}, f32[64,64,128]{2,0,1:T(8,128)}, u32[]{:S(2)}) copy-start(f32[64,64,128]{2,0,1:T(8,128)} %get-tuple-element.37) | copy-start | bytes 6291460
  274.8 10.8 %copy-start.8 = (f32[64,128,4]{1,2,0:T(4,128)S(1)}, f32[64,128,4]{1,2,0:T(4,128)}, u32[]{:S(2)}) copy-start(f32[64,128,4]{1,2,0:T(4,128)} %copy-done.7) | copy-start | bytes 393220
  274.9 10.8 %copy-start.17 = (f32[64]{0:T(128)S(1)}, f32[64]{0:T(128)}, u32[]{:S(2)}) copy-start(f32[64]{0:T(128)} %param.15) | copy-start | bytes 772
  275.0 9.9 %collective-permute-start.43 = (bf16[1,64,1]{2,1,0:T(8,128)(2,1)S(1)}, bf16[1,64,1]{2,1,0:T(8,128)(2,1)S(1)}, u32[]{:S(2)}, u32[]{:S(2)}) collective-permute-start(bf16[1,64,1]{2,1,0:T(8,128)(2,1)S(1)} %get-tuple-element.33), channel_id=1, source_target_pairs={{0,1},{1,2},{2,3},{3,4},{4,5},{5,6},{6,7},{7,8},{8,9},{9,10},{10,1... | collective-permute-start | bytes 392 | tf_op jit(solution)/shard_map/ppermute | solution.py:22
  277.0 8.4 %collective-permute-start.42 = (bf16[1,64,1]{2,1,0:T(8,128)(2,1)S(1)}, bf16[1,64,1]{2,1,0:T(8,128)(2,1)S(1)}, u32[]{:S(2)}, u32[]{:S(2)}) collective-permute-start(bf16[1,64,1]{2,1,0:T(8,128)(2,1)S(1)} %get-tuple-element.32), channel_id=1, source_target_pairs={{1,0},{2,1},{3,2},{4,3},{5,4},{6,5},{7,6},{8,7},{9,8},{10,9},{11,1... | collective-permute-start | bytes 392 | tf_op jit(solution)/shard_map/ppermute | solution.py:24
Sparse Core Ops, SparseCore 0:
  275.0 287.3 all-reduce.4
where the time goes:
time: 576 us; the launch traced here: 572 us
  starting transfers between devices  202 us (35%)
  waiting for transfers between devices  194 us (34%)
  blocking collectives  104 us (18%)
  local copies, waits for them, and re-layouts  29 us (5%)
  matrix products  19.7 us (3%)
  between operations  16.1 us (3%)
  other arithmetic  7.12 us (1%)
    ppermute x40, starting transfers between devices, from_behind(): return lax.ppermute(value, axis, pairs)  183 us
    unnamed x2, waiting for transfers between devices  169 us
    psum x1, blocking collectives, per_device(): lax.psum((term_conv, term_bias, jnp.stack(mix_terms), term_embed, term_ga...  104 us
    unnamed x63, local copies, waits for them, and re-layouts  24.8 us
    ppermute x40, waiting for transfers between devices, from_behind(): return lax.ppermute(value, axis, pairs)  17.6 us
    ppermute x2, starting transfers between devices, extended(): lax.ppermute(head, axis, [((i + 1) % count, i) for i in range(count)])  14.8 us
  transfers between devices with their start and end apart: 45, of which 10 were waited for; matrix products, arithmetic and copies ran while one was open for 7% of the time, Pallas kernels for 0%

commit v1 on v0

--- a/solution.py
+++ b/solution.py
@@ -121,12 +121,16 @@
     value_heads = split_heads(values, heads)
     reach_blocks = -(-BAND // local)
     offsets = block_offsets(count, reach_blocks)
-    blocks = {0: (key_heads, value_heads, key_prior)}
+    packed = jnp.concatenate(
+        [keys, values, key_prior[:, :, None]], axis=2
+    )
+    gathered = {0: packed}
     for offset in offsets[1:]:
-        blocks[offset] = from_behind((key_heads, value_heads, key_prior), "sites", -offset)
-    key_cat = jnp.concatenate([blocks[offset][0] for offset in offsets], axis=1)
-    value_cat = jnp.concatenate([blocks[offset][1] for offset in offsets], axis=1)
-    prior_cat = jnp.concatenate([blocks[offset][2] for offset in offsets], axis=1)
+        gathered[offset] = from_behind(packed, "sites", -offset)
+    packed_cat = jnp.concatenate([gathered[offset] for offset in offsets], axis=1)
+    key_cat = split_heads(packed_cat[:, :, :width], heads)
+    value_cat = split_heads(packed_cat[:, :, width : 2 * width], heads)
+    prior_cat = packed_cat[:, :, 2 * width]
     key_places = jnp.concatenate([(place + offset) % count * local + ordinal for offset in offsets])
     query_places = place * local + ordinal
     scores, inside = band_scores(
@@ -164,16 +168,12 @@
     value_sum = value_part[:, 0:local]
     for position, offset in enumerate(offsets[1:], start=1):
         lower = position * local
-        back_keys, back_values = (
-            from_behind(
-                key_part[:, lower : lower + local].astype(jnp.bfloat16), "sites", offset
-            ).astype(jnp.float32),
-            from_behind(
-                value_part[:, lower : lower + local].astype(jnp.bfloat16), "sites", offset
-            ).astype(jnp.float32),
-        )
-        key_sum = key_sum + back_keys
-        value_sum = value_sum + back_values
+        both = jnp.concatenate(
+            [key_part[:, lower : lower + local], value_part[:, lower : lower + local]], axis=2
+        ).astype(jnp.bfloat16)
+        back = from_behind(both, "sites", offset).astype(jnp.float32)
+        key_sum = key_sum + back[:, :, :heads]
+        value_sum = value_sum + back[:, :, heads:]
     grad_keys = key_sum.astype(jnp.bfloat16).reshape(sims, local, width)
     grad_values = value_sum.astype(jnp.bfloat16).reshape(sims, local, width)
     term_query = jnp.einsum("std,ste->de", normed, grad_query, preferred_element_type=jnp.float32)
@@ -182,7 +182,10 @@
     term_output = jnp.einsum("std,ste->de", attended, cotangent, preferred_element_type=jnp.float32)
     flat_terms = jnp.stack([term_query, term_keys, term_values, term_output]).reshape(-1)
     grad_attention = lax.psum_scatter(
-        flat_terms, ("sims", "sites"), scatter_dimension=0, tiled=True
+        lax.psum_scatter(flat_terms, "sims", scatter_dimension=0, tiled=True),
+        "sites",
+        scatter_dimension=0,
+        tiled=True,
     )
     grad_normed = jnp.einsum(
         "ste,de->std", grad_query, attn_weight[0], preferred_element_type=jnp.float32
@@ -226,9 +229,14 @@
     grad_pre = (grad_pooled / haps)[:, None] * silu_slope(pre)
     term_conv = jnp.einsum("shtk,shct->kc", patches, grad_pre, precision=HIGH)
     term_bias = jnp.sum(grad_pre, axis=(0, 1, 3))
-    grad_conv, grad_bias, grad_mix, grad_embed, grad_gain = lax.psum(
-        (term_conv, term_bias, jnp.stack(mix_terms), term_embed, term_gain), ("sims", "sites")
-    )
+    small = (term_conv, term_bias, jnp.stack(mix_terms), term_embed, term_gain)
+    flat_small = lax.psum(jnp.concatenate([t.reshape(-1) for t in small]), ("sims", "sites"))
+    pieces = []
+    lower = 0
+    for t in small:
+        pieces.append(flat_small[lower : lower + t.size].reshape(t.shape))
+        lower += t.size
+    grad_conv, grad_bias, grad_mix, grad_embed, grad_gain = pieces
     return (grad_attention, grad_conv, grad_bias, grad_mix, grad_embed, grad_gain)
 
 

time: 576 us -> 870 us (1.51)
  waiting for transfers between devices: 194 us -> 681 us
  blocking collectives: 104 us -> 0 us
  starting transfers between devices: 202 us -> 102 us
    psum x0 -> x1, waiting for transfers between devices: none -> 263 us  [per_device(): lax.psum(jnp.concatenate([t.reshape(-1) for t in small]), ('sims', 'sites'))]
    unnamed x2 -> x5, waiting for transfers between devices: 169 us -> 385 us
    psum x1 -> x0, blocking collectives: 104 us -> none  [per_device(): lax.psum((term_conv, term_bias, jnp.stack(mix_terms), term_embed, term_ga...]
    ppermute x40 -> x16, starting transfers between devices: 183 us -> 79.8 us  [from_behind(): return lax.ppermute(value, axis, pairs)]
    slice x2 -> x10, local copies, waits for them, and re-layouts: 0.45 us -> 10.8 us  [the longest x5 5.09 us: per_device(): pieces.append(flat_small[lower:lower + t.size].reshape(t.shape))]
    ppermute x40 -> x16, waiting for transfers between devices: 17.6 us -> 26.6 us  [from_behind(): return lax.ppermute(value, axis, pairs)]
    unnamed x63 -> x49, local copies, waits for them, and re-layouts: 24.8 us -> 20.3 us
  transfers between devices with their start and end apart: 45 -> 23, of which waited for: 10 -> 8; matrix products, arithmetic and copies ran while one was open for 7% -> 4% of each run, Pallas kernels for 0% -> 0%
where the time goes in v1:
time: 870 us; the launch traced here: 865 us
  waiting for transfers between devices  681 us (78%)
  starting transfers between devices  102 us (12%)
  local copies, waits for them, and re-layouts  35.6 us (4%)
  matrix products  19.2 us (2%)
  between operations  16.8 us (2%)
  other arithmetic  9.7 us (1%)
    unnamed x5, waiting for transfers between devices  385 us
    psum x1, waiting for transfers between devices, per_device(): lax.psum(jnp.concatenate([t.reshape(-1) for t in small]), ('sims', 'sites'))  263 us
    ppermute x16, starting transfers between devices, from_behind(): return lax.ppermute(value, axis, pairs)  79.8 us
    ppermute x16, waiting for transfers between devices, from_behind(): return lax.ppermute(value, axis, pairs)  26.6 us
    unnamed x49, local copies, waits for them, and re-layouts  20.3 us
  transfers between devices with their start and end apart: 23, of which 8 were waited for; matrix products, arithmetic and copies ran while one was open for 4% of the time, Pallas kernels for 0%

profile of v1, /device:TPU:6, one launch (start us, length us, event | category | flops | bytes accessed | tf_op | source)
XLA Modules:
  0.0 864.8 jit_solution(17943417780981665908)
XLA Ops:
  7.2 0.9 convert_element_type.177
  8.5 4.5 fusion.16
  13.1 11.2 %collective-permute-start.1 = (f32[1,64,1]{2,1,0:T(8,128)S(1)}, f32[1,64,1]{2,1,0:T(8,128)S(1)}, u32[]{:S(2)}, u32[]{:S(2)}) collective-permute-start(f32[1,64,1]{2,1,0:T(8,128)S(1)} %get-tuple-element.31), channel_id=1, source_target_pairs={{1,0},{2,1},{3,2},{4,3},{5,4},{6,5},{7,6},{8,7},{9,8},{10,9},{11,1... | collective-permute-start | bytes 776 | tf_op jit(solution)/shard_map/ppermute | solution.py:24
  24.3 1.9 collective-permute-start
  28.3 4.8 collective-permute-done
  35.5 0.9 pad_maximum_fusion.1
  36.3 2.1 collective-permute-start.2
  38.9 4.6 collective-permute-start.3
  43.5 1.9 collective-permute-start.4
  45.5 7.8 collective-permute-start.5
  53.3 1.9 collective-permute-start.6
  55.6 10.8 %collective-permute-done.2 = bf16[1,128,1025]{2,1,0:T(8,128)(2,1)} collective-permute-done((bf16[1,128,1025]{2,1,0:T(8,128)(2,1)}, bf16[1,128,1025]{2,1,0:T(8,128)(2,1)}, u32[]{:S(2)}, u32[]{:S(2)}) %collective-permute-start.2) | collective-permute-done | bytes 262432 | tf_op jit(solution)/shard_map/ppermute | solution.py:34
  66.4 1.9 collective-permute-start.7
  68.3 1.7 constant_dynamic-update-slice_fusion.7
  70.0 21.6 %collective-permute-start.8 = (bf16[1,128,1025]{2,1,0:T(8,128)(2,1)}, bf16[1,128,1025]{2,1,0:T(8,128)(2,1)S(1)}, u32[]{:S(2)}, u32[]{:S(2)}) collective-permute-start(bf16[1,128,1025]{2,1,0:T(8,128)(2,1)} %get-tuple-element.28), channel_id=1, source_target_pairs={{0,12},{1,13},{2,14},{3,15},{4,0},{5,1},{6,2},{7,3},{8,4},{9,5},{1... | collective-permute-start | bytes 787208 | tf_op jit(solution)/shard_map/ppermute | solution.py:34
  91.6 1.7 constant_dynamic-update-slice_fusion.6
  93.3 2.1 collective-permute-start.9
  95.4 1.7 constant_dynamic-update-slice_fusion.5
  97.1 1.7 constant_dynamic-update-slice_fusion.4
  98.8 1.7 constant_dynamic-update-slice_fusion.3
  100.5 0.7 constant_dynamic-update-slice_fusion.2
  101.3 0.7 constant_dynamic-update-slice_fusion.1
  102.1 0.7 constant_dynamic-update-slice_fusion
  102.9 2.8 fusion.114
  105.7 1.7 convert_reduce_fusion
  107.4 0.7 copy.38
  108.1 1.7 copy.41
  109.8 1.5 fusion.5
  111.3 1.8 fusion.119
  113.7 1.0 bitcast_convert_fusion
  115.3 1.3 fusion.8
  117.6 5.3 collective-permute-start.10
  122.9 3.6 collective-permute-start.11
  126.5 4.6 collective-permute-start.12
  131.1 6.1 collective-permute-start.13
  137.3 1.9 collective-permute-start.14
  139.3 5.7 collective-permute-start.15
  145.0 6.8 collective-permute-start.16
  151.8 1.9 collective-permute-start.17
  153.8 1.0 convolution_convert_fusion.5
  155.6 15.6 %collective-permute-done.14 = bf16[1,128,16,64]{1,3,2,0:T(8,128)(2,1)S(1)} collective-permute-done((bf16[1,128,16,64]{1,3,2,0:T(8,128)(2,1)S(1)}, bf16[1,128,16,64]{1,3,2,0:T(8,128)(2,1)S(1)}, u32[]{:S(2)}, u32[]{:S(2)}) %collective-permute-start.14) | collective-permute-done | bytes 262176 | tf_op jit(solution)/shard_map/ppermute | solution.py:34
  173.0 3.1 copy.52
  176.4 1.3 copy-done.2
  180.6 4.1 collective-permute-start.19
  184.8 4.8 collective-permute-start.18
  189.9 1.5 collective-permute-done.18
  191.6 2.4 fusion.30
  194.1 1.0 fusion.33
  195.1 0.8 concatenate.137
  196.0 1.3 dynamic-slice
  197.9 227.0 %all-reduce.8.cloned.1.call-done = f32[1048576]{0:T(1024)} async-done(((f32[1048576]{0:T(1024)}), f32[1048576]{0:T(1024)}) %all-reduce.8.cloned.1.call-update) | async-done | bytes 4194320
  424.9 1.6 dynamic-slice.1
  426.5 1.3 dynamic-slice.2
  428.4 263.4 %all-reduce.6.cloned.1.call-done = f32[45888]{0:T(1024)} async-done(((f32[45888]{0:T(1024)}), f32[45888]{0:T(1024)}) %all-reduce.6.cloned.1.call-update) | async-done | bytes 183568 | tf_op jit(solution)/shard_map/psum | solution.py:233
  691.8 1.0 slice.309
  692.8 0.7 reshape.612
  693.5 0.9 slice.308
  694.4 0.7 reshape.611
  695.1 0.7 slice.306
  695.8 0.7 reshape.610
  696.4 1.3 slice.310
  697.7 1.2 slice.307
  698.9 158.0 %all-reduce.10.cloned.1.call-done = f32[32768]{0:T(1024)} async-done(((f32[32768]{0:T(1024)}), f32[32768]{0:T(1024)}) %all-reduce.10.cloned.1.call-update) | async-done | bytes 131088
  857.0 1.3 dynamic-slice.3
  (130 shorter events, 13.3 us)
Async XLA Ops:
  7.2 26.3 %copy-start = (f32[64,512]{1,0:T(8,128)S(1)}, f32[64,512]{1,0:T(8,128)}, u32[]{:S(2)}) copy-start(f32[64,512]{1,0:T(8,128)} %param.17) | copy-start | bytes 393220
  7.2 417.7 %all-reduce.8.cloned.1.call-start = ((), (), s32[]{:S(2)}) async-start(), calls=%async_computation.1 | async-start | bytes 8388608
  8.4 4.6 copy-start.7
  8.5 19.2 %copy-start.5 = (f32[3,64,64]{2,1,0:T(8,128)S(1)}, f32[3,64,64]{2,1,0:T(8,128)}, u32[]{:S(2)}) copy-start(f32[3,64,64]{2,1,0:T(8,128)} %param.16) | copy-start | bytes 147460
  8.5 19.4 %copy-start.15 = (bf16[1,128]{1,0:T(2,128)(2,1)S(1)}, bf16[1,128]{1,0:T(2,128)(2,1)}, u32[]{:S(2)}) copy-start(bf16[1,128]{1,0:T(2,128)(2,1)} %param.11) | copy-start | bytes 772
  8.5 26.0 %copy-start.11 = (f32[512]{0:T(512)S(1)}, f32[512]{0:T(512)}, u32[]{:S(2)}) copy-start(f32[512]{0:T(512)} %param.18) | copy-start | bytes 6148
  8.5 26.5 %copy-start.1 = (bf16[4,512,512]{2,1,0:T(8,128)(2,1)S(1)}, bf16[4,512,512]{2,1,0:T(8,128)(2,1)}, u32[]{:S(2)}) copy-start(bf16[4,512,512]{2,1,0:T(8,128)(2,1)} %param.19) | copy-start | bytes 6291460
  13.1 25.4 %copy-start.4 = (bf16[1,128,512]{2,1,0:T(8,128)(2,1)S(1)}, bf16[1,128,512]{2,1,0:T(8,128)(2,1)}, u32[]{:S(2)}) copy-start(bf16[1,128,512]{2,1,0:T(8,128)(2,1)} %param.13) | copy-start | bytes 393220
  13.1 14.9 %collective-permute-start.1 = (f32[1,64,1]{2,1,0:T(8,128)S(1)}, f32[1,64,1]{2,1,0:T(8,128)S(1)}, u32[]{:S(2)}, u32[]{:S(2)}) collective-permute-start(f32[1,64,1]{2,1,0:T(8,128)S(1)} %get-tuple-element.31), channel_id=1, source_target_pairs={{1,0},{2,1},{3,2},{4,3},{5,4},{6,5},{7,6},{8,7},{9,8},{10,9},{11,1... | collective-permute-start | bytes 776 | tf_op jit(solution)/shard_map/ppermute | solution.py:24
  24.3 8.8 %collective-permute-start = (f32[1,64,1]{2,1,0:T(8,128)S(1)}, f32[1,64,1]{2,1,0:T(8,128)S(1)}, u32[]{:S(2)}, u32[]{:S(2)}) collective-permute-start(f32[1,64,1]{2,1,0:T(8,128)S(1)} %get-tuple-element.30), channel_id=1, source_target_pairs={{0,1},{1,2},{2,3},{3,4},{4,5},{5,6},{6,7},{7,8},{8,9},{9,10},{10,1... | collective-permute-start | bytes 776 | tf_op jit(solution)/shard_map/ppermute | solution.py:22
  33.2 1.4 copy-start.9
  34.5 0.5 copy-start.13
  36.3 30.0 %collective-permute-start.2 = (bf16[1,128,1025]{2,1,0:T(8,128)(2,1)}, bf16[1,128,1025]{2,1,0:T(8,128)(2,1)}, u32[]{:S(2)}, u32[]{:S(2)}) collective-permute-start(bf16[1,128,1025]{2,1,0:T(8,128)(2,1)} %get-tuple-element.28), channel_id=1, source_target_pairs={{0,15},{1,0},{2,1},{3,2},{4,3},{5,4},{6,5},{7,6},{8,7},{9,8},{10,9... | collective-permute-start | bytes 787208 | tf_op jit(solution)/shard_map/ppermute | solution.py:34
  38.9 31.1 %collective-permute-start.3 = (bf16[1,128,1025]{2,1,0:T(8,128)(2,1)}, bf16[1,128,1025]{2,1,0:T(8,128)(2,1)}, u32[]{:S(2)}, u32[]{:S(2)}) collective-permute-start(bf16[1,128,1025]{2,1,0:T(8,128)(2,1)} %get-tuple-element.28), channel_id=1, source_target_pairs={{0,1},{1,2},{2,3},{3,4},{4,5},{5,6},{6,7},{7,8},{8,9},{9,10},{10,1... | collective-permute-start | bytes 787208 | tf_op jit(solution)/shard_map/ppermute | solution.py:34
  43.5 49.8 %collective-permute-start.4 = (bf16[1,128,1025]{2,1,0:T(8,128)(2,1)}, bf16[1,128,1025]{2,1,0:T(8,128)(2,1)}, u32[]{:S(2)}, u32[]{:S(2)}) collective-permute-start(bf16[1,128,1025]{2,1,0:T(8,128)(2,1)} %get-tuple-element.28), channel_id=1, source_target_pairs={{0,14},{1,15},{2,0},{3,1},{4,2},{5,3},{6,4},{7,5},{8,6},{9,7},{10,... | collective-permute-start | bytes 787208 | tf_op jit(solution)/shard_map/ppermute | solution.py:34
  45.5 51.7 %collective-permute-start.5 = (bf16[1,128,1025]{2,1,0:T(8,128)(2,1)}, bf16[1,128,1025]{2,1,0:T(8,128)(2,1)}, u32[]{:S(2)}, u32[]{:S(2)}) collective-permute-start(bf16[1,128,1025]{2,1,0:T(8,128)(2,1)} %get-tuple-element.28), channel_id=1, source_target_pairs={{0,2},{1,3},{2,4},{3,5},{4,6},{5,7},{6,8},{7,9},{8,10},{9,11},{10,... | collective-permute-start | bytes 787208 | tf_op jit(solution)/shard_map/ppermute | solution.py:34
  53.3 45.5 %collective-permute-start.6 = (bf16[1,128,1025]{2,1,0:T(8,128)(2,1)}, bf16[1,128,1025]{2,1,0:T(8,128)(2,1)}, u32[]{:S(2)}, u32[]{:S(2)}) collective-permute-start(bf16[1,128,1025]{2,1,0:T(8,128)(2,1)} %get-tuple-element.28), channel_id=1, source_target_pairs={{0,13},{1,14},{2,15},{3,0},{4,1},{5,2},{6,3},{7,4},{8,5},{9,6},{10... | collective-permute-start | bytes 787208 | tf_op jit(solution)/shard_map/ppermute | solution.py:34
  66.4 34.2 %collective-permute-start.7 = (bf16[1,128,1025]{2,1,0:T(8,128)(2,1)}, bf16[1,128,1025]{2,1,0:T(8,128)(2,1)S(1)}, u32[]{:S(2)}, u32[]{:S(2)}) collective-permute-start(bf16[1,128,1025]{2,1,0:T(8,128)(2,1)} %get-tuple-element.28), channel_id=1, source_target_pairs={{0,3},{1,4},{2,5},{3,6},{4,7},{5,8},{6,9},{7,10},{8,11},{9,12},{10... | collective-permute-start | bytes 787208 | tf_op jit(solution)/shard_map/ppermute | solution.py:34
  70.0 31.3 %collective-permute-start.8 = (bf16[1,128,1025]{2,1,0:T(8,128)(2,1)}, bf16[1,128,1025]{2,1,0:T(8,128)(2,1)S(1)}, u32[]{:S(2)}, u32[]{:S(2)}) collective-permute-start(bf16[1,128,1025]{2,1,0:T(8,128)(2,1)} %get-tuple-element.28), channel_id=1, source_target_pairs={{0,12},{1,13},{2,14},{3,15},{4,0},{5,1},{6,2},{7,3},{8,4},{9,5},{1... | collective-permute-start | bytes 787208 | tf_op jit(solution)/shard_map/ppermute | solution.py:34
  93.3 8.8 %collective-permute-start.9 = (bf16[1,128,1025]{2,1,0:T(8,128)(2,1)}, bf16[1,128,1025]{2,1,0:T(8,128)(2,1)S(1)}, u32[]{:S(2)}, u32[]{:S(2)}) collective-permute-start(bf16[1,128,1025]{2,1,0:T(8,128)(2,1)} %get-tuple-element.28), channel_id=1, source_target_pairs={{0,4},{1,5},{2,6},{3,7},{4,8},{5,9},{6,10},{7,11},{8,12},{9,13},{1... | collective-permute-start | bytes 787208 | tf_op jit(solution)/shard_map/ppermute | solution.py:34
  117.6 21.7 %collective-permute-start.10 = (bf16[1,128,16,64]{1,3,2,0:T(8,128)(2,1)S(1)}, bf16[1,128,16,64]{1,3,2,0:T(8,128)(2,1)S(1)}, u32[]{:S(2)}, u32[]{:S(2)}) collective-permute-start(bf16[1,128,16,64]{1,3,2,0:T(8,128)(2,1)S(1)} %pad_maximum_fusion.2), channel_id=1, source_target_pairs={{0,1},{1,2},{2,3},{3,4},{4,5},{5,6},{6,7},{7,8},{8,9},{9,10},{10,1... | collective-permute-start | bytes 786440 | tf_op jit(solution)/shard_map/ppermute | solution.py:34
  122.9 22.1 %collective-permute-start.11 = (bf16[1,128,16,64]{1,3,2,0:T(8,128)(2,1)S(1)}, bf16[1,128,16,64]{1,3,2,0:T(8,128)(2,1)S(1)}, u32[]{:S(2)}, u32[]{:S(2)}) collective-permute-start(bf16[1,128,16,64]{1,3,2,0:T(8,128)(2,1)S(1)} %pad_maximum_fusion.3), channel_id=1, source_target_pairs={{0,15},{1,0},{2,1},{3,2},{4,3},{5,4},{6,5},{7,6},{8,7},{9,8},{10,9... | collective-permute-start | bytes 786440 | tf_op jit(solution)/shard_map/ppermute | solution.py:34
  126.5 25.3 %collective-permute-start.12 = (bf16[1,128,16,64]{1,3,2,0:T(8,128)(2,1)S(1)}, bf16[1,128,16,64]{1,3,2,0:T(8,128)(2,1)S(1)}, u32[]{:S(2)}, u32[]{:S(2)}) collective-permute-start(bf16[1,128,16,64]{1,3,2,0:T(8,128)(2,1)S(1)} %pad_maximum_fusion.4), channel_id=1, source_target_pairs={{0,2},{1,3},{2,4},{3,5},{4,6},{5,7},{6,8},{7,9},{8,10},{9,11},{10,... | collective-permute-start | bytes 786440 | tf_op jit(solution)/shard_map/ppermute | solution.py:34
  131.1 24.4 %collective-permute-start.13 = (bf16[1,128,16,64]{1,3,2,0:T(8,128)(2,1)S(1)}, bf16[1,128,16,64]{1,3,2,0:T(8,128)(2,1)S(1)}, u32[]{:S(2)}, u32[]{:S(2)}) collective-permute-start(bf16[1,128,16,64]{1,3,2,0:T(8,128)(2,1)S(1)} %pad_maximum_fusion.5), channel_id=1, source_target_pairs={{0,14},{1,15},{2,0},{3,1},{4,2},{5,3},{6,4},{7,5},{8,6},{9,7},{10,... | collective-permute-start | bytes 786440 | tf_op jit(solution)/shard_map/ppermute | solution.py:34
  137.3 33.9 %collective-permute-start.14 = (bf16[1,128,16,64]{1,3,2,0:T(8,128)(2,1)S(1)}, bf16[1,128,16,64]{1,3,2,0:T(8,128)(2,1)S(1)}, u32[]{:S(2)}, u32[]{:S(2)}) collective-permute-start(bf16[1,128,16,64]{1,3,2,0:T(8,128)(2,1)S(1)} %pad_maximum_fusion.6), channel_id=1, source_target_pairs={{0,3},{1,4},{2,5},{3,6},{4,7},{5,8},{6,9},{7,10},{8,11},{9,12},{10... | collective-permute-start | bytes 786440 | tf_op jit(solution)/shard_map/ppermute | solution.py:34
  139.3 32.0 %collective-permute-start.15 = (bf16[1,128,16,64]{1,3,2,0:T(8,128)(2,1)S(1)}, bf16[1,128,16,64]{1,3,2,0:T(8,128)(2,1)S(1)}, u32[]{:S(2)}, u32[]{:S(2)}) collective-permute-start(bf16[1,128,16,64]{1,3,2,0:T(8,128)(2,1)S(1)} %pad_maximum_fusion.7), channel_id=1, source_target_pairs={{0,13},{1,14},{2,15},{3,0},{4,1},{5,2},{6,3},{7,4},{8,5},{9,6},{10... | collective-permute-start | bytes 786440 | tf_op jit(solution)/shard_map/ppermute | solution.py:34
  145.0 26.3 %collective-permute-start.16 = (bf16[1,128,16,64]{1,3,2,0:T(8,128)(2,1)S(1)}, bf16[1,128,16,64]{1,3,2,0:T(8,128)(2,1)S(1)}, u32[]{:S(2)}, u32[]{:S(2)}) collective-permute-start(bf16[1,128,16,64]{1,3,2,0:T(8,128)(2,1)S(1)} %pad_maximum_fusion.8), channel_id=1, source_target_pairs={{0,4},{1,5},{2,6},{3,7},{4,8},{5,9},{6,10},{7,11},{8,12},{9,13},{1... | collective-permute-start | bytes 786440 | tf_op jit(solution)/shard_map/ppermute | solution.py:34
  151.8 19.5 %collective-permute-start.17 = (bf16[1,128,16,64]{1,3,2,0:T(8,128)(2,1)S(1)}, bf16[1,128,16,64]{1,3,2,0:T(8,128)(2,1)S(1)}, u32[]{:S(2)}, u32[]{:S(2)}) collective-permute-start(bf16[1,128,16,64]{1,3,2,0:T(8,128)(2,1)S(1)} %pad_maximum_fusion.9), channel_id=1, source_target_pairs={{0,12},{1,13},{2,14},{3,15},{4,0},{5,1},{6,2},{7,3},{8,4},{9,5},{1... | collective-permute-start | bytes 786440 | tf_op jit(solution)/shard_map/ppermute | solution.py:34
  176.1 1.6 copy-start.2
  176.1 2.2 copy-start.12
  176.1 2.2 copy-start.14
  176.2 2.7 copy-start.16
  176.2 515.6 %all-reduce.6.cloned.1.call-start = ((), (), s32[]{:S(2)}) async-start(), calls=%async_computation | async-start | bytes 368640 | tf_op jit(solution)/shard_map/psum | solution.py:233
  178.0 1.7 copy-start.10
  178.4 6.3 copy-start.6
  178.4 13.2 %copy-start.8 = (f32[64,128,4]{1,2,0:T(4,128)S(1)}, f32[64,128,4]{1,2,0:T(4,128)}, u32[]{:S(2)}) copy-start(f32[64,128,4]{1,2,0:T(4,128)} %copy-done.7) | copy-start | bytes 393220
  178.4 13.2 %copy-start.17 = (f32[64]{0:T(128)S(1)}, f32[64]{0:T(128)}, u32[]{:S(2)}) copy-start(f32[64]{0:T(128)} %param.15) | copy-start | bytes 772
  178.8 12.8 %copy-start.3 = (f32[64,64,128]{2,0,1:T(8,128)S(1)}, f32[64,64,128]{2,0,1:T(8,128)}, u32[]{:S(2)}) copy-start(f32[64,64,128]{2,0,1:T(8,128)} %get-tuple-element.37) | copy-start | bytes 6291460
  180.6 9.0 %collective-permute-start.19 = (bf16[1,64,1]{2,1,0:T(8,128)(2,1)S(1)}, bf16[1,64,1]{2,1,0:T(8,128)(2,1)S(1)}, u32[]{:S(2)}, u32[]{:S(2)}) collective-permute-start(bf16[1,64,1]{2,1,0:T(8,128)(2,1)S(1)} %get-tuple-element.33), channel_id=1, source_target_pairs={{0,1},{1,2},{2,3},{3,4},{4,5},{5,6},{6,7},{7,8},{8,9},{9,10},{10,1... | collective-permute-start | bytes 392 | tf_op jit(solution)/shard_map/ppermute | solution.py:22
  184.8 6.5 collective-permute-start.18
  195.9 661.1 %all-reduce.10.cloned.1.call-start = ((), (), s32[]{:S(2)}) async-start(), calls=%async_computation.2 | async-start | bytes 262144
Sparse Core Ops, SparseCore 0:
  176.3 248.5 all-reduce.7
  429.9 261.8 all-reduce.5
  694.9 161.9 all-reduce.9

commit v2 on v1

--- a/solution.py
+++ b/solution.py
@@ -61,6 +61,50 @@
     apart = jnp.minimum(apart, cycle_tokens - apart)
     inside = apart[None, None] <= limit[:, None, None, None]
     return (scores, inside)
+
+
+def bit_count(size):
+    bits = size.bit_length() - 1
+    assert 1 << bits == size
+    return bits
+
+
+def butterfly_sum(flat, small):
+    sims_bits = bit_count(lax.axis_size("sims"))
+    sites_bits = bit_count(lax.axis_size("sites"))
+    total_bits = sims_bits + sites_bits
+    chunk = flat.shape[0] >> total_bits
+    cells = flat.reshape((2,) * total_bits + (chunk,))
+    dim_of = {}
+    for bit in range(sims_bits):
+        dim_of[("sims", bit)] = sims_bits - 1 - bit
+    for bit in range(sites_bits):
+        dim_of[("sites", bit)] = total_bits - 1 - bit
+    order = [("sims", 0), ("sims", sims_bits - 1)]
+    pending = [("sims", b) for b in range(1, sims_bits - 1)]
+    pending_sites = [("sites", b) for b in (2, 3, 0, 1) if b < sites_bits]
+    pending_sites += [("sites", b) for b in range(sites_bits) if ("sites", b) not in pending_sites]
+    while pending or pending_sites:
+        if pending:
+            order.append(pending.pop(0))
+        if pending_sites:
+            order.append(pending_sites.pop(0))
+    order = list(dict.fromkeys(order))
+    kept_dims = list(range(total_bits))
+    for axis, bit in order:
+        dim = kept_dims.index(dim_of[(axis, bit)])
+        kept_dims.pop(dim)
+        count = lax.axis_size(axis)
+        mine = (lax.axis_index(axis) >> bit) & 1
+        keep = lax.dynamic_index_in_dim(cells, mine, axis=dim, keepdims=False)
+        send = lax.dynamic_index_in_dim(cells, 1 - mine, axis=dim, keepdims=False)
+        shape = keep.shape
+        outgoing = jnp.concatenate([send.reshape(-1), small])
+        pairs = [(i, i ^ (1 << bit)) for i in range(count)]
+        incoming = lax.ppermute(outgoing, axis, pairs)
+        cells = keep + incoming[: keep.size].reshape(shape)
+        small = small + incoming[keep.size :]
+    return cells.reshape(chunk), small
 
 
 def per_device(
@@ -181,12 +225,6 @@
     term_values = jnp.einsum("std,ste->de", normed, grad_values, preferred_element_type=jnp.float32)
     term_output = jnp.einsum("std,ste->de", attended, cotangent, preferred_element_type=jnp.float32)
     flat_terms = jnp.stack([term_query, term_keys, term_values, term_output]).reshape(-1)
-    grad_attention = lax.psum_scatter(
-        lax.psum_scatter(flat_terms, "sims", scatter_dimension=0, tiled=True),
-        "sites",
-        scatter_dimension=0,
-        tiled=True,
-    )
     grad_normed = jnp.einsum(
         "ste,de->std", grad_query, attn_weight[0], preferred_element_type=jnp.float32
     )
@@ -230,7 +268,8 @@
     term_conv = jnp.einsum("shtk,shct->kc", patches, grad_pre, precision=HIGH)
     term_bias = jnp.sum(grad_pre, axis=(0, 1, 3))
     small = (term_conv, term_bias, jnp.stack(mix_terms), term_embed, term_gain)
-    flat_small = lax.psum(jnp.concatenate([t.reshape(-1) for t in small]), ("sims", "sites"))
+    flat_small = jnp.concatenate([t.reshape(-1) for t in small])
+    grad_attention, flat_small = butterfly_sum(flat_terms, flat_small)
     pieces = []
     lower = 0
     for t in small:

time: 870 us -> 386 us (0.44)
  waiting for transfers between devices: 681 us -> 148 us
  starting transfers between devices: 102 us -> 132 us
  local copies, waits for them, and re-layouts: 35.6 us -> 54.4 us
  between operations: 16.8 us -> 2.89 us
  other arithmetic: 9.7 us -> 22.7 us
    unnamed x5 -> x0, waiting for transfers between devices: 385 us -> none
    psum x1 -> x0, waiting for transfers between devices: 263 us -> none  [per_device(): lax.psum(jnp.concatenate([t.reshape(-1) for t in small]), ('sims', 'sites'))]
    ppermute x0 -> x9, waiting for transfers between devices: none -> 105 us  [butterfly_sum(): incoming = lax.ppermute(outgoing, axis, pairs)]
    ppermute x0 -> x9, starting transfers between devices: none -> 33 us  [butterfly_sum(): incoming = lax.ppermute(outgoing, axis, pairs)]
    concatenate x1 -> x2, local copies, waits for them, and re-layouts: 0.82 us -> 14.6 us  [the longest x1 14.5 us: butterfly_sum(): outgoing = jnp.concatenate([send.reshape(-1), small])]
    ppermute x16, waiting for transfers between devices: 26.6 us -> 37.6 us  [from_behind(): return lax.ppermute(value, axis, pairs)]
    add x0 -> x18, other arithmetic: none -> 9.36 us  [the longest x9 7.31 us: butterfly_sum(): cells = keep + incoming[:keep.size].reshape(shape)]
    unnamed x49 -> x64, local copies, waits for them, and re-layouts: 20.3 us -> 12.1 us
  transfers between devices with their start and end apart: 23 -> 29, of which waited for: 8 -> 14; matrix products, arithmetic and copies ran while one was open for 4% -> 8% of each run, Pallas kernels for 0% -> 0%
where the time goes in v2:
time: 386 us; the launch traced here: 383 us
  waiting for transfers between devices  148 us (38%)
  starting transfers between devices  132 us (34%)
  local copies, waits for them, and re-layouts  54.4 us (14%)
  matrix products  23.4 us (6%)
  other arithmetic  22.7 us (6%)
    ppermute x9, waiting for transfers between devices, butterfly_sum(): incoming = lax.ppermute(outgoing, axis, pairs)  105 us
    ppermute x16, starting transfers between devices, from_behind(): return lax.ppermute(value, axis, pairs)  77 us
    ppermute x16, waiting for transfers between devices, from_behind(): return lax.ppermute(value, axis, pairs)  37.6 us
    ppermute x9, starting transfers between devices, butterfly_sum(): incoming = lax.ppermute(outgoing, axis, pairs)  33 us
    ppermute x2, starting transfers between devices, extended(): lax.ppermute(head, axis, [((i + 1) % count, i) for i in range(count)])  15.6 us
    concatenate x1, local copies, waits for them, and re-layouts, butterfly_sum(): outgoing = jnp.concatenate([send.reshape(-1), small])  14.5 us
    unnamed x64, local copies, waits for them, and re-layouts  12.1 us
  transfers between devices with their start and end apart: 29, of which 14 were waited for; matrix products, arithmetic and copies ran while one was open for 8% of the time, Pallas kernels for 0%

profile of v2, /device:TPU:6, one launch (start us, length us, event | category | flops | bytes accessed | tf_op | source)
XLA Modules:
  0.0 383.2 jit_solution(14314522591504527704)
XLA Ops:
  1.9 4.5 %fusion.16 = (f32[64,128]{1,0:T(8,128)S(1)}, f32[64,64,128]{2,0,1:T(8,128)}) fusion(f32[64]{0:T(128)} %param.15, f32[64,128,4]{1,2,0:T(4,128)S(1)} %copy.28, f32[4,64]{1,0:T(4,128)} %param.14), kind=kOutput, calls=%fused_computation.26 | convolution fusion | flops 28303360 | bytes 2262272 | tf_op jit(solution)/shard_map/shtk,kc->shct/dot_general | solution.py:134
  6.5 11.3 %collective-permute-start.1 = (f32[1,64,1]{2,1,0:T(8,128)S(1)}, f32[1,64,1]{2,1,0:T(8,128)S(1)}, u32[]{:S(2)}, u32[]{:S(2)}) collective-permute-start(f32[1,64,1]{2,1,0:T(8,128)S(1)} %get-tuple-element.33), channel_id=1, source_target_pairs={{1,0},{2,1},{3,2},{4,3},{5,4},{6,5},{7,6},{8,7},{9,8},{10,9},{11,1... | collective-permute-start | bytes 776 | tf_op jit(solution)/shard_map/ppermute | solution.py:24
  17.9 1.9 collective-permute-start
  21.8 4.8 %collective-permute-done = f32[1,64,1]{2,1,0:T(8,128)S(1)} collective-permute-done((f32[1,64,1]{2,1,0:T(8,128)S(1)}, f32[1,64,1]{2,1,0:T(8,128)S(1)}, u32[]{:S(2)}, u32[]{:S(2)}) %collective-permute-start) | collective-permute-done | bytes 288 | tf_op jit(solution)/shard_map/ppermute | solution.py:22
  28.9 2.1 collective-permute-start.2
  31.5 4.6 %collective-permute-start.3 = (bf16[1,128,1025]{2,1,0:T(8,128)(2,1)}, bf16[1,128,1025]{2,1,0:T(8,128)(2,1)}, u32[]{:S(2)}, u32[]{:S(2)}) collective-permute-start(bf16[1,128,1025]{2,1,0:T(8,128)(2,1)} %get-tuple-element.28), channel_id=1, source_target_pairs={{0,1},{1,2},{2,3},{3,4},{4,5},{5,6},{6,7},{7,8},{8,9},{9,10},{10,1... | collective-permute-start | bytes 787208 | tf_op jit(solution)/shard_map/ppermute | solution.py:34
  36.2 1.9 collective-permute-start.4
  38.1 7.8 %collective-permute-start.5 = (bf16[1,128,1025]{2,1,0:T(8,128)(2,1)}, bf16[1,128,1025]{2,1,0:T(8,128)(2,1)}, u32[]{:S(2)}, u32[]{:S(2)}) collective-permute-start(bf16[1,128,1025]{2,1,0:T(8,128)(2,1)} %get-tuple-element.28), channel_id=1, source_target_pairs={{0,2},{1,3},{2,4},{3,5},{4,6},{5,7},{6,8},{7,9},{8,10},{9,11},{10,... | collective-permute-start | bytes 787208 | tf_op jit(solution)/shard_map/ppermute | solution.py:34
  45.9 1.9 collective-permute-start.6
  48.2 10.7 %collective-permute-done.2 = bf16[1,128,1025]{2,1,0:T(8,128)(2,1)} collective-permute-done((bf16[1,128,1025]{2,1,0:T(8,128)(2,1)}, bf16[1,128,1025]{2,1,0:T(8,128)(2,1)}, u32[]{:S(2)}, u32[]{:S(2)}) %collective-permute-start.2) | collective-permute-done | bytes 262432 | tf_op jit(solution)/shard_map/ppermute | solution.py:34
  59.0 1.9 collective-permute-start.7
  60.9 1.7 constant_dynamic-update-slice_fusion.7
  62.6 21.6 %collective-permute-start.8 = (bf16[1,128,1025]{2,1,0:T(8,128)(2,1)}, bf16[1,128,1025]{2,1,0:T(8,128)(2,1)S(1)}, u32[]{:S(2)}, u32[]{:S(2)}) collective-permute-start(bf16[1,128,1025]{2,1,0:T(8,128)(2,1)} %get-tuple-element.28), channel_id=1, source_target_pairs={{0,12},{1,13},{2,14},{3,15},{4,0},{5,1},{6,2},{7,3},{8,4},{9,5},{1... | collective-permute-start | bytes 787208 | tf_op jit(solution)/shard_map/ppermute | solution.py:34
  84.2 1.7 constant_dynamic-update-slice_fusion.6
  85.9 1.9 collective-permute-start.9
  87.8 1.7 constant_dynamic-update-slice_fusion.5
  89.5 1.7 constant_dynamic-update-slice_fusion.4
  91.2 1.7 constant_dynamic-update-slice_fusion.3
  95.5 2.8 fusion.114
  100.2 1.7 copy.33
  102.7 1.8 fusion.119
  108.9 3.8 collective-permute-start.17
  112.7 3.4 collective-permute-start.16
  116.2 4.5 %collective-permute-start.15 = (bf16[1,128,16,64]{1,3,2,0:T(8,128)(2,1)S(1)}, bf16[1,128,16,64]{1,3,2,0:T(8,128)(2,1)S(1)}, u32[]{:S(2)}, u32[]{:S(2)}) collective-permute-start(bf16[1,128,16,64]{1,3,2,0:T(8,128)(2,1)S(1)} %pad_maximum_fusion.11), channel_id=1, source_target_pairs={{0,13},{1,14},{2,15},{3,0},{4,1},{5,2},{6,3},{7,4},{8,5},{9,6},{10... | collective-permute-start | bytes 786440 | tf_op jit(solution)/shard_map/ppermute | solution.py:34
  120.8 3.4 collective-permute-start.14
  124.2 5.6 %collective-permute-start.13 = (bf16[1,128,16,64]{1,3,2,0:T(8,128)(2,1)S(1)}, bf16[1,128,16,64]{1,3,2,0:T(8,128)(2,1)S(1)}, u32[]{:S(2)}, u32[]{:S(2)}) collective-permute-start(bf16[1,128,16,64]{1,3,2,0:T(8,128)(2,1)S(1)} %pad_maximum_fusion.9), channel_id=1, source_target_pairs={{0,14},{1,15},{2,0},{3,1},{4,2},{5,3},{6,4},{7,5},{8,6},{9,7},{10,... | collective-permute-start | bytes 786440 | tf_op jit(solution)/shard_map/ppermute | solution.py:34
  131.2 4.2 %collective-permute-start.12 = (bf16[1,128,16,64]{1,3,2,0:T(8,128)(2,1)S(1)}, bf16[1,128,16,64]{1,3,2,0:T(8,128)(2,1)S(1)}, u32[]{:S(2)}, u32[]{:S(2)}) collective-permute-start(bf16[1,128,16,64]{1,3,2,0:T(8,128)(2,1)S(1)} %pad_maximum_fusion.8), channel_id=1, source_target_pairs={{0,2},{1,3},{2,4},{3,5},{4,6},{5,7},{6,8},{7,9},{8,10},{9,11},{10,... | collective-permute-start | bytes 786440 | tf_op jit(solution)/shard_map/ppermute | solution.py:34
  135.4 4.5 %collective-permute-start.11 = (bf16[1,128,16,64]{1,3,2,0:T(8,128)(2,1)S(1)}, bf16[1,128,16,64]{1,3,2,0:T(8,128)(2,1)S(1)}, u32[]{:S(2)}, u32[]{:S(2)}) collective-permute-start(bf16[1,128,16,64]{1,3,2,0:T(8,128)(2,1)S(1)} %pad_maximum_fusion.7), channel_id=1, source_target_pairs={{0,15},{1,0},{2,1},{3,2},{4,3},{5,4},{6,5},{7,6},{8,7},{9,8},{10,9... | collective-permute-start | bytes 786440 | tf_op jit(solution)/shard_map/ppermute | solution.py:34
  140.0 3.7 collective-permute-start.10
  144.5 17.5 %collective-permute-done.14 = bf16[1,128,16,64]{1,3,2,0:T(8,128)(2,1)S(1)} collective-permute-done((bf16[1,128,16,64]{1,3,2,0:T(8,128)(2,1)S(1)}, bf16[1,128,16,64]{1,3,2,0:T(8,128)(2,1)S(1)}, u32[]{:S(2)}, u32[]{:S(2)}) %collective-permute-start.14) | collective-permute-done | bytes 262176 | tf_op jit(solution)/shard_map/ppermute | solution.py:34
  162.1 9.1 %collective-permute-done.11 = bf16[1,128,16,64]{1,3,2,0:T(8,128)(2,1)S(1)} collective-permute-done((bf16[1,128,16,64]{1,3,2,0:T(8,128)(2,1)S(1)}, bf16[1,128,16,64]{1,3,2,0:T(8,128)(2,1)S(1)}, u32[]{:S(2)}, u32[]{:S(2)}) %collective-permute-start.11) | collective-permute-done | bytes 262176 | tf_op jit(solution)/shard_map/ppermute | solution.py:34
  174.3 1.5 fusion.70
  177.1 1.3 convolution_bitcast_fusion.4
  178.4 4.6 %collective-permute-start.19 = (bf16[1,64,1]{2,1,0:T(8,128)(2,1)}, bf16[1,64,1]{2,1,0:T(8,128)(2,1)}, u32[]{:S(2)}, u32[]{:S(2)}) collective-permute-start(bf16[1,64,1]{2,1,0:T(8,128)(2,1)} %get-tuple-element.37), channel_id=1, source_target_pairs={{0,1},{1,2},{2,3},{3,4},{4,5},{5,6},{6,7},{7,8},{8,9},{9,10},{10,1... | collective-permute-start | bytes 392 | tf_op jit(solution)/shard_map/ppermute | solution.py:22
  183.0 4.2 %collective-permute-start.18 = (bf16[1,64,1]{2,1,0:T(8,128)(2,1)}, bf16[1,64,1]{2,1,0:T(8,128)(2,1)}, u32[]{:S(2)}, u32[]{:S(2)}) collective-permute-start(bf16[1,64,1]{2,1,0:T(8,128)(2,1)} %get-tuple-element.36), channel_id=1, source_target_pairs={{1,0},{2,1},{3,2},{4,3},{5,4},{6,5},{7,6},{8,7},{9,8},{10,9},{11,1... | collective-permute-start | bytes 392 | tf_op jit(solution)/shard_map/ppermute | solution.py:24
  189.7 3.9 %pad_maximum_fusion = f32[4,512,512]{2,1,0:T(8,128)} fusion(f32[1,512,512]{2,1,0:T(8,128)S(1)} %convolution_bitcast_fusion.2, f32[1,512,512]{2,1,0:T(8,128)S(1)} %convolution_bitcast_fusion.3, f32[1,512,512]{2,1,0:T(8,128)} %convolution_bitcast_fusion.4, f32[1,512,512]{2,1,0:T(8,128)S(1)} %convolution_bitcast_fusion.5), kind=kLoop, calls=%fused_computation.10 | loop fusion | flops 3145728 | bytes 8388608 | tf_op jit(solution)/shard_map/stack | solution.py:227
  193.5 6.4 %reshape_reshape.3 = f32[2,2,2,2,2,2,2,2,2,2048]{9,8,7,6,5,4,3,2,1,0:T(2,128)} reshape(f32[4,512,512]{2,1,0:T(8,128)} %pad_maximum_fusion) | data formatting | bytes 8388608 | tf_op jit(solution)/shard_map/reshape;reshape | solution.py:77
  199.9 1.8 constant_dynamic-slice_fusion.9
  204.5 2.4 fusion.30
  208.0 14.5 %concatenate.165 = f32[570176]{0:T(1024)} concatenate(f32[524288]{0:T(1024)S(1)} %bitcast.277, f32[256]{0:T(256)S(1)} %reshape.727, f32[64]{0:T(128)S(1)} %fusion.33, f32[12288]{0:T(1024)S(1)} %copy-done.8, f32[32768]{0:T(1024)S(1)} %bitcast.295, f32[512]{0:T(512)S(1)} %copy-done.21), dimensions={0} | concatenate | bytes 4561408 | tf_op jit(solution)/shard_map/concatenate | solution.py:102
  222.4 2.1 collective-permute-start.20
  224.7 4.4 %collective-permute-done.20 = f32[570176]{0:T(1024)} collective-permute-done((f32[570176]{0:T(1024)}, f32[570176]{0:T(1024)}, u32[]{:S(2)}, u32[]{:S(2)}) %collective-permute-start.20) | collective-permute-done | bytes 2280736 | tf_op jit(solution)/shard_map/ppermute | solution.py:104
  229.1 1.7 slice.459
  230.8 2.2 reshape.731
  233.0 4.1 %bitcast_add_fusion = f32[2,2,2,2,2,2,2,2,2048]{8,7,6,5,4,3,2,1,0:T(2,128)S(1)} fusion(f32[2,2,2,2,2,2,2,2,2048]{8,7,6,5,4,3,2,1,0:T(2,128)} %reshape.731, f32[2,2,2,2,2,2,2,2,2,2048]{9,8,7,6,5,4,3,2,1,0:T(2,128)} %reshape_reshape.3, s32[]{:T(128)S(6)} %select_n.133), kind=kLoop, calls=%fused_computation.19 | loop fusion | flops 524288 | bytes 6291460 | tf_op jit(solution)/shard_map/add | solution.py:105
  239.4 3.4 collective-permute-start.21
  242.8 27.9 %collective-permute-done.21 = f32[308032]{0:T(1024)} collective-permute-done((f32[308032]{0:T(1024)}, f32[308032]{0:T(1024)}, u32[]{:S(2)}, u32[]{:S(2)}) %collective-permute-start.21) | collective-permute-done | bytes 1232160 | tf_op jit(solution)/shard_map/ppermute | solution.py:104
  270.7 1.3 slice.461
  272.0 1.5 reshape.733
  273.5 2.0 bitcast_add_fusion.2
  276.6 3.5 collective-permute-start.22
  280.1 15.5 %collective-permute-done.22 = f32[176960]{0:T(1024)S(1)} collective-permute-done((f32[176960]{0:T(1024)S(1)}, f32[176960]{0:T(1024)S(1)}, u32[]{:S(2)}, u32[]{:S(2)}) %collective-permute-start.22) | collective-permute-done | bytes 707872 | tf_op jit(solution)/shard_map/ppermute | solution.py:104
  296.4 1.9 collective-permute-start.23
  298.3 10.5 %collective-permute-done.23 = f32[111424]{0:T(1024)S(1)} collective-permute-done((f32[111424]{0:T(1024)S(1)}, f32[111424]{0:T(1024)S(1)}, u32[]{:S(2)}, u32[]{:S(2)}) %collective-permute-start.23) | collective-permute-done | bytes 445728 | tf_op jit(solution)/shard_map/ppermute | solution.py:104
  309.2 4.5 %collective-permute-start.24 = (f32[78656]{0:T(1024)S(1)}, f32[78656]{0:T(1024)S(1)}, u32[]{:S(2)}, u32[]{:S(2)}) collective-permute-start(f32[78656]{0:T(1024)S(1)} %pad_maximum_fusion.4), channel_id=1, source_target_pairs={{0,64},{16,80},{32,96},{48,112},{64,0},{80,16},{96,32},{112,48},{1... | collective-permute-start | bytes 943880 | tf_op jit(solution)/shard_map/ppermute | solution.py:104
  313.8 11.9 %collective-permute-done.24 = f32[78656]{0:T(1024)S(1)} collective-permute-done((f32[78656]{0:T(1024)S(1)}, f32[78656]{0:T(1024)S(1)}, u32[]{:S(2)}, u32[]{:S(2)}) %collective-permute-start.24) | collective-permute-done | bytes 314656 | tf_op jit(solution)/shard_map/ppermute | solution.py:104
  325.9 3.3 collective-permute-start.25
  329.2 7.0 %collective-permute-done.25 = f32[62272]{0:T(1024)S(1)} collective-permute-done((f32[62272]{0:T(1024)S(1)}, f32[62272]{0:T(1024)S(1)}, u32[]{:S(2)}, u32[]{:S(2)}) %collective-permute-start.25) | collective-permute-done | bytes 249120 | tf_op jit(solution)/shard_map/ppermute | solution.py:104
  336.4 8.7 %collective-permute-start.26 = (f32[54080]{0:T(1024)S(1)}, f32[54080]{0:T(1024)S(1)}, u32[]{:S(2)}, u32[]{:S(2)}) collective-permute-start(f32[54080]{0:T(1024)S(1)} %pad_maximum_fusion.15), channel_id=1, source_target_pairs={{0,128},{16,144},{32,160},{48,176},{64,192},{80,208},{96,224},{112... | collective-permute-start | bytes 648968 | tf_op jit(solution)/shard_map/ppermute | solution.py:104
  345.1 7.5 %collective-permute-done.26 = f32[54080]{0:T(1024)S(1)} collective-permute-done((f32[54080]{0:T(1024)S(1)}, f32[54080]{0:T(1024)S(1)}, u32[]{:S(2)}, u32[]{:S(2)}) %collective-permute-start.26) | collective-permute-done | bytes 216352 | tf_op jit(solution)/shard_map/ppermute | solution.py:104
  352.8 2.4 collective-permute-start.27
  355.2 9.8 %collective-permute-done.27 = f32[49984]{0:T(1024)S(1)} collective-permute-done((f32[49984]{0:T(1024)S(1)}, f32[49984]{0:T(1024)S(1)}, u32[]{:S(2)}, u32[]{:S(2)}) %collective-permute-start.27) | collective-permute-done | bytes 199968 | tf_op jit(solution)/shard_map/ppermute | solution.py:104
  365.2 3.1 collective-permute-start.28
  368.3 10.9 %collective-permute-done.28 = f32[47936]{0:T(1024)S(1)} collective-permute-done((f32[47936]{0:T(1024)S(1)}, f32[47936]{0:T(1024)S(1)}, u32[]{:S(2)}, u32[]{:S(2)}) %collective-permute-start.28) | collective-permute-done | bytes 191776 | tf_op jit(solution)/shard_map/ppermute | solution.py:104
  (205 shorter events, 37.0 us)
Async XLA Ops:
  0.6 26.3 %copy-start = (f32[64,512]{1,0:T(8,128)S(1)}, f32[64,512]{1,0:T(8,128)}, u32[]{:S(2)}) copy-start(f32[64,512]{1,0:T(8,128)} %param.17) | copy-start | bytes 393220
  1.9 4.5 %copy-start.13 = (f32[64,128,4]{1,2,0:T(4,128)}, f32[64,128,4]{1,2,0:T(4,128)S(1)}, u32[]{:S(2)}) copy-start(f32[64,128,4]{1,2,0:T(4,128)S(1)} %copy.28) | copy-start | bytes 393220
  1.9 19.3 %copy-start.9 = (f32[3,64,64]{2,1,0:T(8,128)S(1)}, f32[3,64,64]{2,1,0:T(8,128)}, u32[]{:S(2)}) copy-start(f32[3,64,64]{2,1,0:T(8,128)} %param.16) | copy-start | bytes 147460
  1.9 19.5 %copy-start.22 = (bf16[1,128]{1,0:T(2,128)(2,1)S(1)}, bf16[1,128]{1,0:T(2,128)(2,1)}, u32[]{:S(2)}) copy-start(bf16[1,128]{1,0:T(2,128)(2,1)} %param.11) | copy-start | bytes 772
  1.9 25.6 %copy-start.20 = (f32[512]{0:T(512)S(1)}, f32[512]{0:T(512)}, u32[]{:S(2)}) copy-start(f32[512]{0:T(512)} %param.18) | copy-start | bytes 6148
  1.9 25.7 %copy-start.2 = (bf16[4,512,512]{2,1,0:T(8,128)(2,1)S(1)}, bf16[4,512,512]{2,1,0:T(8,128)(2,1)}, u32[]{:S(2)}) copy-start(bf16[4,512,512]{2,1,0:T(8,128)(2,1)} %param.19) | copy-start | bytes 6291460
  6.4 21.1 %copy-start.11 = (f32[64,128]{1,0:T(8,128)}, f32[64,128]{1,0:T(8,128)S(1)}, u32[]{:S(2)}) copy-start(f32[64,128]{1,0:T(8,128)S(1)} %get-tuple-element.40) | copy-start | bytes 98308
  6.4 21.0 %copy-start.5 = (f32[1,64,128]{2,1,0:T(8,128)}, f32[1,64,128]{2,1,0:T(8,128)S(1)}, u32[]{:S(2)}) copy-start(f32[1,64,128]{2,1,0:T(8,128)S(1)} %multiply_bitcast_fusion) | copy-start | bytes 98308
  6.5 24.5 %copy-start.7 = (bf16[1,128,512]{2,1,0:T(8,128)(2,1)S(1)}, bf16[1,128,512]{2,1,0:T(8,128)(2,1)}, u32[]{:S(2)}) copy-start(bf16[1,128,512]{2,1,0:T(8,128)(2,1)} %param.13) | copy-start | bytes 393220
  6.5 15.0 %collective-permute-start.1 = (f32[1,64,1]{2,1,0:T(8,128)S(1)}, f32[1,64,1]{2,1,0:T(8,128)S(1)}, u32[]{:S(2)}, u32[]{:S(2)}) collective-permute-start(f32[1,64,1]{2,1,0:T(8,128)S(1)} %get-tuple-element.33), channel_id=1, source_target_pairs={{1,0},{2,1},{3,2},{4,3},{5,4},{6,5},{7,6},{8,7},{9,8},{10,9},{11,1... | collective-permute-start | bytes 776 | tf_op jit(solution)/shard_map/ppermute | solution.py:24
  17.9 8.8 %collective-permute-start = (f32[1,64,1]{2,1,0:T(8,128)S(1)}, f32[1,64,1]{2,1,0:T(8,128)S(1)}, u32[]{:S(2)}, u32[]{:S(2)}) collective-permute-start(f32[1,64,1]{2,1,0:T(8,128)S(1)} %get-tuple-element.32), channel_id=1, source_target_pairs={{0,1},{1,2},{2,3},{3,4},{4,5},{5,6},{6,7},{7,8},{8,9},{9,10},{10,1... | collective-permute-start | bytes 776 | tf_op jit(solution)/shard_map/ppermute | solution.py:22
  21.6 9.8 %copy-start.16 = (f32[1,64,1]{2,1,0:T(8,128)}, f32[1,64,1]{2,1,0:T(8,128)S(1)}, u32[]{:S(2)}) copy-start(f32[1,64,1]{2,1,0:T(8,128)S(1)} %collective-permute-done.1) | copy-start | bytes 772
  26.7 4.7 %copy-start.18 = (f32[1,64,1]{2,1,0:T(8,128)}, f32[1,64,1]{2,1,0:T(8,128)S(1)}, u32[]{:S(2)}) copy-start(f32[1,64,1]{2,1,0:T(8,128)S(1)} %collective-permute-done) | copy-start | bytes 772
  28.9 30.0 %collective-permute-start.2 = (bf16[1,128,1025]{2,1,0:T(8,128)(2,1)}, bf16[1,128,1025]{2,1,0:T(8,128)(2,1)}, u32[]{:S(2)}, u32[]{:S(2)}) collective-permute-start(bf16[1,128,1025]{2,1,0:T(8,128)(2,1)} %get-tuple-element.28), channel_id=1, source_target_pairs={{0,15},{1,0},{2,1},{3,2},{4,3},{5,4},{6,5},{7,6},{8,7},{9,8},{10,9... | collective-permute-start | bytes 787208 | tf_op jit(solution)/shard_map/ppermute | solution.py:34
  31.5 31.1 %collective-permute-start.3 = (bf16[1,128,1025]{2,1,0:T(8,128)(2,1)}, bf16[1,128,1025]{2,1,0:T(8,128)(2,1)}, u32[]{:S(2)}, u32[]{:S(2)}) collective-permute-start(bf16[1,128,1025]{2,1,0:T(8,128)(2,1)} %get-tuple-element.28), channel_id=1, source_target_pairs={{0,1},{1,2},{2,3},{3,4},{4,5},{5,6},{6,7},{7,8},{8,9},{9,10},{10,1... | collective-permute-start | bytes 787208 | tf_op jit(solution)/shard_map/ppermute | solution.py:34
  36.2 49.8 %collective-permute-start.4 = (bf16[1,128,1025]{2,1,0:T(8,128)(2,1)}, bf16[1,128,1025]{2,1,0:T(8,128)(2,1)}, u32[]{:S(2)}, u32[]{:S(2)}) collective-permute-start(bf16[1,128,1025]{2,1,0:T(8,128)(2,1)} %get-tuple-element.28), channel_id=1, source_target_pairs={{0,14},{1,15},{2,0},{3,1},{4,2},{5,3},{6,4},{7,5},{8,6},{9,7},{10,... | collective-permute-start | bytes 787208 | tf_op jit(solution)/shard_map/ppermute | solution.py:34
  38.1 51.5 %collective-permute-start.5 = (bf16[1,128,1025]{2,1,0:T(8,128)(2,1)}, bf16[1,128,1025]{2,1,0:T(8,128)(2,1)}, u32[]{:S(2)}, u32[]{:S(2)}) collective-permute-start(bf16[1,128,1025]{2,1,0:T(8,128)(2,1)} %get-tuple-element.28), channel_id=1, source_target_pairs={{0,2},{1,3},{2,4},{3,5},{4,6},{5,7},{6,8},{7,9},{8,10},{9,11},{10,... | collective-permute-start | bytes 787208 | tf_op jit(solution)/shard_map/ppermute | solution.py:34
  45.9 45.3 %collective-permute-start.6 = (bf16[1,128,1025]{2,1,0:T(8,128)(2,1)}, bf16[1,128,1025]{2,1,0:T(8,128)(2,1)}, u32[]{:S(2)}, u32[]{:S(2)}) collective-permute-start(bf16[1,128,1025]{2,1,0:T(8,128)(2,1)} %get-tuple-element.28), channel_id=1, source_target_pairs={{0,13},{1,14},{2,15},{3,0},{4,1},{5,2},{6,3},{7,4},{8,5},{9,6},{10... | collective-permute-start | bytes 787208 | tf_op jit(solution)/shard_map/ppermute | solution.py:34
  59.0 34.0 %collective-permute-start.7 = (bf16[1,128,1025]{2,1,0:T(8,128)(2,1)}, bf16[1,128,1025]{2,1,0:T(8,128)(2,1)S(1)}, u32[]{:S(2)}, u32[]{:S(2)}) collective-permute-start(bf16[1,128,1025]{2,1,0:T(8,128)(2,1)} %get-tuple-element.28), channel_id=1, source_target_pairs={{0,3},{1,4},{2,5},{3,6},{4,7},{5,8},{6,9},{7,10},{8,11},{9,12},{10... | collective-permute-start | bytes 787208 | tf_op jit(solution)/shard_map/ppermute | solution.py:34
  62.6 31.1 %collective-permute-start.8 = (bf16[1,128,1025]{2,1,0:T(8,128)(2,1)}, bf16[1,128,1025]{2,1,0:T(8,128)(2,1)S(1)}, u32[]{:S(2)}, u32[]{:S(2)}) collective-permute-start(bf16[1,128,1025]{2,1,0:T(8,128)(2,1)} %get-tuple-element.28), channel_id=1, source_target_pairs={{0,12},{1,13},{2,14},{3,15},{4,0},{5,1},{6,2},{7,3},{8,4},{9,5},{1... | collective-permute-start | bytes 787208 | tf_op jit(solution)/shard_map/ppermute | solution.py:34
  85.9 8.8 %collective-permute-start.9 = (bf16[1,128,1025]{2,1,0:T(8,128)(2,1)}, bf16[1,128,1025]{2,1,0:T(8,128)(2,1)S(1)}, u32[]{:S(2)}, u32[]{:S(2)}) collective-permute-start(bf16[1,128,1025]{2,1,0:T(8,128)(2,1)} %get-tuple-element.28), channel_id=1, source_target_pairs={{0,4},{1,5},{2,6},{3,7},{4,8},{5,9},{6,10},{7,11},{8,12},{9,13},{1... | collective-permute-start | bytes 787208 | tf_op jit(solution)/shard_map/ppermute | solution.py:34
  108.9 22.3 %collective-permute-start.17 = (bf16[1,128,16,64]{1,3,2,0:T(8,128)(2,1)S(1)}, bf16[1,128,16,64]{1,3,2,0:T(8,128)(2,1)S(1)}, u32[]{:S(2)}, u32[]{:S(2)}) collective-permute-start(bf16[1,128,16,64]{1,3,2,0:T(8,128)(2,1)S(1)} %pad_maximum_fusion.13), channel_id=1, source_target_pairs={{0,12},{1,13},{2,14},{3,15},{4,0},{5,1},{6,2},{7,3},{8,4},{9,5},{1... | collective-permute-start | bytes 786440 | tf_op jit(solution)/shard_map/ppermute | solution.py:34
  112.7 22.7 %collective-permute-start.16 = (bf16[1,128,16,64]{1,3,2,0:T(8,128)(2,1)S(1)}, bf16[1,128,16,64]{1,3,2,0:T(8,128)(2,1)S(1)}, u32[]{:S(2)}, u32[]{:S(2)}) collective-permute-start(bf16[1,128,16,64]{1,3,2,0:T(8,128)(2,1)S(1)} %pad_maximum_fusion.12), channel_id=1, source_target_pairs={{0,4},{1,5},{2,6},{3,7},{4,8},{5,9},{6,10},{7,11},{8,12},{9,13},{1... | collective-permute-start | bytes 786440 | tf_op jit(solution)/shard_map/ppermute | solution.py:34
  116.2 23.8 %collective-permute-start.15 = (bf16[1,128,16,64]{1,3,2,0:T(8,128)(2,1)S(1)}, bf16[1,128,16,64]{1,3,2,0:T(8,128)(2,1)S(1)}, u32[]{:S(2)}, u32[]{:S(2)}) collective-permute-start(bf16[1,128,16,64]{1,3,2,0:T(8,128)(2,1)S(1)} %pad_maximum_fusion.11), channel_id=1, source_target_pairs={{0,13},{1,14},{2,15},{3,0},{4,1},{5,2},{6,3},{7,4},{8,5},{9,6},{10... | collective-permute-start | bytes 786440 | tf_op jit(solution)/shard_map/ppermute | solution.py:34
  120.8 41.2 %collective-permute-start.14 = (bf16[1,128,16,64]{1,3,2,0:T(8,128)(2,1)S(1)}, bf16[1,128,16,64]{1,3,2,0:T(8,128)(2,1)S(1)}, u32[]{:S(2)}, u32[]{:S(2)}) collective-permute-start(bf16[1,128,16,64]{1,3,2,0:T(8,128)(2,1)S(1)} %pad_maximum_fusion.10), channel_id=1, source_target_pairs={{0,3},{1,4},{2,5},{3,6},{4,7},{5,8},{6,9},{7,10},{8,11},{9,12},{10... | collective-permute-start | bytes 786440 | tf_op jit(solution)/shard_map/ppermute | solution.py:34
  124.2 37.8 %collective-permute-start.13 = (bf16[1,128,16,64]{1,3,2,0:T(8,128)(2,1)S(1)}, bf16[1,128,16,64]{1,3,2,0:T(8,128)(2,1)S(1)}, u32[]{:S(2)}, u32[]{:S(2)}) collective-permute-start(bf16[1,128,16,64]{1,3,2,0:T(8,128)(2,1)S(1)} %pad_maximum_fusion.9), channel_id=1, source_target_pairs={{0,14},{1,15},{2,0},{3,1},{4,2},{5,3},{6,4},{7,5},{8,6},{9,7},{10,... | collective-permute-start | bytes 786440 | tf_op jit(solution)/shard_map/ppermute | solution.py:34
  130.2 13.8 %copy-start.3 = (bf16[4,512,512]{2,1,0:T(8,128)(2,1)S(1)}, bf16[4,512,512]{2,1,0:T(8,128)(2,1)}, u32[]{:S(2)}) copy-start(bf16[4,512,512]{2,1,0:T(8,128)(2,1)} %param.19) | copy-start | bytes 6291460
  131.2 30.8 %collective-permute-start.12 = (bf16[1,128,16,64]{1,3,2,0:T(8,128)(2,1)S(1)}, bf16[1,128,16,64]{1,3,2,0:T(8,128)(2,1)S(1)}, u32[]{:S(2)}, u32[]{:S(2)}) collective-permute-start(bf16[1,128,16,64]{1,3,2,0:T(8,128)(2,1)S(1)} %pad_maximum_fusion.8), channel_id=1, source_target_pairs={{0,2},{1,3},{2,4},{3,5},{4,6},{5,7},{6,8},{7,9},{8,10},{9,11},{10,... | collective-permute-start | bytes 786440 | tf_op jit(solution)/shard_map/ppermute | solution.py:34
  135.4 35.8 %collective-permute-start.11 = (bf16[1,128,16,64]{1,3,2,0:T(8,128)(2,1)S(1)}, bf16[1,128,16,64]{1,3,2,0:T(8,128)(2,1)S(1)}, u32[]{:S(2)}, u32[]{:S(2)}) collective-permute-start(bf16[1,128,16,64]{1,3,2,0:T(8,128)(2,1)S(1)} %pad_maximum_fusion.7), channel_id=1, source_target_pairs={{0,15},{1,0},{2,1},{3,2},{4,3},{5,4},{6,5},{7,6},{8,7},{9,8},{10,9... | collective-permute-start | bytes 786440 | tf_op jit(solution)/shard_map/ppermute | solution.py:34
  140.0 31.3 %collective-permute-start.10 = (bf16[1,128,16,64]{1,3,2,0:T(8,128)(2,1)S(1)}, bf16[1,128,16,64]{1,3,2,0:T(8,128)(2,1)S(1)}, u32[]{:S(2)}, u32[]{:S(2)}) collective-permute-start(bf16[1,128,16,64]{1,3,2,0:T(8,128)(2,1)S(1)} %pad_maximum_fusion.6), channel_id=1, source_target_pairs={{0,1},{1,2},{2,3},{3,4},{4,5},{5,6},{6,7},{7,8},{8,9},{9,10},{10,1... | collective-permute-start | bytes 786440 | tf_op jit(solution)/shard_map/ppermute | solution.py:34
  173.0 14.2 %copy-start.12 = (f32[64,128]{1,0:T(8,128)S(1)}, f32[64,128]{1,0:T(8,128)}, u32[]{:S(2)}) copy-start(f32[64,128]{1,0:T(8,128)} %copy-done.11) | copy-start | bytes 98308
  173.2 14.3 %copy-start.6 = (f32[1,64,128]{2,1,0:T(8,128)S(1)}, f32[1,64,128]{2,1,0:T(8,128)}, u32[]{:S(2)}) copy-start(f32[1,64,128]{2,1,0:T(8,128)} %copy-done.5) | copy-start | bytes 98308
  173.2 14.3 %copy-start.17 = (f32[1,64,1]{2,1,0:T(8,128)S(1)}, f32[1,64,1]{2,1,0:T(8,128)}, u32[]{:S(2)}) copy-start(f32[1,64,1]{2,1,0:T(8,128)} %copy-done.16) | copy-start | bytes 772
  173.2 14.5 %copy-start.19 = (f32[1,64,1]{2,1,0:T(8,128)S(1)}, f32[1,64,1]{2,1,0:T(8,128)}, u32[]{:S(2)}) copy-start(f32[1,64,1]{2,1,0:T(8,128)} %copy-done.18) | copy-start | bytes 772
  178.4 23.5 %collective-permute-start.19 = (bf16[1,64,1]{2,1,0:T(8,128)(2,1)}, bf16[1,64,1]{2,1,0:T(8,128)(2,1)}, u32[]{:S(2)}, u32[]{:S(2)}) collective-permute-start(bf16[1,64,1]{2,1,0:T(8,128)(2,1)} %get-tuple-element.37), channel_id=1, source_target_pairs={{0,1},{1,2},{2,3},{3,4},{4,5},{5,6},{6,7},{7,8},{8,9},{9,10},{10,1... | collective-permute-start | bytes 392 | tf_op jit(solution)/shard_map/ppermute | solution.py:22
  183.0 20.5 %collective-permute-start.18 = (bf16[1,64,1]{2,1,0:T(8,128)(2,1)}, bf16[1,64,1]{2,1,0:T(8,128)(2,1)}, u32[]{:S(2)}, u32[]{:S(2)}) collective-permute-start(bf16[1,64,1]{2,1,0:T(8,128)(2,1)} %get-tuple-element.36), channel_id=1, source_target_pairs={{1,0},{2,1},{3,2},{4,3},{5,4},{6,5},{7,6},{8,7},{9,8},{10,9},{11,1... | collective-permute-start | bytes 392 | tf_op jit(solution)/shard_map/ppermute | solution.py:24
  201.7 0.9 copy-start.10
  201.7 1.8 copy-start.15
  201.7 2.8 copy-start.4
  201.7 2.8 copy-start.14
  201.7 2.8 copy-start.23
  206.9 1.1 copy-start.8
  206.9 1.1 copy-start.21
  222.4 6.6 %collective-permute-start.20 = (f32[570176]{0:T(1024)}, f32[570176]{0:T(1024)}, u32[]{:S(2)}, u32[]{:S(2)}) collective-permute-start(f32[570176]{0:T(1024)} %concatenate.165), channel_id=1, source_target_pairs={{0,16},{16,0},{32,48},{48,32},{64,80},{80,64},{96,112},{112,96},{1... | collective-permute-start | bytes 6842120 | tf_op jit(solution)/shard_map/ppermute | solution.py:104
  239.4 31.3 %collective-permute-start.21 = (f32[308032]{0:T(1024)}, f32[308032]{0:T(1024)}, u32[]{:S(2)}, u32[]{:S(2)}) collective-permute-start(f32[308032]{0:T(1024)} %pad_maximum_fusion.1), channel_id=1, source_target_pairs={{0,256},{16,272},{32,288},{48,304},{64,320},{80,336},{96,352},{112... | collective-permute-start | bytes 3696392 | tf_op jit(solution)/shard_map/ppermute | solution.py:104
  276.6 19.0 %collective-permute-start.22 = (f32[176960]{0:T(1024)S(1)}, f32[176960]{0:T(1024)S(1)}, u32[]{:S(2)}, u32[]{:S(2)}) collective-permute-start(f32[176960]{0:T(1024)S(1)} %pad_maximum_fusion.2), channel_id=1, source_target_pairs={{0,32},{16,48},{32,0},{48,16},{64,96},{80,112},{96,64},{112,80},{1... | collective-permute-start | bytes 2123528 | tf_op jit(solution)/shard_map/ppermute | solution.py:104
  296.4 12.4 %collective-permute-start.23 = (f32[111424]{0:T(1024)S(1)}, f32[111424]{0:T(1024)S(1)}, u32[]{:S(2)}, u32[]{:S(2)}) collective-permute-start(f32[111424]{0:T(1024)S(1)} %pad_maximum_fusion.3), channel_id=1, source_target_pairs={{0,4},{1,5},{2,6},{3,7},{4,0},{5,1},{6,2},{7,3},{8,12},{9,13},{10,... | collective-permute-start | bytes 1337096 | tf_op jit(solution)/shard_map/ppermute | solution.py:104
  309.2 16.4 %collective-permute-start.24 = (f32[78656]{0:T(1024)S(1)}, f32[78656]{0:T(1024)S(1)}, u32[]{:S(2)}, u32[]{:S(2)}) collective-permute-start(f32[78656]{0:T(1024)S(1)} %pad_maximum_fusion.4), channel_id=1, source_target_pairs={{0,64},{16,80},{32,96},{48,112},{64,0},{80,16},{96,32},{112,48},{1... | collective-permute-start | bytes 943880 | tf_op jit(solution)/shard_map/ppermute | solution.py:104
  325.9 10.3 %collective-permute-start.25 = (f32[62272]{0:T(1024)S(1)}, f32[62272]{0:T(1024)S(1)}, u32[]{:S(2)}, u32[]{:S(2)}) collective-permute-start(f32[62272]{0:T(1024)S(1)} %pad_maximum_fusion.14), channel_id=1, source_target_pairs={{0,8},{1,9},{2,10},{3,11},{4,12},{5,13},{6,14},{7,15},{8,0},{9,1},... | collective-permute-start | bytes 747272 | tf_op jit(solution)/shard_map/ppermute | solution.py:104
  336.3 46.9 %copy-start.1 = (f32[64,512]{1,0:T(8,128)S(1)}, f32[64,512]{1,0:T(8,128)}, u32[]{:S(2)}) copy-start(f32[64,512]{1,0:T(8,128)} %param.17) | copy-start | bytes 393220
  336.4 16.3 %collective-permute-start.26 = (f32[54080]{0:T(1024)S(1)}, f32[54080]{0:T(1024)S(1)}, u32[]{:S(2)}, u32[]{:S(2)}) collective-permute-start(f32[54080]{0:T(1024)S(1)} %pad_maximum_fusion.15), channel_id=1, source_target_pairs={{0,128},{16,144},{32,160},{48,176},{64,192},{80,208},{96,224},{112... | collective-permute-start | bytes 648968 | tf_op jit(solution)/shard_map/ppermute | solution.py:104
  352.8 12.3 %collective-permute-start.27 = (f32[49984]{0:T(1024)S(1)}, f32[49984]{0:T(1024)S(1)}, u32[]{:S(2)}, u32[]{:S(2)}) collective-permute-start(f32[49984]{0:T(1024)S(1)} %pad_maximum_fusion.16), channel_id=1, source_target_pairs={{0,1},{1,0},{2,3},{3,2},{4,5},{5,4},{6,7},{7,6},{8,9},{9,8},{10,11... | collective-permute-start | bytes 599816 | tf_op jit(solution)/shard_map/ppermute | solution.py:104
  365.2 14.0 %collective-permute-start.28 = (f32[47936]{0:T(1024)S(1)}, f32[47936]{0:T(1024)S(1)}, u32[]{:S(2)}, u32[]{:S(2)}) collective-permute-start(f32[47936]{0:T(1024)S(1)} %pad_maximum_fusion.17), channel_id=1, source_target_pairs={{0,2},{1,3},{2,0},{3,1},{4,6},{5,7},{6,4},{7,5},{8,10},{9,11},{10,... | collective-permute-start | bytes 575240 | tf_op jit(solution)/shard_map/ppermute | solution.py:104

commit v3 on v2

--- a/solution.py
+++ b/solution.py
@@ -74,7 +74,6 @@
     sites_bits = bit_count(lax.axis_size("sites"))
     total_bits = sims_bits + sites_bits
     chunk = flat.shape[0] >> total_bits
-    cells = flat.reshape((2,) * total_bits + (chunk,))
     dim_of = {}
     for bit in range(sims_bits):
         dim_of[("sims", bit)] = sims_bits - 1 - bit
@@ -90,22 +89,21 @@
         if pending_sites:
             order.append(pending_sites.pop(0))
     order = list(dict.fromkeys(order))
-    kept_dims = list(range(total_bits))
+    cells = flat.reshape((2,) * total_bits + (chunk // 512, 512))
+    cells = cells.transpose([dim_of[o] for o in order] + [total_bits, total_bits + 1])
+    current = cells.reshape(-1)
     for axis, bit in order:
-        dim = kept_dims.index(dim_of[(axis, bit)])
-        kept_dims.pop(dim)
         count = lax.axis_size(axis)
+        half = current.shape[0] // 2
         mine = (lax.axis_index(axis) >> bit) & 1
-        keep = lax.dynamic_index_in_dim(cells, mine, axis=dim, keepdims=False)
-        send = lax.dynamic_index_in_dim(cells, 1 - mine, axis=dim, keepdims=False)
-        shape = keep.shape
-        outgoing = jnp.concatenate([send.reshape(-1), small])
+        keep = lax.dynamic_slice_in_dim(current, mine * half, half)
+        send = lax.dynamic_slice_in_dim(current, (1 - mine) * half, half)
+        outgoing = jnp.concatenate([send, small])
         pairs = [(i, i ^ (1 << bit)) for i in range(count)]
         incoming = lax.ppermute(outgoing, axis, pairs)
-        cells = keep + incoming[: keep.size].reshape(shape)
-        small = small + incoming[keep.size :]
-    return cells.reshape(chunk), small
-
+        current = keep + incoming[:half]
+        small = small + incoming[half:]
+    return current, small
 
 def per_device(
     genotypes,

time: 386 us -> 379 us (0.982)
  local copies, waits for them, and re-layouts: 54.4 us -> 48.6 us
    reshape x9 -> x1, local copies, waits for them, and re-layouts: 4.37 us -> 0.14 us  [the longest x8 4.24 us: butterfly_sum(): cells = keep + incoming[:keep.size].reshape(shape)]
    another operation x1 -> x2, local copies, waits for them, and re-layouts: 6.36 us -> 8.62 us  [butterfly_sum(): cells = flat.reshape((2,) * total_bits + (chunk // 512, 512))]
    unnamed x64 -> x59, local copies, waits for them, and re-layouts: 12.1 us -> 12.9 us
  transfers between devices with their start and end apart: 29 -> 29, of which waited for: 14 -> 14; matrix products, arithmetic and copies ran while one was open for 8% -> 9% of each run, Pallas kernels for 0% -> 0%
where the time goes in v3:
time: 379 us; the launch traced here: 376 us
  waiting for transfers between devices  148 us (39%)
  starting transfers between devices  132 us (35%)
  local copies, waits for them, and re-layouts  48.6 us (13%)
  matrix products  24.7 us (7%)
  other arithmetic  19.8 us (5%)
    ppermute x9, waiting for transfers between devices, butterfly_sum(): incoming = lax.ppermute(outgoing, axis, pairs)  105 us
    ppermute x16, starting transfers between devices, from_behind(): return lax.ppermute(value, axis, pairs)  76.9 us
    ppermute x16, waiting for transfers between devices, from_behind(): return lax.ppermute(value, axis, pairs)  37.7 us
    ppermute x9, starting transfers between devices, butterfly_sum(): incoming = lax.ppermute(outgoing, axis, pairs)  33 us
    ppermute x2, starting transfers between devices, extended(): lax.ppermute(head, axis, [((i + 1) % count, i) for i in range(count)])  15.4 us
    concatenate x1, local copies, waits for them, and re-layouts, butterfly_sum(): outgoing = jnp.concatenate([send, small])  14.6 us
    unnamed x59, local copies, waits for them, and re-layouts  12.9 us
    another operation x2, local copies, waits for them, and re-layouts, butterfly_sum(): cells = flat.reshape((2,) * total_bits + (chunk // 512, 512))  8.62 us
  transfers between devices with their start and end apart: 29, of which 14 were waited for; matrix products, arithmetic and copies ran while one was open for 9% of the time, Pallas kernels for 0%

profile of v3, /device:TPU:6, one launch (start us, length us, event | category | flops | bytes accessed | tf_op | source)
XLA Modules:
  0.0 375.7 jit_solution(2948103269441927480)
XLA Ops:
  1.9 4.5 %fusion.16 = (f32[64,128]{1,0:T(8,128)S(1)}, f32[64,64,128]{2,0,1:T(8,128)}) fusion(f32[64]{0:T(128)} %param.15, f32[64,128,4]{1,2,0:T(4,128)S(1)} %copy.28, f32[4,64]{1,0:T(4,128)} %param.14), kind=kOutput, calls=%fused_computation.26 | convolution fusion | flops 28303360 | bytes 2262272 | tf_op jit(solution)/shard_map/shtk,kc->shct/dot_general | solution.py:132
  6.5 11.2 %collective-permute-start.1 = (f32[1,64,1]{2,1,0:T(8,128)S(1)}, f32[1,64,1]{2,1,0:T(8,128)S(1)}, u32[]{:S(2)}, u32[]{:S(2)}) collective-permute-start(f32[1,64,1]{2,1,0:T(8,128)S(1)} %get-tuple-element.31), channel_id=1, source_target_pairs={{1,0},{2,1},{3,2},{4,3},{5,4},{6,5},{7,6},{8,7},{9,8},{10,9},{11,1... | collective-permute-start | bytes 776 | tf_op jit(solution)/shard_map/ppermute | solution.py:24
  17.7 1.9 collective-permute-start
  21.7 4.8 %collective-permute-done = f32[1,64,1]{2,1,0:T(8,128)S(1)} collective-permute-done((f32[1,64,1]{2,1,0:T(8,128)S(1)}, f32[1,64,1]{2,1,0:T(8,128)S(1)}, u32[]{:S(2)}, u32[]{:S(2)}) %collective-permute-start) | collective-permute-done | bytes 288 | tf_op jit(solution)/shard_map/ppermute | solution.py:22
  28.8 2.1 collective-permute-start.2
  31.4 4.6 %collective-permute-start.3 = (bf16[1,128,1025]{2,1,0:T(8,128)(2,1)}, bf16[1,128,1025]{2,1,0:T(8,128)(2,1)}, u32[]{:S(2)}, u32[]{:S(2)}) collective-permute-start(bf16[1,128,1025]{2,1,0:T(8,128)(2,1)} %get-tuple-element.28), channel_id=1, source_target_pairs={{0,1},{1,2},{2,3},{3,4},{4,5},{5,6},{6,7},{7,8},{8,9},{9,10},{10,1... | collective-permute-start | bytes 787208 | tf_op jit(solution)/shard_map/ppermute | solution.py:34
  36.0 1.9 collective-permute-start.4
  38.0 7.8 %collective-permute-start.5 = (bf16[1,128,1025]{2,1,0:T(8,128)(2,1)}, bf16[1,128,1025]{2,1,0:T(8,128)(2,1)}, u32[]{:S(2)}, u32[]{:S(2)}) collective-permute-start(bf16[1,128,1025]{2,1,0:T(8,128)(2,1)} %get-tuple-element.28), channel_id=1, source_target_pairs={{0,2},{1,3},{2,4},{3,5},{4,6},{5,7},{6,8},{7,9},{8,10},{9,11},{10,... | collective-permute-start | bytes 787208 | tf_op jit(solution)/shard_map/ppermute | solution.py:34
  45.8 1.9 collective-permute-start.6
  48.1 10.8 %collective-permute-done.2 = bf16[1,128,1025]{2,1,0:T(8,128)(2,1)} collective-permute-done((bf16[1,128,1025]{2,1,0:T(8,128)(2,1)}, bf16[1,128,1025]{2,1,0:T(8,128)(2,1)}, u32[]{:S(2)}, u32[]{:S(2)}) %collective-permute-start.2) | collective-permute-done | bytes 262432 | tf_op jit(solution)/shard_map/ppermute | solution.py:34
  58.9 1.9 collective-permute-start.7
  60.9 1.7 constant_dynamic-update-slice_fusion.7
  62.6 21.5 %collective-permute-start.8 = (bf16[1,128,1025]{2,1,0:T(8,128)(2,1)}, bf16[1,128,1025]{2,1,0:T(8,128)(2,1)S(1)}, u32[]{:S(2)}, u32[]{:S(2)}) collective-permute-start(bf16[1,128,1025]{2,1,0:T(8,128)(2,1)} %get-tuple-element.28), channel_id=1, source_target_pairs={{0,12},{1,13},{2,14},{3,15},{4,0},{5,1},{6,2},{7,3},{8,4},{9,5},{1... | collective-permute-start | bytes 787208 | tf_op jit(solution)/shard_map/ppermute | solution.py:34
  84.1 1.7 constant_dynamic-update-slice_fusion.6
  85.8 1.9 collective-permute-start.9
  87.7 1.7 constant_dynamic-update-slice_fusion.5
  89.4 1.7 constant_dynamic-update-slice_fusion.4
  91.1 1.7 constant_dynamic-update-slice_fusion.3
  95.4 2.8 fusion.114
  98.2 1.1 convert_reduce_fusion
  100.0 1.7 copy.33
  102.5 1.8 fusion.119
  106.4 1.3 fusion.8
  108.7 3.8 %collective-permute-start.17 = (bf16[1,128,16,64]{1,3,2,0:T(8,128)(2,1)S(1)}, bf16[1,128,16,64]{1,3,2,0:T(8,128)(2,1)S(1)}, u32[]{:S(2)}, u32[]{:S(2)}) collective-permute-start(bf16[1,128,16,64]{1,3,2,0:T(8,128)(2,1)S(1)} %pad_maximum_fusion.13), channel_id=1, source_target_pairs={{0,12},{1,13},{2,14},{3,15},{4,0},{5,1},{6,2},{7,3},{8,4},{9,5},{1... | collective-permute-start | bytes 786440 | tf_op jit(solution)/shard_map/ppermute | solution.py:34
  112.6 3.4 collective-permute-start.16
  116.1 4.5 %collective-permute-start.15 = (bf16[1,128,16,64]{1,3,2,0:T(8,128)(2,1)S(1)}, bf16[1,128,16,64]{1,3,2,0:T(8,128)(2,1)S(1)}, u32[]{:S(2)}, u32[]{:S(2)}) collective-permute-start(bf16[1,128,16,64]{1,3,2,0:T(8,128)(2,1)S(1)} %pad_maximum_fusion.11), channel_id=1, source_target_pairs={{0,13},{1,14},{2,15},{3,0},{4,1},{5,2},{6,3},{7,4},{8,5},{9,6},{10... | collective-permute-start | bytes 786440 | tf_op jit(solution)/shard_map/ppermute | solution.py:34
  120.6 3.4 collective-permute-start.14
  124.1 5.6 %collective-permute-start.13 = (bf16[1,128,16,64]{1,3,2,0:T(8,128)(2,1)S(1)}, bf16[1,128,16,64]{1,3,2,0:T(8,128)(2,1)S(1)}, u32[]{:S(2)}, u32[]{:S(2)}) collective-permute-start(bf16[1,128,16,64]{1,3,2,0:T(8,128)(2,1)S(1)} %pad_maximum_fusion.9), channel_id=1, source_target_pairs={{0,14},{1,15},{2,0},{3,1},{4,2},{5,3},{6,4},{7,5},{8,6},{9,7},{10,... | collective-permute-start | bytes 786440 | tf_op jit(solution)/shard_map/ppermute | solution.py:34
  131.1 4.1 %collective-permute-start.12 = (bf16[1,128,16,64]{1,3,2,0:T(8,128)(2,1)S(1)}, bf16[1,128,16,64]{1,3,2,0:T(8,128)(2,1)S(1)}, u32[]{:S(2)}, u32[]{:S(2)}) collective-permute-start(bf16[1,128,16,64]{1,3,2,0:T(8,128)(2,1)S(1)} %pad_maximum_fusion.8), channel_id=1, source_target_pairs={{0,2},{1,3},{2,4},{3,5},{4,6},{5,7},{6,8},{7,9},{8,10},{9,11},{10,... | collective-permute-start | bytes 786440 | tf_op jit(solution)/shard_map/ppermute | solution.py:34
  135.3 4.6 %collective-permute-start.11 = (bf16[1,128,16,64]{1,3,2,0:T(8,128)(2,1)S(1)}, bf16[1,128,16,64]{1,3,2,0:T(8,128)(2,1)S(1)}, u32[]{:S(2)}, u32[]{:S(2)}) collective-permute-start(bf16[1,128,16,64]{1,3,2,0:T(8,128)(2,1)S(1)} %pad_maximum_fusion.7), channel_id=1, source_target_pairs={{0,15},{1,0},{2,1},{3,2},{4,3},{5,4},{6,5},{7,6},{8,7},{9,8},{10,9... | collective-permute-start | bytes 786440 | tf_op jit(solution)/shard_map/ppermute | solution.py:34
  139.8 3.7 collective-permute-start.10
  144.4 17.4 %collective-permute-done.14 = bf16[1,128,16,64]{1,3,2,0:T(8,128)(2,1)S(1)} collective-permute-done((bf16[1,128,16,64]{1,3,2,0:T(8,128)(2,1)S(1)}, bf16[1,128,16,64]{1,3,2,0:T(8,128)(2,1)S(1)}, u32[]{:S(2)}, u32[]{:S(2)}) %collective-permute-start.14) | collective-permute-done | bytes 262176 | tf_op jit(solution)/shard_map/ppermute | solution.py:34
  161.9 9.1 %collective-permute-done.11 = bf16[1,128,16,64]{1,3,2,0:T(8,128)(2,1)S(1)} collective-permute-done((bf16[1,128,16,64]{1,3,2,0:T(8,128)(2,1)S(1)}, bf16[1,128,16,64]{1,3,2,0:T(8,128)(2,1)S(1)}, u32[]{:S(2)}, u32[]{:S(2)}) %collective-permute-start.11) | collective-permute-done | bytes 262176 | tf_op jit(solution)/shard_map/ppermute | solution.py:34
  174.2 1.5 fusion.70
  177.0 1.3 convolution_bitcast_fusion.4
  178.3 4.6 %collective-permute-start.19 = (bf16[1,64,1]{2,1,0:T(8,128)(2,1)}, bf16[1,64,1]{2,1,0:T(8,128)(2,1)}, u32[]{:S(2)}, u32[]{:S(2)}) collective-permute-start(bf16[1,64,1]{2,1,0:T(8,128)(2,1)} %get-tuple-element.33), channel_id=1, source_target_pairs={{0,1},{1,2},{2,3},{3,4},{4,5},{5,6},{6,7},{7,8},{8,9},{9,10},{10,1... | collective-permute-start | bytes 392 | tf_op jit(solution)/shard_map/ppermute | solution.py:22
  182.9 4.2 %collective-permute-start.18 = (bf16[1,64,1]{2,1,0:T(8,128)(2,1)}, bf16[1,64,1]{2,1,0:T(8,128)(2,1)}, u32[]{:S(2)}, u32[]{:S(2)}) collective-permute-start(bf16[1,64,1]{2,1,0:T(8,128)(2,1)} %get-tuple-element.32), channel_id=1, source_target_pairs={{1,0},{2,1},{3,2},{4,3},{5,4},{6,5},{7,6},{8,7},{9,8},{10,9},{11,1... | collective-permute-start | bytes 392 | tf_op jit(solution)/shard_map/ppermute | solution.py:24
  189.5 3.8 %pad_maximum_fusion = f32[4,512,512]{2,1,0:T(8,128)} fusion(f32[1,512,512]{2,1,0:T(8,128)S(1)} %convolution_bitcast_fusion.2, f32[1,512,512]{2,1,0:T(8,128)S(1)} %convolution_bitcast_fusion.3, f32[1,512,512]{2,1,0:T(8,128)} %convolution_bitcast_fusion.4, f32[1,512,512]{2,1,0:T(8,128)S(1)} %convolution_bitcast_fusion.5), kind=kLoop, calls=%fused_computation.10 | loop fusion | flops 3145728 | bytes 8388608 | tf_op jit(solution)/shard_map/stack | solution.py:225
  193.4 5.2 %reshape_reshape.3 = f32[2,2,2,2,2,2,2,2,2,4,512]{10,9,8,7,6,5,4,3,2,1,0:T(4,128)} reshape(f32[4,512,512]{2,1,0:T(8,128)} %pad_maximum_fusion) | data formatting | bytes 8388608 | tf_op jit(solution)/shard_map/reshape;reshape | solution.py:92
  198.6 3.4 copy.34
  204.1 2.2 fusion.66
  207.3 2.4 fusion.30
  210.8 14.6 %concatenate.165 = f32[570176]{0:T(1024)} concatenate(f32[524288]{0:T(1024)S(1)} %dynamic_slice.55, f32[256]{0:T(256)S(1)} %reshape.674, f32[64]{0:T(128)S(1)} %fusion.33, f32[12288]{0:T(1024)S(1)} %copy-done.9, f32[32768]{0:T(1024)S(1)} %bitcast.261, f32[512]{0:T(512)S(1)} %copy-done.22), dimensions={0} | concatenate | bytes 4561408 | tf_op jit(solution)/shard_map/concatenate | solution.py:101
  225.3 1.9 collective-permute-start.20
  227.4 4.6 %collective-permute-done.20 = f32[570176]{0:T(1024)} collective-permute-done((f32[570176]{0:T(1024)}, f32[570176]{0:T(1024)}, u32[]{:S(2)}, u32[]{:S(2)}) %collective-permute-start.20) | collective-permute-done | bytes 2280736 | tf_op jit(solution)/shard_map/ppermute | solution.py:103
  232.0 2.4 slice_add_fusion
  235.4 1.1 pad_maximum_fusion.1
  236.6 3.4 collective-permute-start.21
  240.0 27.9 %collective-permute-done.21 = f32[308032]{0:T(1024)} collective-permute-done((f32[308032]{0:T(1024)}, f32[308032]{0:T(1024)}, u32[]{:S(2)}, u32[]{:S(2)}) %collective-permute-start.21) | collective-permute-done | bytes 1232160 | tf_op jit(solution)/shard_map/ppermute | solution.py:103
  267.9 1.3 slice_add_fusion.1
  270.3 3.5 collective-permute-start.22
  273.8 15.5 %collective-permute-done.22 = f32[176960]{0:T(1024)S(1)} collective-permute-done((f32[176960]{0:T(1024)S(1)}, f32[176960]{0:T(1024)S(1)}, u32[]{:S(2)}, u32[]{:S(2)}) %collective-permute-start.22) | collective-permute-done | bytes 707872 | tf_op jit(solution)/shard_map/ppermute | solution.py:103
  289.5 1.9 collective-permute-start.23
  291.4 10.5 %collective-permute-done.23 = f32[111424]{0:T(1024)S(1)} collective-permute-done((f32[111424]{0:T(1024)S(1)}, f32[111424]{0:T(1024)S(1)}, u32[]{:S(2)}, u32[]{:S(2)}) %collective-permute-start.23) | collective-permute-done | bytes 445728 | tf_op jit(solution)/shard_map/ppermute | solution.py:103
  302.0 4.5 %collective-permute-start.24 = (f32[78656]{0:T(1024)S(1)}, f32[78656]{0:T(1024)S(1)}, u32[]{:S(2)}, u32[]{:S(2)}) collective-permute-start(f32[78656]{0:T(1024)S(1)} %pad_maximum_fusion.4), channel_id=1, source_target_pairs={{0,64},{16,80},{32,96},{48,112},{64,0},{80,16},{96,32},{112,48},{1... | collective-permute-start | bytes 943880 | tf_op jit(solution)/shard_map/ppermute | solution.py:103
  306.6 11.8 %collective-permute-done.24 = f32[78656]{0:T(1024)S(1)} collective-permute-done((f32[78656]{0:T(1024)S(1)}, f32[78656]{0:T(1024)S(1)}, u32[]{:S(2)}, u32[]{:S(2)}) %collective-permute-start.24) | collective-permute-done | bytes 314656 | tf_op jit(solution)/shard_map/ppermute | solution.py:103
  318.5 3.3 collective-permute-start.25
  321.8 7.0 %collective-permute-done.25 = f32[62272]{0:T(1024)S(1)} collective-permute-done((f32[62272]{0:T(1024)S(1)}, f32[62272]{0:T(1024)S(1)}, u32[]{:S(2)}, u32[]{:S(2)}) %collective-permute-start.25) | collective-permute-done | bytes 249120 | tf_op jit(solution)/shard_map/ppermute | solution.py:103
  328.9 8.7 %collective-permute-start.26 = (f32[54080]{0:T(1024)S(1)}, f32[54080]{0:T(1024)S(1)}, u32[]{:S(2)}, u32[]{:S(2)}) collective-permute-start(f32[54080]{0:T(1024)S(1)} %pad_maximum_fusion.15), channel_id=1, source_target_pairs={{0,128},{16,144},{32,160},{48,176},{64,192},{80,208},{96,224},{112... | collective-permute-start | bytes 648968 | tf_op jit(solution)/shard_map/ppermute | solution.py:103
  337.6 7.5 %collective-permute-done.26 = f32[54080]{0:T(1024)S(1)} collective-permute-done((f32[54080]{0:T(1024)S(1)}, f32[54080]{0:T(1024)S(1)}, u32[]{:S(2)}, u32[]{:S(2)}) %collective-permute-start.26) | collective-permute-done | bytes 216352 | tf_op jit(solution)/shard_map/ppermute | solution.py:103
  345.2 2.5 collective-permute-start.27
  347.7 9.8 %collective-permute-done.27 = f32[49984]{0:T(1024)S(1)} collective-permute-done((f32[49984]{0:T(1024)S(1)}, f32[49984]{0:T(1024)S(1)}, u32[]{:S(2)}, u32[]{:S(2)}) %collective-permute-start.27) | collective-permute-done | bytes 199968 | tf_op jit(solution)/shard_map/ppermute | solution.py:103
  357.6 3.2 collective-permute-start.28
  360.7 10.9 %collective-permute-done.28 = f32[47936]{0:T(1024)S(1)} collective-permute-done((f32[47936]{0:T(1024)S(1)}, f32[47936]{0:T(1024)S(1)}, u32[]{:S(2)}, u32[]{:S(2)}) %collective-permute-start.28) | collective-permute-done | bytes 191776 | tf_op jit(solution)/shard_map/ppermute | solution.py:103
  (186 shorter events, 32.4 us)
Async XLA Ops:
  0.6 26.2 %copy-start = (f32[64,512]{1,0:T(8,128)S(1)}, f32[64,512]{1,0:T(8,128)}, u32[]{:S(2)}) copy-start(f32[64,512]{1,0:T(8,128)} %param.17) | copy-start | bytes 393220
  1.9 4.5 %copy-start.14 = (f32[64,128,4]{1,2,0:T(4,128)}, f32[64,128,4]{1,2,0:T(4,128)S(1)}, u32[]{:S(2)}) copy-start(f32[64,128,4]{1,2,0:T(4,128)S(1)} %copy.28) | copy-start | bytes 393220
  1.9 19.1 %copy-start.10 = (f32[3,64,64]{2,1,0:T(8,128)S(1)}, f32[3,64,64]{2,1,0:T(8,128)}, u32[]{:S(2)}) copy-start(f32[3,64,64]{2,1,0:T(8,128)} %param.16) | copy-start | bytes 147460
  1.9 19.4 %copy-start.23 = (bf16[1,128]{1,0:T(2,128)(2,1)S(1)}, bf16[1,128]{1,0:T(2,128)(2,1)}, u32[]{:S(2)}) copy-start(bf16[1,128]{1,0:T(2,128)(2,1)} %param.11) | copy-start | bytes 772
  1.9 25.5 %copy-start.21 = (f32[512]{0:T(512)S(1)}, f32[512]{0:T(512)}, u32[]{:S(2)}) copy-start(f32[512]{0:T(512)} %param.18) | copy-start | bytes 6148
  1.9 25.6 %copy-start.3 = (bf16[4,512,512]{2,1,0:T(8,128)(2,1)S(1)}, bf16[4,512,512]{2,1,0:T(8,128)(2,1)}, u32[]{:S(2)}) copy-start(bf16[4,512,512]{2,1,0:T(8,128)(2,1)} %param.19) | copy-start | bytes 6291460
  6.4 20.9 %copy-start.12 = (f32[64,128]{1,0:T(8,128)}, f32[64,128]{1,0:T(8,128)S(1)}, u32[]{:S(2)}) copy-start(f32[64,128]{1,0:T(8,128)S(1)} %get-tuple-element.36) | copy-start | bytes 98308
  6.4 24.5 %copy-start.8 = (bf16[1,128,512]{2,1,0:T(8,128)(2,1)S(1)}, bf16[1,128,512]{2,1,0:T(8,128)(2,1)}, u32[]{:S(2)}) copy-start(bf16[1,128,512]{2,1,0:T(8,128)(2,1)} %param.13) | copy-start | bytes 393220
  6.4 20.9 %copy-start.6 = (f32[1,64,128]{2,1,0:T(8,128)}, f32[1,64,128]{2,1,0:T(8,128)S(1)}, u32[]{:S(2)}) copy-start(f32[1,64,128]{2,1,0:T(8,128)S(1)} %multiply_bitcast_fusion) | copy-start | bytes 98308
  6.5 14.9 %collective-permute-start.1 = (f32[1,64,1]{2,1,0:T(8,128)S(1)}, f32[1,64,1]{2,1,0:T(8,128)S(1)}, u32[]{:S(2)}, u32[]{:S(2)}) collective-permute-start(f32[1,64,1]{2,1,0:T(8,128)S(1)} %get-tuple-element.31), channel_id=1, source_target_pairs={{1,0},{2,1},{3,2},{4,3},{5,4},{6,5},{7,6},{8,7},{9,8},{10,9},{11,1... | collective-permute-start | bytes 776 | tf_op jit(solution)/shard_map/ppermute | solution.py:24
  17.7 8.8 %collective-permute-start = (f32[1,64,1]{2,1,0:T(8,128)S(1)}, f32[1,64,1]{2,1,0:T(8,128)S(1)}, u32[]{:S(2)}, u32[]{:S(2)}) collective-permute-start(f32[1,64,1]{2,1,0:T(8,128)S(1)} %get-tuple-element.30), channel_id=1, source_target_pairs={{0,1},{1,2},{2,3},{3,4},{4,5},{5,6},{6,7},{7,8},{8,9},{9,10},{10,1... | collective-permute-start | bytes 776 | tf_op jit(solution)/shard_map/ppermute | solution.py:22
  21.4 9.5 %copy-start.17 = (f32[1,64,1]{2,1,0:T(8,128)}, f32[1,64,1]{2,1,0:T(8,128)S(1)}, u32[]{:S(2)}) copy-start(f32[1,64,1]{2,1,0:T(8,128)S(1)} %collective-permute-done.1) | copy-start | bytes 772
  26.5 4.4 %copy-start.19 = (f32[1,64,1]{2,1,0:T(8,128)}, f32[1,64,1]{2,1,0:T(8,128)S(1)}, u32[]{:S(2)}) copy-start(f32[1,64,1]{2,1,0:T(8,128)S(1)} %collective-permute-done) | copy-start | bytes 772
  28.8 30.1 %collective-permute-start.2 = (bf16[1,128,1025]{2,1,0:T(8,128)(2,1)}, bf16[1,128,1025]{2,1,0:T(8,128)(2,1)}, u32[]{:S(2)}, u32[]{:S(2)}) collective-permute-start(bf16[1,128,1025]{2,1,0:T(8,128)(2,1)} %get-tuple-element.28), channel_id=1, source_target_pairs={{0,15},{1,0},{2,1},{3,2},{4,3},{5,4},{6,5},{7,6},{8,7},{9,8},{10,9... | collective-permute-start | bytes 787208 | tf_op jit(solution)/shard_map/ppermute | solution.py:34
  31.4 31.1 %collective-permute-start.3 = (bf16[1,128,1025]{2,1,0:T(8,128)(2,1)}, bf16[1,128,1025]{2,1,0:T(8,128)(2,1)}, u32[]{:S(2)}, u32[]{:S(2)}) collective-permute-start(bf16[1,128,1025]{2,1,0:T(8,128)(2,1)} %get-tuple-element.28), channel_id=1, source_target_pairs={{0,1},{1,2},{2,3},{3,4},{4,5},{5,6},{6,7},{7,8},{8,9},{9,10},{10,1... | collective-permute-start | bytes 787208 | tf_op jit(solution)/shard_map/ppermute | solution.py:34
  36.0 49.8 %collective-permute-start.4 = (bf16[1,128,1025]{2,1,0:T(8,128)(2,1)}, bf16[1,128,1025]{2,1,0:T(8,128)(2,1)}, u32[]{:S(2)}, u32[]{:S(2)}) collective-permute-start(bf16[1,128,1025]{2,1,0:T(8,128)(2,1)} %get-tuple-element.28), channel_id=1, source_target_pairs={{0,14},{1,15},{2,0},{3,1},{4,2},{5,3},{6,4},{7,5},{8,6},{9,7},{10,... | collective-permute-start | bytes 787208 | tf_op jit(solution)/shard_map/ppermute | solution.py:34
  38.0 51.4 %collective-permute-start.5 = (bf16[1,128,1025]{2,1,0:T(8,128)(2,1)}, bf16[1,128,1025]{2,1,0:T(8,128)(2,1)}, u32[]{:S(2)}, u32[]{:S(2)}) collective-permute-start(bf16[1,128,1025]{2,1,0:T(8,128)(2,1)} %get-tuple-element.28), channel_id=1, source_target_pairs={{0,2},{1,3},{2,4},{3,5},{4,6},{5,7},{6,8},{7,9},{8,10},{9,11},{10,... | collective-permute-start | bytes 787208 | tf_op jit(solution)/shard_map/ppermute | solution.py:34
  45.8 45.3 %collective-permute-start.6 = (bf16[1,128,1025]{2,1,0:T(8,128)(2,1)}, bf16[1,128,1025]{2,1,0:T(8,128)(2,1)}, u32[]{:S(2)}, u32[]{:S(2)}) collective-permute-start(bf16[1,128,1025]{2,1,0:T(8,128)(2,1)} %get-tuple-element.28), channel_id=1, source_target_pairs={{0,13},{1,14},{2,15},{3,0},{4,1},{5,2},{6,3},{7,4},{8,5},{9,6},{10... | collective-permute-start | bytes 787208 | tf_op jit(solution)/shard_map/ppermute | solution.py:34
  58.9 33.9 %collective-permute-start.7 = (bf16[1,128,1025]{2,1,0:T(8,128)(2,1)}, bf16[1,128,1025]{2,1,0:T(8,128)(2,1)S(1)}, u32[]{:S(2)}, u32[]{:S(2)}) collective-permute-start(bf16[1,128,1025]{2,1,0:T(8,128)(2,1)} %get-tuple-element.28), channel_id=1, source_target_pairs={{0,3},{1,4},{2,5},{3,6},{4,7},{5,8},{6,9},{7,10},{8,11},{9,12},{10... | collective-permute-start | bytes 787208 | tf_op jit(solution)/shard_map/ppermute | solution.py:34
  62.6 31.0 %collective-permute-start.8 = (bf16[1,128,1025]{2,1,0:T(8,128)(2,1)}, bf16[1,128,1025]{2,1,0:T(8,128)(2,1)S(1)}, u32[]{:S(2)}, u32[]{:S(2)}) collective-permute-start(bf16[1,128,1025]{2,1,0:T(8,128)(2,1)} %get-tuple-element.28), channel_id=1, source_target_pairs={{0,12},{1,13},{2,14},{3,15},{4,0},{5,1},{6,2},{7,3},{8,4},{9,5},{1... | collective-permute-start | bytes 787208 | tf_op jit(solution)/shard_map/ppermute | solution.py:34
  85.8 8.8 %collective-permute-start.9 = (bf16[1,128,1025]{2,1,0:T(8,128)(2,1)}, bf16[1,128,1025]{2,1,0:T(8,128)(2,1)S(1)}, u32[]{:S(2)}, u32[]{:S(2)}) collective-permute-start(bf16[1,128,1025]{2,1,0:T(8,128)(2,1)} %get-tuple-element.28), channel_id=1, source_target_pairs={{0,4},{1,5},{2,6},{3,7},{4,8},{5,9},{6,10},{7,11},{8,12},{9,13},{1... | collective-permute-start | bytes 787208 | tf_op jit(solution)/shard_map/ppermute | solution.py:34
  108.7 22.4 %collective-permute-start.17 = (bf16[1,128,16,64]{1,3,2,0:T(8,128)(2,1)S(1)}, bf16[1,128,16,64]{1,3,2,0:T(8,128)(2,1)S(1)}, u32[]{:S(2)}, u32[]{:S(2)}) collective-permute-start(bf16[1,128,16,64]{1,3,2,0:T(8,128)(2,1)S(1)} %pad_maximum_fusion.13), channel_id=1, source_target_pairs={{0,12},{1,13},{2,14},{3,15},{4,0},{5,1},{6,2},{7,3},{8,4},{9,5},{1... | collective-permute-start | bytes 786440 | tf_op jit(solution)/shard_map/ppermute | solution.py:34
  112.6 22.6 %collective-permute-start.16 = (bf16[1,128,16,64]{1,3,2,0:T(8,128)(2,1)S(1)}, bf16[1,128,16,64]{1,3,2,0:T(8,128)(2,1)S(1)}, u32[]{:S(2)}, u32[]{:S(2)}) collective-permute-start(bf16[1,128,16,64]{1,3,2,0:T(8,128)(2,1)S(1)} %pad_maximum_fusion.12), channel_id=1, source_target_pairs={{0,4},{1,5},{2,6},{3,7},{4,8},{5,9},{6,10},{7,11},{8,12},{9,13},{1... | collective-permute-start | bytes 786440 | tf_op jit(solution)/shard_map/ppermute | solution.py:34
  116.1 23.8 %collective-permute-start.15 = (bf16[1,128,16,64]{1,3,2,0:T(8,128)(2,1)S(1)}, bf16[1,128,16,64]{1,3,2,0:T(8,128)(2,1)S(1)}, u32[]{:S(2)}, u32[]{:S(2)}) collective-permute-start(bf16[1,128,16,64]{1,3,2,0:T(8,128)(2,1)S(1)} %pad_maximum_fusion.11), channel_id=1, source_target_pairs={{0,13},{1,14},{2,15},{3,0},{4,1},{5,2},{6,3},{7,4},{8,5},{9,6},{10... | collective-permute-start | bytes 786440 | tf_op jit(solution)/shard_map/ppermute | solution.py:34
  120.6 41.2 %collective-permute-start.14 = (bf16[1,128,16,64]{1,3,2,0:T(8,128)(2,1)S(1)}, bf16[1,128,16,64]{1,3,2,0:T(8,128)(2,1)S(1)}, u32[]{:S(2)}, u32[]{:S(2)}) collective-permute-start(bf16[1,128,16,64]{1,3,2,0:T(8,128)(2,1)S(1)} %pad_maximum_fusion.10), channel_id=1, source_target_pairs={{0,3},{1,4},{2,5},{3,6},{4,7},{5,8},{6,9},{7,10},{8,11},{9,12},{10... | collective-permute-start | bytes 786440 | tf_op jit(solution)/shard_map/ppermute | solution.py:34
  124.1 37.7 %collective-permute-start.13 = (bf16[1,128,16,64]{1,3,2,0:T(8,128)(2,1)S(1)}, bf16[1,128,16,64]{1,3,2,0:T(8,128)(2,1)S(1)}, u32[]{:S(2)}, u32[]{:S(2)}) collective-permute-start(bf16[1,128,16,64]{1,3,2,0:T(8,128)(2,1)S(1)} %pad_maximum_fusion.9), channel_id=1, source_target_pairs={{0,14},{1,15},{2,0},{3,1},{4,2},{5,3},{6,4},{7,5},{8,6},{9,7},{10,... | collective-permute-start | bytes 786440 | tf_op jit(solution)/shard_map/ppermute | solution.py:34
  130.1 13.8 %copy-start.4 = (bf16[4,512,512]{2,1,0:T(8,128)(2,1)S(1)}, bf16[4,512,512]{2,1,0:T(8,128)(2,1)}, u32[]{:S(2)}) copy-start(bf16[4,512,512]{2,1,0:T(8,128)(2,1)} %param.19) | copy-start | bytes 6291460
  131.1 30.8 %collective-permute-start.12 = (bf16[1,128,16,64]{1,3,2,0:T(8,128)(2,1)S(1)}, bf16[1,128,16,64]{1,3,2,0:T(8,128)(2,1)S(1)}, u32[]{:S(2)}, u32[]{:S(2)}) collective-permute-start(bf16[1,128,16,64]{1,3,2,0:T(8,128)(2,1)S(1)} %pad_maximum_fusion.8), channel_id=1, source_target_pairs={{0,2},{1,3},{2,4},{3,5},{4,6},{5,7},{6,8},{7,9},{8,10},{9,11},{10,... | collective-permute-start | bytes 786440 | tf_op jit(solution)/shard_map/ppermute | solution.py:34
  135.3 35.8 %collective-permute-start.11 = (bf16[1,128,16,64]{1,3,2,0:T(8,128)(2,1)S(1)}, bf16[1,128,16,64]{1,3,2,0:T(8,128)(2,1)S(1)}, u32[]{:S(2)}, u32[]{:S(2)}) collective-permute-start(bf16[1,128,16,64]{1,3,2,0:T(8,128)(2,1)S(1)} %pad_maximum_fusion.7), channel_id=1, source_target_pairs={{0,15},{1,0},{2,1},{3,2},{4,3},{5,4},{6,5},{7,6},{8,7},{9,8},{10,9... | collective-permute-start | bytes 786440 | tf_op jit(solution)/shard_map/ppermute | solution.py:34
  139.8 31.3 %collective-permute-start.10 = (bf16[1,128,16,64]{1,3,2,0:T(8,128)(2,1)S(1)}, bf16[1,128,16,64]{1,3,2,0:T(8,128)(2,1)S(1)}, u32[]{:S(2)}, u32[]{:S(2)}) collective-permute-start(bf16[1,128,16,64]{1,3,2,0:T(8,128)(2,1)S(1)} %pad_maximum_fusion.6), channel_id=1, source_target_pairs={{0,1},{1,2},{2,3},{3,4},{4,5},{5,6},{6,7},{7,8},{8,9},{9,10},{10,1... | collective-permute-start | bytes 786440 | tf_op jit(solution)/shard_map/ppermute | solution.py:34
  172.9 14.2 %copy-start.13 = (f32[64,128]{1,0:T(8,128)S(1)}, f32[64,128]{1,0:T(8,128)}, u32[]{:S(2)}) copy-start(f32[64,128]{1,0:T(8,128)} %copy-done.12) | copy-start | bytes 98308
  172.9 14.4 %copy-start.7 = (f32[1,64,128]{2,1,0:T(8,128)S(1)}, f32[1,64,128]{2,1,0:T(8,128)}, u32[]{:S(2)}) copy-start(f32[1,64,128]{2,1,0:T(8,128)} %copy-done.6) | copy-start | bytes 98308
  172.9 14.4 %copy-start.18 = (f32[1,64,1]{2,1,0:T(8,128)S(1)}, f32[1,64,1]{2,1,0:T(8,128)}, u32[]{:S(2)}) copy-start(f32[1,64,1]{2,1,0:T(8,128)} %copy-done.17) | copy-start | bytes 772
  172.9 14.7 %copy-start.20 = (f32[1,64,1]{2,1,0:T(8,128)S(1)}, f32[1,64,1]{2,1,0:T(8,128)}, u32[]{:S(2)}) copy-start(f32[1,64,1]{2,1,0:T(8,128)} %copy-done.19) | copy-start | bytes 772
  178.3 25.0 %collective-permute-start.19 = (bf16[1,64,1]{2,1,0:T(8,128)(2,1)}, bf16[1,64,1]{2,1,0:T(8,128)(2,1)}, u32[]{:S(2)}, u32[]{:S(2)}) collective-permute-start(bf16[1,64,1]{2,1,0:T(8,128)(2,1)} %get-tuple-element.33), channel_id=1, source_target_pairs={{0,1},{1,2},{2,3},{3,4},{4,5},{5,6},{6,7},{7,8},{8,9},{9,10},{10,1... | collective-permute-start | bytes 392 | tf_op jit(solution)/shard_map/ppermute | solution.py:22
  182.9 23.4 %collective-permute-start.18 = (bf16[1,64,1]{2,1,0:T(8,128)(2,1)}, bf16[1,64,1]{2,1,0:T(8,128)(2,1)}, u32[]{:S(2)}, u32[]{:S(2)}) collective-permute-start(bf16[1,64,1]{2,1,0:T(8,128)(2,1)} %get-tuple-element.32), channel_id=1, source_target_pairs={{1,0},{2,1},{3,2},{4,3},{5,4},{6,5},{7,6},{8,7},{9,8},{10,9},{11,1... | collective-permute-start | bytes 392 | tf_op jit(solution)/shard_map/ppermute | solution.py:24
  203.1 6.6 %copy-start.2 = (f32[512,4,4,128]{3,1,2,0:T(4,128)}, f32[512,4,4,128]{3,1,2,0:T(4,128)S(1)}, u32[]{:S(2)}) copy-start(f32[512,4,4,128]{3,1,2,0:T(4,128)S(1)} %copy.45) | copy-start | bytes 12582916
  203.1 1.0 copy-start.11
  203.1 3.2 copy-start.16
  203.1 4.1 %copy-start.5 = (f32[64,64,128]{2,0,1:T(8,128)S(1)}, f32[64,64,128]{2,0,1:T(8,128)}, u32[]{:S(2)}) copy-start(f32[64,64,128]{2,0,1:T(8,128)} %get-tuple-element.37) | copy-start | bytes 6291460
  203.1 4.1 %copy-start.15 = (f32[64,128,4]{1,2,0:T(4,128)S(1)}, f32[64,128,4]{1,2,0:T(4,128)}, u32[]{:S(2)}) copy-start(f32[64,128,4]{1,2,0:T(4,128)} %copy-done.14) | copy-start | bytes 393220
  203.1 4.1 %copy-start.24 = (f32[64]{0:T(128)S(1)}, f32[64]{0:T(128)}, u32[]{:S(2)}) copy-start(f32[64]{0:T(128)} %param.15) | copy-start | bytes 772
  207.3 3.5 copy-start.9
  207.3 3.5 copy-start.22
  225.3 6.6 %collective-permute-start.20 = (f32[570176]{0:T(1024)}, f32[570176]{0:T(1024)}, u32[]{:S(2)}, u32[]{:S(2)}) collective-permute-start(f32[570176]{0:T(1024)} %concatenate.165), channel_id=1, source_target_pairs={{0,16},{16,0},{32,48},{48,32},{64,80},{80,64},{96,112},{112,96},{1... | collective-permute-start | bytes 6842120 | tf_op jit(solution)/shard_map/ppermute | solution.py:103
  236.6 31.3 %collective-permute-start.21 = (f32[308032]{0:T(1024)}, f32[308032]{0:T(1024)}, u32[]{:S(2)}, u32[]{:S(2)}) collective-permute-start(f32[308032]{0:T(1024)} %pad_maximum_fusion.1), channel_id=1, source_target_pairs={{0,256},{16,272},{32,288},{48,304},{64,320},{80,336},{96,352},{112... | collective-permute-start | bytes 3696392 | tf_op jit(solution)/shard_map/ppermute | solution.py:103
  270.3 19.0 %collective-permute-start.22 = (f32[176960]{0:T(1024)S(1)}, f32[176960]{0:T(1024)S(1)}, u32[]{:S(2)}, u32[]{:S(2)}) collective-permute-start(f32[176960]{0:T(1024)S(1)} %pad_maximum_fusion.2), channel_id=1, source_target_pairs={{0,32},{16,48},{32,0},{48,16},{64,96},{80,112},{96,64},{112,80},{1... | collective-permute-start | bytes 2123528 | tf_op jit(solution)/shard_map/ppermute | solution.py:103
  289.5 12.4 %collective-permute-start.23 = (f32[111424]{0:T(1024)S(1)}, f32[111424]{0:T(1024)S(1)}, u32[]{:S(2)}, u32[]{:S(2)}) collective-permute-start(f32[111424]{0:T(1024)S(1)} %pad_maximum_fusion.3), channel_id=1, source_target_pairs={{0,4},{1,5},{2,6},{3,7},{4,0},{5,1},{6,2},{7,3},{8,12},{9,13},{10,... | collective-permute-start | bytes 1337096 | tf_op jit(solution)/shard_map/ppermute | solution.py:103
  302.0 16.4 %collective-permute-start.24 = (f32[78656]{0:T(1024)S(1)}, f32[78656]{0:T(1024)S(1)}, u32[]{:S(2)}, u32[]{:S(2)}) collective-permute-start(f32[78656]{0:T(1024)S(1)} %pad_maximum_fusion.4), channel_id=1, source_target_pairs={{0,64},{16,80},{32,96},{48,112},{64,0},{80,16},{96,32},{112,48},{1... | collective-permute-start | bytes 943880 | tf_op jit(solution)/shard_map/ppermute | solution.py:103
  318.5 10.3 %collective-permute-start.25 = (f32[62272]{0:T(1024)S(1)}, f32[62272]{0:T(1024)S(1)}, u32[]{:S(2)}, u32[]{:S(2)}) collective-permute-start(f32[62272]{0:T(1024)S(1)} %pad_maximum_fusion.14), channel_id=1, source_target_pairs={{0,8},{1,9},{2,10},{3,11},{4,12},{5,13},{6,14},{7,15},{8,0},{9,1},... | collective-permute-start | bytes 747272 | tf_op jit(solution)/shard_map/ppermute | solution.py:103
  328.8 46.9 %copy-start.1 = (f32[64,512]{1,0:T(8,128)S(1)}, f32[64,512]{1,0:T(8,128)}, u32[]{:S(2)}) copy-start(f32[64,512]{1,0:T(8,128)} %param.17) | copy-start | bytes 393220
  328.9 16.3 %collective-permute-start.26 = (f32[54080]{0:T(1024)S(1)}, f32[54080]{0:T(1024)S(1)}, u32[]{:S(2)}, u32[]{:S(2)}) collective-permute-start(f32[54080]{0:T(1024)S(1)} %pad_maximum_fusion.15), channel_id=1, source_target_pairs={{0,128},{16,144},{32,160},{48,176},{64,192},{80,208},{96,224},{112... | collective-permute-start | bytes 648968 | tf_op jit(solution)/shard_map/ppermute | solution.py:103
  345.2 12.3 %collective-permute-start.27 = (f32[49984]{0:T(1024)S(1)}, f32[49984]{0:T(1024)S(1)}, u32[]{:S(2)}, u32[]{:S(2)}) collective-permute-start(f32[49984]{0:T(1024)S(1)} %pad_maximum_fusion.16), channel_id=1, source_target_pairs={{0,1},{1,0},{2,3},{3,2},{4,5},{5,4},{6,7},{7,6},{8,9},{9,8},{10,11... | collective-permute-start | bytes 599816 | tf_op jit(solution)/shard_map/ppermute | solution.py:103
  357.6 14.1 %collective-permute-start.28 = (f32[47936]{0:T(1024)S(1)}, f32[47936]{0:T(1024)S(1)}, u32[]{:S(2)}, u32[]{:S(2)}) collective-permute-start(f32[47936]{0:T(1024)S(1)} %pad_maximum_fusion.17), channel_id=1, source_target_pairs={{0,2},{1,3},{2,0},{3,1},{4,6},{5,7},{6,4},{7,5},{8,10},{9,11},{10,... | collective-permute-start | bytes 575240 | tf_op jit(solution)/shard_map/ppermute | solution.py:103

commit v4 on v3

--- a/solution.py
+++ b/solution.py
@@ -1,6 +1,10 @@
+import functools
+
 import jax
 import jax.numpy as jnp
 from jax import lax
+from jax.experimental import pallas as pl
+from jax.experimental.pallas import tpu as pltpu
 from jax.sharding import PartitionSpec as P
 
 HEADS = 8
@@ -92,18 +96,94 @@
     cells = flat.reshape((2,) * total_bits + (chunk // 512, 512))
     cells = cells.transpose([dim_of[o] for o in order] + [total_bits, total_bits + 1])
     current = cells.reshape(-1)
+    return butterfly_kernel(current, small, order, chunk)
+
+
+LANES = 256
+
+
+def butterfly_body(order, steps_rows, small_rows, big_ref, small_ref, out_ref, small_out_ref,
+                   acc, small_acc, recv, small_recv, send_sems, recv_sems, small_send_sems,
+                   small_recv_sems):
+    me = {"sims": lax.axis_index("sims"), "sites": lax.axis_index("sites")}
+    partners = []
     for axis, bit in order:
-        count = lax.axis_size(axis)
-        half = current.shape[0] // 2
-        mine = (lax.axis_index(axis) >> bit) & 1
-        keep = lax.dynamic_slice_in_dim(current, mine * half, half)
-        send = lax.dynamic_slice_in_dim(current, (1 - mine) * half, half)
-        outgoing = jnp.concatenate([send, small])
-        pairs = [(i, i ^ (1 << bit)) for i in range(count)]
-        incoming = lax.ppermute(outgoing, axis, pairs)
-        current = keep + incoming[:half]
-        small = small + incoming[half:]
-    return current, small
+        step = 1 << bit
+        mine = (me[axis] // step) % 2
+        other = dict(me)
+        other[axis] = me[axis] + (1 - 2 * mine) * step
+        partners.append(((other["sims"], other["sites"]), mine))
+    barrier = pltpu.get_barrier_semaphore()
+    for device, _ in partners:
+        pl.semaphore_signal(barrier, inc=1, device_id=device, device_id_type=pl.DeviceIdType.MESH)
+    pl.semaphore_wait(barrier, len(partners))
+    acc[...] = big_ref[...]
+    small_acc[...] = small_ref[...]
+    base = 0
+    lower = 0
+    for k, ((device, mine), rows) in enumerate(zip(partners, steps_rows)):
+        keep = pl.multiple_of(base + mine * rows, 8)
+        away = pl.multiple_of(base + (1 - mine) * rows, 8)
+        big_copy = pltpu.make_async_remote_copy(
+            src_ref=acc.at[pl.ds(away, rows)],
+            dst_ref=recv.at[pl.ds(lower, rows)],
+            send_sem=send_sems.at[k],
+            recv_sem=recv_sems.at[k],
+            device_id=device,
+            device_id_type=pl.DeviceIdType.MESH,
+        )
+        small_copy = pltpu.make_async_remote_copy(
+            src_ref=small_acc,
+            dst_ref=small_recv.at[k],
+            send_sem=small_send_sems.at[k],
+            recv_sem=small_recv_sems.at[k],
+            device_id=device,
+            device_id_type=pl.DeviceIdType.MESH,
+        )
+        big_copy.start()
+        small_copy.start()
+        big_copy.wait_send()
+        small_copy.wait_send()
+        big_copy.wait_recv()
+        small_copy.wait_recv()
+        acc[pl.ds(keep, rows)] = acc[pl.ds(keep, rows)] + recv[pl.ds(lower, rows)]
+        small_acc[...] = small_acc[...] + small_recv[k]
+        base = keep
+        lower += rows
+    out_ref[...] = acc[pl.ds(pl.multiple_of(base, 8), steps_rows[-1])]
+    small_out_ref[...] = small_acc[...]
+
+
+def butterfly_kernel(current, small, order, chunk):
+    size = small.shape[0]
+    small_rows = -(-size // (LANES * 8)) * 8
+    small_grid = jnp.pad(small, (0, small_rows * LANES - size)).reshape(small_rows, LANES)
+    big_rows = current.shape[0] // LANES
+    steps_rows = [big_rows >> (k + 1) for k in range(len(order))]
+    f32 = jnp.float32
+    out, small_out = pl.pallas_call(
+        functools.partial(butterfly_body, order, steps_rows, small_rows),
+        out_shape=(
+            jax.ShapeDtypeStruct((steps_rows[-1], LANES), f32),
+            jax.ShapeDtypeStruct((small_rows, LANES), f32),
+        ),
+        in_specs=[pl.BlockSpec(memory_space=pltpu.VMEM)] * 2,
+        out_specs=(pl.BlockSpec(memory_space=pltpu.VMEM),) * 2,
+        scratch_shapes=[
+            pltpu.VMEM((big_rows, LANES), f32),
+            pltpu.VMEM((small_rows, LANES), f32),
+            pltpu.VMEM((sum(steps_rows), LANES), f32),
+            pltpu.VMEM((len(order), small_rows, LANES), f32),
+            pltpu.SemaphoreType.DMA((len(order),)),
+            pltpu.SemaphoreType.DMA((len(order),)),
+            pltpu.SemaphoreType.DMA((len(order),)),
+            pltpu.SemaphoreType.DMA((len(order),)),
+        ],
+        compiler_params=pltpu.CompilerParams(
+            collective_id=0, has_side_effects=True, vmem_limit_bytes=48 * 1024 * 1024
+        ),
+    )(current.reshape(big_rows, LANES), small_grid)
+    return out.reshape(chunk), small_out.reshape(-1)[:size]
 
 def per_device(
     genotypes,

time: 379 us -> 350 us (0.923)
  Pallas kernels: 0 us -> 133 us
  waiting for transfers between devices: 148 us -> 32 us
  starting transfers between devices: 132 us -> 102 us
  other arithmetic: 19.8 us -> 11.9 us
  local copies, waits for them, and re-layouts: 48.6 us -> 42.6 us
  matrix products: 24.7 us -> 20.7 us
    pallas_call x0 -> x1, Pallas kernels: none -> 133 us  [butterfly_kernel(): pl.pallas_call(functools.partial(butterfly_body, order, steps_rows, small...]
    ppermute x9 -> x0, waiting for transfers between devices: 105 us -> none  [butterfly_sum(): incoming = lax.ppermute(outgoing, axis, pairs)]
    ppermute x9 -> x0, starting transfers between devices: 33 us -> none  [butterfly_sum(): incoming = lax.ppermute(outgoing, axis, pairs)]
    concatenate x1 -> x0, local copies, waits for them, and re-layouts: 14.6 us -> none  [butterfly_sum(): outgoing = jnp.concatenate([send, small])]
    ppermute x16, waiting for transfers between devices: 37.7 us -> 27.5 us  [from_behind(): return lax.ppermute(value, axis, pairs)]
    add x18 -> x0, other arithmetic: 6.57 us -> none  [the longest x9 4.5 us: butterfly_sum(): current = keep + incoming[:half]]
    another operation x0 -> x1, local copies, waits for them, and re-layouts: none -> 5.59 us  [butterfly_kernel(): current.reshape(big_rows, LANES)]
    unnamed x59 -> x50, local copies, waits for them, and re-layouts: 12.9 us -> 14.6 us
  transfers between devices with their start and end apart: 29 -> 20, of which waited for: 14 -> 5; matrix products, arithmetic and copies ran while one was open for 9% -> 10% of each run, Pallas kernels for 0% -> 0%
where the time goes in v4:
time: 350 us; the launch traced here: 344 us
  Pallas kernels  133 us (38%)
  starting transfers between devices  102 us (29%)
  local copies, waits for them, and re-layouts  42.6 us (12%)
  waiting for transfers between devices  32 us (9%)
  matrix products  20.7 us (6%)
  other arithmetic  11.9 us (3%)
    pallas_call x1, Pallas kernels, butterfly_kernel(): pl.pallas_call(functools.partial(butterfly_body, order, steps_rows, small...  133 us
    ppermute x16, starting transfers between devices, from_behind(): return lax.ppermute(value, axis, pairs)  79.6 us
    ppermute x16, waiting for transfers between devices, from_behind(): return lax.ppermute(value, axis, pairs)  27.5 us
    ppermute x2, starting transfers between devices, extended(): lax.ppermute(head, axis, [((i + 1) % count, i) for i in range(count)])  16.2 us
    unnamed x50, local copies, waits for them, and re-layouts  14.6 us
    another operation x2, local copies, waits for them, and re-layouts, butterfly_sum(): cells = flat.reshape((2,) * total_bits + (chunk // 512, 512))  10.8 us
  transfers between devices with their start and end apart: 20, of which 5 were waited for; matrix products, arithmetic and copies ran while one was open for 10% of the time, Pallas kernels for 0%

profile of v4, /device:TPU:6, one launch (start us, length us, event | category | flops | bytes accessed | tf_op | source)
XLA Modules:
  0.0 343.9 jit_solution(10431913279709851414)
XLA Ops:
  0.6 1.0 convert_element_type.179
  1.9 0.6 copy-done.10
  2.5 4.4 %fusion.16 = (f32[64,128]{1,0:T(8,128)S(1)}, f32[64,64,128]{2,0,1:T(8,128)}) fusion(f32[64]{0:T(128)} %param.15, f32[64,128,4]{1,2,0:T(4,128)S(1)} %copy.29, f32[4,64]{1,0:T(4,128)} %param.14), kind=kOutput, calls=%fused_computation.26 | convolution fusion | flops 28303360 | bytes 2262272 | tf_op jit(solution)/shard_map/shtk,kc->shct/dot_general | solution.py:212
  7.1 11.2 %collective-permute-start.1 = (f32[1,64,1]{2,1,0:T(8,128)S(1)}, f32[1,64,1]{2,1,0:T(8,128)S(1)}, u32[]{:S(2)}, u32[]{:S(2)}) collective-permute-start(f32[1,64,1]{2,1,0:T(8,128)S(1)} %get-tuple-element.35), channel_id=1, source_target_pairs={{1,0},{2,1},{3,2},{4,3},{5,4},{6,5},{7,6},{8,7},{9,8},{10,9},{11,1... | collective-permute-start | bytes 776 | tf_op jit(solution)/shard_map/ppermute | solution.py:28
  18.3 1.9 collective-permute-start
  22.6 4.5 %collective-permute-done = f32[1,64,1]{2,1,0:T(8,128)S(1)} collective-permute-done((f32[1,64,1]{2,1,0:T(8,128)S(1)}, f32[1,64,1]{2,1,0:T(8,128)S(1)}, u32[]{:S(2)}, u32[]{:S(2)}) %collective-permute-start) | collective-permute-done | bytes 288 | tf_op jit(solution)/shard_map/ppermute | solution.py:26
  28.5 0.9 pad_maximum_fusion.1
  29.4 2.4 collective-permute-start.2
  32.2 4.3 %collective-permute-start.3 = (bf16[1,128,1025]{2,1,0:T(8,128)(2,1)}, bf16[1,128,1025]{2,1,0:T(8,128)(2,1)}, u32[]{:S(2)}, u32[]{:S(2)}) collective-permute-start(bf16[1,128,1025]{2,1,0:T(8,128)(2,1)} %get-tuple-element.32), channel_id=1, source_target_pairs={{0,1},{1,2},{2,3},{3,4},{4,5},{5,6},{6,7},{7,8},{8,9},{9,10},{10,1... | collective-permute-start | bytes 787208 | tf_op jit(solution)/shard_map/ppermute | solution.py:38
  36.6 1.9 collective-permute-start.4
  38.5 7.8 %collective-permute-start.5 = (bf16[1,128,1025]{2,1,0:T(8,128)(2,1)}, bf16[1,128,1025]{2,1,0:T(8,128)(2,1)}, u32[]{:S(2)}, u32[]{:S(2)}) collective-permute-start(bf16[1,128,1025]{2,1,0:T(8,128)(2,1)} %get-tuple-element.32), channel_id=1, source_target_pairs={{0,2},{1,3},{2,4},{3,5},{4,6},{5,7},{6,8},{7,9},{8,10},{9,11},{10,... | collective-permute-start | bytes 787208 | tf_op jit(solution)/shard_map/ppermute | solution.py:38
  46.3 1.9 collective-permute-start.6
  48.6 10.8 %collective-permute-done.2 = bf16[1,128,1025]{2,1,0:T(8,128)(2,1)} collective-permute-done((bf16[1,128,1025]{2,1,0:T(8,128)(2,1)}, bf16[1,128,1025]{2,1,0:T(8,128)(2,1)}, u32[]{:S(2)}, u32[]{:S(2)}) %collective-permute-start.2) | collective-permute-done | bytes 262432 | tf_op jit(solution)/shard_map/ppermute | solution.py:38
  59.4 1.9 collective-permute-start.7
  61.4 1.7 constant_dynamic-update-slice_fusion.7
  63.1 21.2 %collective-permute-start.8 = (bf16[1,128,1025]{2,1,0:T(8,128)(2,1)}, bf16[1,128,1025]{2,1,0:T(8,128)(2,1)S(1)}, u32[]{:S(2)}, u32[]{:S(2)}) collective-permute-start(bf16[1,128,1025]{2,1,0:T(8,128)(2,1)} %get-tuple-element.32), channel_id=1, source_target_pairs={{0,12},{1,13},{2,14},{3,15},{4,0},{5,1},{6,2},{7,3},{8,4},{9,5},{1... | collective-permute-start | bytes 787208 | tf_op jit(solution)/shard_map/ppermute | solution.py:38
  84.3 1.7 constant_dynamic-update-slice_fusion.6
  86.0 2.1 collective-permute-start.9
  88.1 1.7 constant_dynamic-update-slice_fusion.5
  89.8 1.7 constant_dynamic-update-slice_fusion.4
  91.8 1.7 constant_dynamic-update-slice_fusion.3
  93.5 0.7 constant_dynamic-update-slice_fusion.2
  94.2 0.7 constant_dynamic-update-slice_fusion.1
  94.9 0.7 constant_dynamic-update-slice_fusion
  95.7 2.8 fusion.114
  98.5 1.1 convert_reduce_fusion
  99.6 0.7 copy.31
  100.4 1.7 copy.34
  102.0 0.8 fusion.5
  102.9 1.8 fusion.119
  104.7 0.6 fusion.20
  105.2 1.0 bitcast_convert_fusion
  106.3 1.3 fusion.8
  107.6 1.0 convolution_convert_fusion.5
  110.1 5.2 %collective-permute-start.10 = (bf16[1,128,16,64]{1,3,2,0:T(8,128)(2,1)S(1)}, bf16[1,128,16,64]{1,3,2,0:T(8,128)(2,1)S(1)}, u32[]{:S(2)}, u32[]{:S(2)}) collective-permute-start(bf16[1,128,16,64]{1,3,2,0:T(8,128)(2,1)S(1)} %pad_maximum_fusion.2), channel_id=1, source_target_pairs={{0,1},{1,2},{2,3},{3,4},{4,5},{5,6},{6,7},{7,8},{8,9},{9,10},{10,1... | collective-permute-start | bytes 786440 | tf_op jit(solution)/shard_map/ppermute | solution.py:38
  115.3 3.8 %collective-permute-start.11 = (bf16[1,128,16,64]{1,3,2,0:T(8,128)(2,1)S(1)}, bf16[1,128,16,64]{1,3,2,0:T(8,128)(2,1)S(1)}, u32[]{:S(2)}, u32[]{:S(2)}) collective-permute-start(bf16[1,128,16,64]{1,3,2,0:T(8,128)(2,1)S(1)} %pad_maximum_fusion.3), channel_id=1, source_target_pairs={{0,15},{1,0},{2,1},{3,2},{4,3},{5,4},{6,5},{7,6},{8,7},{9,8},{10,9... | collective-permute-start | bytes 786440 | tf_op jit(solution)/shard_map/ppermute | solution.py:38
  119.2 4.3 %collective-permute-start.12 = (bf16[1,128,16,64]{1,3,2,0:T(8,128)(2,1)S(1)}, bf16[1,128,16,64]{1,3,2,0:T(8,128)(2,1)S(1)}, u32[]{:S(2)}, u32[]{:S(2)}) collective-permute-start(bf16[1,128,16,64]{1,3,2,0:T(8,128)(2,1)S(1)} %pad_maximum_fusion.4), channel_id=1, source_target_pairs={{0,2},{1,3},{2,4},{3,5},{4,6},{5,7},{6,8},{7,9},{8,10},{9,11},{10,... | collective-permute-start | bytes 786440 | tf_op jit(solution)/shard_map/ppermute | solution.py:38
  123.5 6.4 %collective-permute-start.13 = (bf16[1,128,16,64]{1,3,2,0:T(8,128)(2,1)S(1)}, bf16[1,128,16,64]{1,3,2,0:T(8,128)(2,1)S(1)}, u32[]{:S(2)}, u32[]{:S(2)}) collective-permute-start(bf16[1,128,16,64]{1,3,2,0:T(8,128)(2,1)S(1)} %pad_maximum_fusion.5), channel_id=1, source_target_pairs={{0,14},{1,15},{2,0},{3,1},{4,2},{5,3},{6,4},{7,5},{8,6},{9,7},{10,... | collective-permute-start | bytes 786440 | tf_op jit(solution)/shard_map/ppermute | solution.py:38
  129.9 2.1 collective-permute-start.14
  132.4 5.7 %collective-permute-start.15 = (bf16[1,128,16,64]{1,3,2,0:T(8,128)(2,1)S(1)}, bf16[1,128,16,64]{1,3,2,0:T(8,128)(2,1)S(1)}, u32[]{:S(2)}, u32[]{:S(2)}) collective-permute-start(bf16[1,128,16,64]{1,3,2,0:T(8,128)(2,1)S(1)} %pad_maximum_fusion.7), channel_id=1, source_target_pairs={{0,13},{1,14},{2,15},{3,0},{4,1},{5,2},{6,3},{7,4},{8,5},{9,6},{10... | collective-permute-start | bytes 786440 | tf_op jit(solution)/shard_map/ppermute | solution.py:38
  138.2 6.7 %collective-permute-start.16 = (bf16[1,128,16,64]{1,3,2,0:T(8,128)(2,1)S(1)}, bf16[1,128,16,64]{1,3,2,0:T(8,128)(2,1)S(1)}, u32[]{:S(2)}, u32[]{:S(2)}) collective-permute-start(bf16[1,128,16,64]{1,3,2,0:T(8,128)(2,1)S(1)} %pad_maximum_fusion.8), channel_id=1, source_target_pairs={{0,4},{1,5},{2,6},{3,7},{4,8},{5,9},{6,10},{7,11},{8,12},{9,13},{1... | collective-permute-start | bytes 786440 | tf_op jit(solution)/shard_map/ppermute | solution.py:38
  144.8 1.9 collective-permute-start.17
  147.5 1.0 collective-permute-done.13
  148.6 15.4 %collective-permute-done.14 = bf16[1,128,16,64]{1,3,2,0:T(8,128)(2,1)S(1)} collective-permute-done((bf16[1,128,16,64]{1,3,2,0:T(8,128)(2,1)S(1)}, bf16[1,128,16,64]{1,3,2,0:T(8,128)(2,1)S(1)}, u32[]{:S(2)}, u32[]{:S(2)}) %collective-permute-start.14) | collective-permute-done | bytes 262176 | tf_op jit(solution)/shard_map/ppermute | solution.py:38
  165.0 0.9 multiply_reduce_fusion
  166.8 0.7 fusion.118
  167.5 0.9 fusion.70
  168.7 1.3 convolution_bitcast_fusion.3
  170.1 0.7 copy.46
  171.5 4.0 %collective-permute-start.19 = (bf16[1,64,1]{2,1,0:T(8,128)(2,1)}, bf16[1,64,1]{2,1,0:T(8,128)(2,1)S(1)}, u32[]{:S(2)}, u32[]{:S(2)}) collective-permute-start(bf16[1,64,1]{2,1,0:T(8,128)(2,1)} %get-tuple-element.37), channel_id=1, source_target_pairs={{0,1},{1,2},{2,3},{3,4},{4,5},{5,6},{6,7},{7,8},{8,9},{9,10},{10,1... | collective-permute-start | bytes 392 | tf_op jit(solution)/shard_map/ppermute | solution.py:26
  175.6 5.0 %collective-permute-start.18 = (bf16[1,64,1]{2,1,0:T(8,128)(2,1)}, bf16[1,64,1]{2,1,0:T(8,128)(2,1)S(1)}, u32[]{:S(2)}, u32[]{:S(2)}) collective-permute-start(bf16[1,64,1]{2,1,0:T(8,128)(2,1)} %get-tuple-element.36), channel_id=1, source_target_pairs={{1,0},{2,1},{3,2},{4,3},{5,4},{6,5},{7,6},{8,7},{9,8},{10,9},{11,1... | collective-permute-start | bytes 392 | tf_op jit(solution)/shard_map/ppermute | solution.py:28
  180.6 3.8 %pad_maximum_fusion = f32[4,512,512]{2,1,0:T(8,128)} fusion(f32[1,512,512]{2,1,0:T(8,128)S(1)} %convolution_bitcast_fusion.2, f32[1,512,512]{2,1,0:T(8,128)} %convolution_bitcast_fusion.3, f32[1,512,512]{2,1,0:T(8,128)S(1)} %convolution_bitcast_fusion.4, f32[1,512,512]{2,1,0:T(8,128)S(1)} %convolution_bitcast_fusion.5), kind=kLoop, calls=%fused_computation.10 | loop fusion | flops 3145728 | bytes 8388608 | tf_op jit(solution)/shard_map/stack | solution.py:305
  184.4 5.3 %reshape_reshape.6 = f32[2,2,2,2,2,2,2,2,2,4,512]{10,9,8,7,6,5,4,3,2,1,0:T(4,128)} reshape(f32[4,512,512]{2,1,0:T(8,128)} %pad_maximum_fusion) | data formatting | bytes 8388608 | tf_op jit(solution)/shard_map/reshape;reshape | solution.py:96
  189.7 5.6 %copy.50 = f32[2,2,2,2,2,2,2,2,2,4,512]{10,9,7,8,1,5,2,6,3,0,4:T(4,128)} copy(f32[2,2,2,2,2,2,2,2,2,4,512]{10,9,8,7,6,5,4,3,2,1,0:T(4,128)} %reshape_reshape.6) | data formatting | bytes 8388608 | tf_op jit(solution)/shard_map/reshape;reshape | solution.py:96
  195.3 5.6 %reshape_reshape.7.big_ref = f32[4096,256]{1,0:T(8,128)} reshape(f32[2,2,2,2,2,2,2,2,2,4,512]{10,9,8,7,6,5,4,3,2,1,0:T(4,128)} %bitcast.249) | data formatting | bytes 8388608 | tf_op jit(solution)/shard_map/reshape;reshape | solution.py:185
  201.4 1.0 fusion.33
  202.4 2.4 fusion.30
  205.1 2.2 copy-done.1
  207.3 132.5 %shard_map.145 = (f32[8,256]{1,0:T(8,128)S(1)}, f32[184,256]{1,0:T(8,128)S(1)}) custom-call(f32[4096,256]{1,0:T(8,128)S(1)} %copy-done.1, f32[184,256]{1,0:T(8,128)S(1)} %reshape.608.small_ref), custom_call_target="tpu_custom_call" | custom-call | tf_op jit(solution)/shard_map/pallas_call | solution.py:164
  340.1 0.7 slice.312
  341.3 0.7 reshape.612
  342.0 0.7 reshape.611
  342.7 0.6 copy.47
  343.3 0.7 slice.263
  (128 shorter events, 11.4 us)
Async XLA Ops:
  0.6 26.7 %copy-start = (f32[64,512]{1,0:T(8,128)S(1)}, f32[64,512]{1,0:T(8,128)}, u32[]{:S(2)}) copy-start(f32[64,512]{1,0:T(8,128)} %param.17) | copy-start | bytes 393220
  1.9 0.7 copy-start.10
  2.5 19.1 %copy-start.8 = (f32[3,64,64]{2,1,0:T(8,128)S(1)}, f32[3,64,64]{2,1,0:T(8,128)}, u32[]{:S(2)}) copy-start(f32[3,64,64]{2,1,0:T(8,128)} %param.16) | copy-start | bytes 147460
  2.5 19.3 %copy-start.18 = (bf16[1,128]{1,0:T(2,128)(2,1)S(1)}, bf16[1,128]{1,0:T(2,128)(2,1)}, u32[]{:S(2)}) copy-start(bf16[1,128]{1,0:T(2,128)(2,1)} %param.11) | copy-start | bytes 772
  2.5 25.4 %copy-start.16 = (f32[512]{0:T(512)S(1)}, f32[512]{0:T(512)}, u32[]{:S(2)}) copy-start(f32[512]{0:T(512)} %param.18) | copy-start | bytes 6148
  2.5 25.5 %copy-start.2 = (bf16[4,512,512]{2,1,0:T(8,128)(2,1)S(1)}, bf16[4,512,512]{2,1,0:T(8,128)(2,1)}, u32[]{:S(2)}) copy-start(bf16[4,512,512]{2,1,0:T(8,128)(2,1)} %param.19) | copy-start | bytes 6291460
  7.0 24.8 %copy-start.5 = (bf16[1,128,512]{2,1,0:T(8,128)(2,1)S(1)}, bf16[1,128,512]{2,1,0:T(8,128)(2,1)}, u32[]{:S(2)}) copy-start(bf16[1,128,512]{2,1,0:T(8,128)(2,1)} %param.13) | copy-start | bytes 393220
  7.1 14.9 %collective-permute-start.1 = (f32[1,64,1]{2,1,0:T(8,128)S(1)}, f32[1,64,1]{2,1,0:T(8,128)S(1)}, u32[]{:S(2)}, u32[]{:S(2)}) collective-permute-start(f32[1,64,1]{2,1,0:T(8,128)S(1)} %get-tuple-element.35), channel_id=1, source_target_pairs={{1,0},{2,1},{3,2},{4,3},{5,4},{6,5},{7,6},{8,7},{9,8},{10,9},{11,1... | collective-permute-start | bytes 776 | tf_op jit(solution)/shard_map/ppermute | solution.py:28
  18.3 8.8 %collective-permute-start = (f32[1,64,1]{2,1,0:T(8,128)S(1)}, f32[1,64,1]{2,1,0:T(8,128)S(1)}, u32[]{:S(2)}, u32[]{:S(2)}) collective-permute-start(f32[1,64,1]{2,1,0:T(8,128)S(1)} %get-tuple-element.34), channel_id=1, source_target_pairs={{0,1},{1,2},{2,3},{3,4},{4,5},{5,6},{6,7},{7,8},{8,9},{9,10},{10,1... | collective-permute-start | bytes 776 | tf_op jit(solution)/shard_map/ppermute | solution.py:26
  22.0 0.6 copy-start.12
  27.1 21.2 %copy-start.14 = (f32[1,64,1]{2,1,0:T(8,128)}, f32[1,64,1]{2,1,0:T(8,128)S(1)}, u32[]{:S(2)}) copy-start(f32[1,64,1]{2,1,0:T(8,128)S(1)} %collective-permute-done) | copy-start | bytes 772
  29.4 30.1 %collective-permute-start.2 = (bf16[1,128,1025]{2,1,0:T(8,128)(2,1)}, bf16[1,128,1025]{2,1,0:T(8,128)(2,1)}, u32[]{:S(2)}, u32[]{:S(2)}) collective-permute-start(bf16[1,128,1025]{2,1,0:T(8,128)(2,1)} %get-tuple-element.32), channel_id=1, source_target_pairs={{0,15},{1,0},{2,1},{3,2},{4,3},{5,4},{6,5},{7,6},{8,7},{9,8},{10,9... | collective-permute-start | bytes 787208 | tf_op jit(solution)/shard_map/ppermute | solution.py:38
  32.2 30.8 %collective-permute-start.3 = (bf16[1,128,1025]{2,1,0:T(8,128)(2,1)}, bf16[1,128,1025]{2,1,0:T(8,128)(2,1)}, u32[]{:S(2)}, u32[]{:S(2)}) collective-permute-start(bf16[1,128,1025]{2,1,0:T(8,128)(2,1)} %get-tuple-element.32), channel_id=1, source_target_pairs={{0,1},{1,2},{2,3},{3,4},{4,5},{5,6},{6,7},{7,8},{8,9},{9,10},{10,1... | collective-permute-start | bytes 787208 | tf_op jit(solution)/shard_map/ppermute | solution.py:38
  36.6 49.5 %collective-permute-start.4 = (bf16[1,128,1025]{2,1,0:T(8,128)(2,1)}, bf16[1,128,1025]{2,1,0:T(8,128)(2,1)}, u32[]{:S(2)}, u32[]{:S(2)}) collective-permute-start(bf16[1,128,1025]{2,1,0:T(8,128)(2,1)} %get-tuple-element.32), channel_id=1, source_target_pairs={{0,14},{1,15},{2,0},{3,1},{4,2},{5,3},{6,4},{7,5},{8,6},{9,7},{10,... | collective-permute-start | bytes 787208 | tf_op jit(solution)/shard_map/ppermute | solution.py:38
  38.5 51.4 %collective-permute-start.5 = (bf16[1,128,1025]{2,1,0:T(8,128)(2,1)}, bf16[1,128,1025]{2,1,0:T(8,128)(2,1)}, u32[]{:S(2)}, u32[]{:S(2)}) collective-permute-start(bf16[1,128,1025]{2,1,0:T(8,128)(2,1)} %get-tuple-element.32), channel_id=1, source_target_pairs={{0,2},{1,3},{2,4},{3,5},{4,6},{5,7},{6,8},{7,9},{8,10},{9,11},{10,... | collective-permute-start | bytes 787208 | tf_op jit(solution)/shard_map/ppermute | solution.py:38
  46.3 45.4 %collective-permute-start.6 = (bf16[1,128,1025]{2,1,0:T(8,128)(2,1)}, bf16[1,128,1025]{2,1,0:T(8,128)(2,1)}, u32[]{:S(2)}, u32[]{:S(2)}) collective-permute-start(bf16[1,128,1025]{2,1,0:T(8,128)(2,1)} %get-tuple-element.32), channel_id=1, source_target_pairs={{0,13},{1,14},{2,15},{3,0},{4,1},{5,2},{6,3},{7,4},{8,5},{9,6},{10... | collective-permute-start | bytes 787208 | tf_op jit(solution)/shard_map/ppermute | solution.py:38
  59.4 34.0 %collective-permute-start.7 = (bf16[1,128,1025]{2,1,0:T(8,128)(2,1)}, bf16[1,128,1025]{2,1,0:T(8,128)(2,1)S(1)}, u32[]{:S(2)}, u32[]{:S(2)}) collective-permute-start(bf16[1,128,1025]{2,1,0:T(8,128)(2,1)} %get-tuple-element.32), channel_id=1, source_target_pairs={{0,3},{1,4},{2,5},{3,6},{4,7},{5,8},{6,9},{7,10},{8,11},{9,12},{10... | collective-permute-start | bytes 787208 | tf_op jit(solution)/shard_map/ppermute | solution.py:38
  63.1 31.1 %collective-permute-start.8 = (bf16[1,128,1025]{2,1,0:T(8,128)(2,1)}, bf16[1,128,1025]{2,1,0:T(8,128)(2,1)S(1)}, u32[]{:S(2)}, u32[]{:S(2)}) collective-permute-start(bf16[1,128,1025]{2,1,0:T(8,128)(2,1)} %get-tuple-element.32), channel_id=1, source_target_pairs={{0,12},{1,13},{2,14},{3,15},{4,0},{5,1},{6,2},{7,3},{8,4},{9,5},{1... | collective-permute-start | bytes 787208 | tf_op jit(solution)/shard_map/ppermute | solution.py:38
  86.0 8.9 %collective-permute-start.9 = (bf16[1,128,1025]{2,1,0:T(8,128)(2,1)}, bf16[1,128,1025]{2,1,0:T(8,128)(2,1)S(1)}, u32[]{:S(2)}, u32[]{:S(2)}) collective-permute-start(bf16[1,128,1025]{2,1,0:T(8,128)(2,1)} %get-tuple-element.32), channel_id=1, source_target_pairs={{0,4},{1,5},{2,6},{3,7},{4,8},{5,9},{6,10},{7,11},{8,12},{9,13},{1... | collective-permute-start | bytes 787208 | tf_op jit(solution)/shard_map/ppermute | solution.py:38
  110.1 22.3 %collective-permute-start.10 = (bf16[1,128,16,64]{1,3,2,0:T(8,128)(2,1)S(1)}, bf16[1,128,16,64]{1,3,2,0:T(8,128)(2,1)S(1)}, u32[]{:S(2)}, u32[]{:S(2)}) collective-permute-start(bf16[1,128,16,64]{1,3,2,0:T(8,128)(2,1)S(1)} %pad_maximum_fusion.2), channel_id=1, source_target_pairs={{0,1},{1,2},{2,3},{3,4},{4,5},{5,6},{6,7},{7,8},{8,9},{9,10},{10,1... | collective-permute-start | bytes 786440 | tf_op jit(solution)/shard_map/ppermute | solution.py:38
  115.3 31.5 %copy-start.6 = (bf16[1,128,512]{2,1,0:T(8,128)(2,1)S(1)}, bf16[1,128,512]{2,1,0:T(8,128)(2,1)}, u32[]{:S(2)}) copy-start(bf16[1,128,512]{2,1,0:T(8,128)(2,1)} %param.13) | copy-start | bytes 393220
  115.3 22.8 %collective-permute-start.11 = (bf16[1,128,16,64]{1,3,2,0:T(8,128)(2,1)S(1)}, bf16[1,128,16,64]{1,3,2,0:T(8,128)(2,1)S(1)}, u32[]{:S(2)}, u32[]{:S(2)}) collective-permute-start(bf16[1,128,16,64]{1,3,2,0:T(8,128)(2,1)S(1)} %pad_maximum_fusion.3), channel_id=1, source_target_pairs={{0,15},{1,0},{2,1},{3,2},{4,3},{5,4},{6,5},{7,6},{8,7},{9,8},{10,9... | collective-permute-start | bytes 786440 | tf_op jit(solution)/shard_map/ppermute | solution.py:38
  119.2 25.6 %collective-permute-start.12 = (bf16[1,128,16,64]{1,3,2,0:T(8,128)(2,1)S(1)}, bf16[1,128,16,64]{1,3,2,0:T(8,128)(2,1)S(1)}, u32[]{:S(2)}, u32[]{:S(2)}) collective-permute-start(bf16[1,128,16,64]{1,3,2,0:T(8,128)(2,1)S(1)} %pad_maximum_fusion.4), channel_id=1, source_target_pairs={{0,2},{1,3},{2,4},{3,5},{4,6},{5,7},{6,8},{7,9},{8,10},{9,11},{10,... | collective-permute-start | bytes 786440 | tf_op jit(solution)/shard_map/ppermute | solution.py:38
  123.5 25.0 %collective-permute-start.13 = (bf16[1,128,16,64]{1,3,2,0:T(8,128)(2,1)S(1)}, bf16[1,128,16,64]{1,3,2,0:T(8,128)(2,1)S(1)}, u32[]{:S(2)}, u32[]{:S(2)}) collective-permute-start(bf16[1,128,16,64]{1,3,2,0:T(8,128)(2,1)S(1)} %pad_maximum_fusion.5), channel_id=1, source_target_pairs={{0,14},{1,15},{2,0},{3,1},{4,2},{5,3},{6,4},{7,5},{8,6},{9,7},{10,... | collective-permute-start | bytes 786440 | tf_op jit(solution)/shard_map/ppermute | solution.py:38
  129.9 17.2 %copy-start.3 = (bf16[4,512,512]{2,1,0:T(8,128)(2,1)S(1)}, bf16[4,512,512]{2,1,0:T(8,128)(2,1)}, u32[]{:S(2)}) copy-start(bf16[4,512,512]{2,1,0:T(8,128)(2,1)} %param.19) | copy-start | bytes 6291460
  129.9 34.1 %collective-permute-start.14 = (bf16[1,128,16,64]{1,3,2,0:T(8,128)(2,1)S(1)}, bf16[1,128,16,64]{1,3,2,0:T(8,128)(2,1)S(1)}, u32[]{:S(2)}, u32[]{:S(2)}) collective-permute-start(bf16[1,128,16,64]{1,3,2,0:T(8,128)(2,1)S(1)} %pad_maximum_fusion.6), channel_id=1, source_target_pairs={{0,3},{1,4},{2,5},{3,6},{4,7},{5,8},{6,9},{7,10},{8,11},{9,12},{10... | collective-permute-start | bytes 786440 | tf_op jit(solution)/shard_map/ppermute | solution.py:38
  132.4 31.6 %collective-permute-start.15 = (bf16[1,128,16,64]{1,3,2,0:T(8,128)(2,1)S(1)}, bf16[1,128,16,64]{1,3,2,0:T(8,128)(2,1)S(1)}, u32[]{:S(2)}, u32[]{:S(2)}) collective-permute-start(bf16[1,128,16,64]{1,3,2,0:T(8,128)(2,1)S(1)} %pad_maximum_fusion.7), channel_id=1, source_target_pairs={{0,13},{1,14},{2,15},{3,0},{4,1},{5,2},{6,3},{7,4},{8,5},{9,6},{10... | collective-permute-start | bytes 786440 | tf_op jit(solution)/shard_map/ppermute | solution.py:38
  138.2 25.9 %collective-permute-start.16 = (bf16[1,128,16,64]{1,3,2,0:T(8,128)(2,1)S(1)}, bf16[1,128,16,64]{1,3,2,0:T(8,128)(2,1)S(1)}, u32[]{:S(2)}, u32[]{:S(2)}) collective-permute-start(bf16[1,128,16,64]{1,3,2,0:T(8,128)(2,1)S(1)} %pad_maximum_fusion.8), channel_id=1, source_target_pairs={{0,4},{1,5},{2,6},{3,7},{4,8},{5,9},{6,10},{7,11},{8,12},{9,13},{1... | collective-permute-start | bytes 786440 | tf_op jit(solution)/shard_map/ppermute | solution.py:38
  144.8 19.3 %collective-permute-start.17 = (bf16[1,128,16,64]{1,3,2,0:T(8,128)(2,1)S(1)}, bf16[1,128,16,64]{1,3,2,0:T(8,128)(2,1)S(1)}, u32[]{:S(2)}, u32[]{:S(2)}) collective-permute-start(bf16[1,128,16,64]{1,3,2,0:T(8,128)(2,1)S(1)} %pad_maximum_fusion.9), channel_id=1, source_target_pairs={{0,12},{1,13},{2,14},{3,15},{4,0},{5,1},{6,2},{7,3},{8,4},{9,5},{1... | collective-permute-start | bytes 786440 | tf_op jit(solution)/shard_map/ppermute | solution.py:38
  166.0 5.0 %copy-start.15 = (f32[1,64,1]{2,1,0:T(8,128)S(1)}, f32[1,64,1]{2,1,0:T(8,128)}, u32[]{:S(2)}) copy-start(f32[1,64,1]{2,1,0:T(8,128)} %copy-done.14) | copy-start | bytes 772
  166.0 5.2 %copy-start.13 = (f32[1,64,1]{2,1,0:T(8,128)S(1)}, f32[1,64,1]{2,1,0:T(8,128)}, u32[]{:S(2)}) copy-start(f32[1,64,1]{2,1,0:T(8,128)} %copy-done.12) | copy-start | bytes 772
  171.5 29.3 %collective-permute-start.19 = (bf16[1,64,1]{2,1,0:T(8,128)(2,1)}, bf16[1,64,1]{2,1,0:T(8,128)(2,1)S(1)}, u32[]{:S(2)}, u32[]{:S(2)}) collective-permute-start(bf16[1,64,1]{2,1,0:T(8,128)(2,1)} %get-tuple-element.37), channel_id=1, source_target_pairs={{0,1},{1,2},{2,3},{3,4},{4,5},{5,6},{6,7},{7,8},{8,9},{9,10},{10,1... | collective-permute-start | bytes 392 | tf_op jit(solution)/shard_map/ppermute | solution.py:26
  175.6 25.5 %collective-permute-start.18 = (bf16[1,64,1]{2,1,0:T(8,128)(2,1)}, bf16[1,64,1]{2,1,0:T(8,128)(2,1)S(1)}, u32[]{:S(2)}, u32[]{:S(2)}) collective-permute-start(bf16[1,64,1]{2,1,0:T(8,128)(2,1)} %get-tuple-element.36), channel_id=1, source_target_pairs={{1,0},{2,1},{3,2},{4,3},{5,4},{6,5},{7,6},{8,7},{9,8},{10,9},{11,1... | collective-permute-start | bytes 392 | tf_op jit(solution)/shard_map/ppermute | solution.py:28
  195.3 5.6 %copy-start.9 = (f32[3,64,64]{2,1,0:T(8,128)S(1)}, f32[3,64,64]{2,1,0:T(8,128)}, u32[]{:S(2)}) copy-start(f32[3,64,64]{2,1,0:T(8,128)} %param.16) | copy-start | bytes 147460
  195.3 6.1 %copy-start.4 = (f32[64,64,128]{2,0,1:T(8,128)S(1)}, f32[64,64,128]{2,0,1:T(8,128)}, u32[]{:S(2)}) copy-start(f32[64,64,128]{2,0,1:T(8,128)} %get-tuple-element.41) | copy-start | bytes 6291460
  195.3 6.1 %copy-start.19 = (f32[64]{0:T(128)S(1)}, f32[64]{0:T(128)}, u32[]{:S(2)}) copy-start(f32[64]{0:T(128)} %param.15) | copy-start | bytes 772
  200.9 1.5 copy-start.11
  202.3 2.5 copy-start.7
  202.4 2.5 copy-start.17
  205.1 2.2 copy-start.1

commit v5 on v4

--- a/solution.py
+++ b/solution.py
@@ -93,26 +93,32 @@
         if pending_sites:
             order.append(pending_sites.pop(0))
     order = list(dict.fromkeys(order))
-    cells = flat.reshape((2,) * total_bits + (chunk // 512, 512))
+    cells = flat.reshape((2,) * total_bits + (chunk // LANES, LANES))
     cells = cells.transpose([dim_of[o] for o in order] + [total_bits, total_bits + 1])
-    current = cells.reshape(-1)
-    return butterfly_kernel(current, small, order, chunk)
+    current = cells.reshape(-1, LANES)
+    small_order = order[3:4] + order[2:3] + order[1:2] + order[0:1] + order[5:6] + order[4:5]
+    small_order += order[8:9] + order[6:7] + order[7:8]
+    small_order += [o for o in order if o not in small_order]
+    small_order = list(dict.fromkeys(small_order))
+    return butterfly_kernel(current, small, order, small_order, chunk)
 
 
 LANES = 256
 
 
-def butterfly_body(order, steps_rows, small_rows, big_ref, small_ref, out_ref, small_out_ref,
+def butterfly_body(order, small_order, steps_rows, small_rows, big_ref, small_ref, out_ref, small_out_ref,
                    acc, small_acc, recv, small_recv, send_sems, recv_sems, small_send_sems,
                    small_recv_sems):
     me = {"sims": lax.axis_index("sims"), "sites": lax.axis_index("sites")}
-    partners = []
-    for axis, bit in order:
+    def partner(axis, bit):
         step = 1 << bit
         mine = (me[axis] // step) % 2
         other = dict(me)
         other[axis] = me[axis] + (1 - 2 * mine) * step
-        partners.append(((other["sims"], other["sites"]), mine))
+        return ((other["sims"], other["sites"]), mine)
+
+    partners = [partner(axis, bit) for axis, bit in order]
+    small_partners = [partner(axis, bit)[0] for axis, bit in small_order]
     barrier = pltpu.get_barrier_semaphore()
     for device, _ in partners:
         pl.semaphore_signal(barrier, inc=1, device_id=device, device_id_type=pl.DeviceIdType.MESH)
@@ -137,7 +143,7 @@
             dst_ref=small_recv.at[k],
             send_sem=small_send_sems.at[k],
             recv_sem=small_recv_sems.at[k],
-            device_id=device,
+            device_id=small_partners[k],
             device_id_type=pl.DeviceIdType.MESH,
         )
         big_copy.start()
@@ -154,15 +160,15 @@
     small_out_ref[...] = small_acc[...]
 
 
-def butterfly_kernel(current, small, order, chunk):
+def butterfly_kernel(current, small, order, small_order, chunk):
     size = small.shape[0]
     small_rows = -(-size // (LANES * 8)) * 8
     small_grid = jnp.pad(small, (0, small_rows * LANES - size)).reshape(small_rows, LANES)
-    big_rows = current.shape[0] // LANES
+    big_rows = current.shape[0]
     steps_rows = [big_rows >> (k + 1) for k in range(len(order))]
     f32 = jnp.float32
     out, small_out = pl.pallas_call(
-        functools.partial(butterfly_body, order, steps_rows, small_rows),
+        functools.partial(butterfly_body, order, small_order, steps_rows, small_rows),
         out_shape=(
             jax.ShapeDtypeStruct((steps_rows[-1], LANES), f32),
             jax.ShapeDtypeStruct((small_rows, LANES), f32),
@@ -182,7 +188,7 @@
         compiler_params=pltpu.CompilerParams(
             collective_id=0, has_side_effects=True, vmem_limit_bytes=48 * 1024 * 1024
         ),
-    )(current.reshape(big_rows, LANES), small_grid)
+    )(current, small_grid)
     return out.reshape(chunk), small_out.reshape(-1)[:size]
 
 def per_device(

time: 350 us -> 311 us (0.89)
  Pallas kernels: 133 us -> 102 us
  waiting for transfers between devices: 32 us -> 15.5 us
  starting transfers between devices: 102 us -> 118 us
  local copies, waits for them, and re-layouts: 42.6 us -> 36.1 us
    pallas_call x1, Pallas kernels: 133 us -> 102 us  [butterfly_kernel(): pl.pallas_call(functools.partial(butterfly_body, order, small_order, step...]
    ppermute x16, starting transfers between devices: 79.6 us -> 96.3 us  [from_behind(): return lax.ppermute(value, axis, pairs)]
    ppermute x16, waiting for transfers between devices: 27.5 us -> 11 us  [from_behind(): return lax.ppermute(value, axis, pairs)]
    another operation x3 -> x2, local copies, waits for them, and re-layouts: 16.4 us -> 9.91 us  [butterfly_sum(): cells = flat.reshape((2,) * total_bits + (chunk // LANES, LANES))]
  transfers between devices with their start and end apart: 20 -> 20, of which waited for: 5 -> 2; matrix products, arithmetic and copies ran while one was open for 10% -> 9% of each run, Pallas kernels for 0% -> 0%
where the time goes in v5:
time: 311 us; the launch traced here: 307 us
  starting transfers between devices  118 us (38%)
  Pallas kernels  102 us (33%)
  local copies, waits for them, and re-layouts  36.1 us (12%)
  matrix products  20.8 us (7%)
  waiting for transfers between devices  15.5 us (5%)
  other arithmetic  11.9 us (4%)
    pallas_call x1, Pallas kernels, butterfly_kernel(): pl.pallas_call(functools.partial(butterfly_body, order, small_order, step...  102 us
    ppermute x16, starting transfers between devices, from_behind(): return lax.ppermute(value, axis, pairs)  96.3 us
    ppermute x2, starting transfers between devices, extended(): lax.ppermute(head, axis, [((i + 1) % count, i) for i in range(count)])  16.6 us
    unnamed x50, local copies, waits for them, and re-layouts  14.6 us
    ppermute x16, waiting for transfers between devices, from_behind(): return lax.ppermute(value, axis, pairs)  11 us
    another operation x2, local copies, waits for them, and re-layouts, butterfly_sum(): cells = flat.reshape((2,) * total_bits + (chunk // LANES, LANES))  9.91 us
  transfers between devices with their start and end apart: 20, of which 2 were waited for; matrix products, arithmetic and copies ran while one was open for 9% of the time, Pallas kernels for 0%

profile of v5, /device:TPU:6, one launch (start us, length us, event | category | flops | bytes accessed | tf_op | source)
XLA Modules:
  0.0 307.1 jit_solution(5069949762542367457)
XLA Ops:
  0.6 1.0 convert_element_type.179
  1.9 0.6 copy-done.10
  2.5 4.5 %fusion.16 = (f32[64,128]{1,0:T(8,128)S(1)}, f32[64,64,128]{2,0,1:T(8,128)}) fusion(f32[64]{0:T(128)} %param.15, f32[64,128,4]{1,2,0:T(4,128)S(1)} %copy.29, f32[4,64]{1,0:T(4,128)} %param.14), kind=kOutput, calls=%fused_computation.25 | convolution fusion | flops 28303360 | bytes 2262272 | tf_op jit(solution)/shard_map/shtk,kc->shct/dot_general | solution.py:218
  7.2 11.2 %collective-permute-start.1 = (f32[1,64,1]{2,1,0:T(8,128)S(1)}, f32[1,64,1]{2,1,0:T(8,128)S(1)}, u32[]{:S(2)}, u32[]{:S(2)}) collective-permute-start(f32[1,64,1]{2,1,0:T(8,128)S(1)} %get-tuple-element.35), channel_id=1, source_target_pairs={{1,0},{2,1},{3,2},{4,3},{5,4},{6,5},{7,6},{8,7},{9,8},{10,9},{11,1... | collective-permute-start | bytes 776 | tf_op jit(solution)/shard_map/ppermute | solution.py:28
  18.4 1.9 collective-permute-start
  22.7 4.5 %collective-permute-done = f32[1,64,1]{2,1,0:T(8,128)S(1)} collective-permute-done((f32[1,64,1]{2,1,0:T(8,128)S(1)}, f32[1,64,1]{2,1,0:T(8,128)S(1)}, u32[]{:S(2)}, u32[]{:S(2)}) %collective-permute-start) | collective-permute-done | bytes 288 | tf_op jit(solution)/shard_map/ppermute | solution.py:26
  27.5 0.5 multiply_reduce_fusion.2
  28.6 0.9 pad_maximum_fusion.1
  29.5 2.4 collective-permute-start.2
  32.3 4.3 %collective-permute-start.3 = (bf16[1,128,1025]{2,1,0:T(8,128)(2,1)}, bf16[1,128,1025]{2,1,0:T(8,128)(2,1)}, u32[]{:S(2)}, u32[]{:S(2)}) collective-permute-start(bf16[1,128,1025]{2,1,0:T(8,128)(2,1)} %get-tuple-element.32), channel_id=1, source_target_pairs={{0,1},{1,2},{2,3},{3,4},{4,5},{5,6},{6,7},{7,8},{8,9},{9,10},{10,1... | collective-permute-start | bytes 787208 | tf_op jit(solution)/shard_map/ppermute | solution.py:38
  36.6 1.9 collective-permute-start.4
  38.6 7.8 %collective-permute-start.5 = (bf16[1,128,1025]{2,1,0:T(8,128)(2,1)}, bf16[1,128,1025]{2,1,0:T(8,128)(2,1)}, u32[]{:S(2)}, u32[]{:S(2)}) collective-permute-start(bf16[1,128,1025]{2,1,0:T(8,128)(2,1)} %get-tuple-element.32), channel_id=1, source_target_pairs={{0,2},{1,3},{2,4},{3,5},{4,6},{5,7},{6,8},{7,9},{8,10},{9,11},{10,... | collective-permute-start | bytes 787208 | tf_op jit(solution)/shard_map/ppermute | solution.py:38
  46.4 1.9 collective-permute-start.6
  48.7 8.8 %collective-permute-start.7 = (bf16[1,128,1025]{2,1,0:T(8,128)(2,1)}, bf16[1,128,1025]{2,1,0:T(8,128)(2,1)S(1)}, u32[]{:S(2)}, u32[]{:S(2)}) collective-permute-start(bf16[1,128,1025]{2,1,0:T(8,128)(2,1)} %get-tuple-element.32), channel_id=1, source_target_pairs={{0,3},{1,4},{2,5},{3,6},{4,7},{5,8},{6,9},{7,10},{8,11},{9,12},{10... | collective-permute-start | bytes 787208 | tf_op jit(solution)/shard_map/ppermute | solution.py:38
  57.6 1.7 constant_dynamic-update-slice_fusion.7
  59.3 25.1 %collective-permute-start.8 = (bf16[1,128,1025]{2,1,0:T(8,128)(2,1)}, bf16[1,128,1025]{2,1,0:T(8,128)(2,1)S(1)}, u32[]{:S(2)}, u32[]{:S(2)}) collective-permute-start(bf16[1,128,1025]{2,1,0:T(8,128)(2,1)} %get-tuple-element.32), channel_id=1, source_target_pairs={{0,12},{1,13},{2,14},{3,15},{4,0},{5,1},{6,2},{7,3},{8,4},{9,5},{1... | collective-permute-start | bytes 787208 | tf_op jit(solution)/shard_map/ppermute | solution.py:38
  84.4 1.7 constant_dynamic-update-slice_fusion.6
  86.1 3.1 %collective-permute-start.9 = (bf16[1,128,1025]{2,1,0:T(8,128)(2,1)}, bf16[1,128,1025]{2,1,0:T(8,128)(2,1)S(1)}, u32[]{:S(2)}, u32[]{:S(2)}) collective-permute-start(bf16[1,128,1025]{2,1,0:T(8,128)(2,1)} %get-tuple-element.32), channel_id=1, source_target_pairs={{0,4},{1,5},{2,6},{3,7},{4,8},{5,9},{6,10},{7,11},{8,12},{9,13},{1... | collective-permute-start | bytes 787208 | tf_op jit(solution)/shard_map/ppermute | solution.py:38
  89.2 1.7 constant_dynamic-update-slice_fusion.5
  90.9 1.7 constant_dynamic-update-slice_fusion.4
  92.6 1.7 constant_dynamic-update-slice_fusion.3
  94.3 0.7 constant_dynamic-update-slice_fusion.2
  95.1 0.7 constant_dynamic-update-slice_fusion.1
  95.8 0.7 constant_dynamic-update-slice_fusion
  96.5 2.8 fusion.114
  99.4 1.1 convert_reduce_fusion
  100.5 0.7 copy.31
  101.2 1.7 copy.34
  102.9 0.8 fusion.5
  103.7 1.8 fusion.119
  105.5 0.6 fusion.20
  106.1 1.0 bitcast_convert_fusion
  107.1 1.3 fusion.8
  108.4 1.0 convolution_convert_fusion.5
  109.4 0.5 fusion.121
  110.9 7.5 %collective-permute-start.10 = (bf16[1,128,16,64]{1,3,2,0:T(8,128)(2,1)S(1)}, bf16[1,128,16,64]{1,3,2,0:T(8,128)(2,1)S(1)}, u32[]{:S(2)}, u32[]{:S(2)}) collective-permute-start(bf16[1,128,16,64]{1,3,2,0:T(8,128)(2,1)S(1)} %pad_maximum_fusion.2), channel_id=1, source_target_pairs={{0,1},{1,2},{2,3},{3,4},{4,5},{5,6},{6,7},{7,8},{8,9},{9,10},{10,1... | collective-permute-start | bytes 786440 | tf_op jit(solution)/shard_map/ppermute | solution.py:38
  118.5 2.1 collective-permute-start.11
  120.6 5.5 %collective-permute-start.12 = (bf16[1,128,16,64]{1,3,2,0:T(8,128)(2,1)S(1)}, bf16[1,128,16,64]{1,3,2,0:T(8,128)(2,1)S(1)}, u32[]{:S(2)}, u32[]{:S(2)}) collective-permute-start(bf16[1,128,16,64]{1,3,2,0:T(8,128)(2,1)S(1)} %pad_maximum_fusion.4), channel_id=1, source_target_pairs={{0,2},{1,3},{2,4},{3,5},{4,6},{5,7},{6,8},{7,9},{8,10},{9,11},{10,... | collective-permute-start | bytes 786440 | tf_op jit(solution)/shard_map/ppermute | solution.py:38
  126.1 5.2 %collective-permute-start.13 = (bf16[1,128,16,64]{1,3,2,0:T(8,128)(2,1)S(1)}, bf16[1,128,16,64]{1,3,2,0:T(8,128)(2,1)S(1)}, u32[]{:S(2)}, u32[]{:S(2)}) collective-permute-start(bf16[1,128,16,64]{1,3,2,0:T(8,128)(2,1)S(1)} %pad_maximum_fusion.5), channel_id=1, source_target_pairs={{0,14},{1,15},{2,0},{3,1},{4,2},{5,3},{6,4},{7,5},{8,6},{9,7},{10,... | collective-permute-start | bytes 786440 | tf_op jit(solution)/shard_map/ppermute | solution.py:38
  131.3 2.5 collective-permute-start.14
  134.3 5.3 %collective-permute-start.15 = (bf16[1,128,16,64]{1,3,2,0:T(8,128)(2,1)S(1)}, bf16[1,128,16,64]{1,3,2,0:T(8,128)(2,1)S(1)}, u32[]{:S(2)}, u32[]{:S(2)}) collective-permute-start(bf16[1,128,16,64]{1,3,2,0:T(8,128)(2,1)S(1)} %pad_maximum_fusion.7), channel_id=1, source_target_pairs={{0,13},{1,14},{2,15},{3,0},{4,1},{5,2},{6,3},{7,4},{8,5},{9,6},{10... | collective-permute-start | bytes 786440 | tf_op jit(solution)/shard_map/ppermute | solution.py:38
  139.6 11.0 %collective-permute-start.16 = (bf16[1,128,16,64]{1,3,2,0:T(8,128)(2,1)S(1)}, bf16[1,128,16,64]{1,3,2,0:T(8,128)(2,1)S(1)}, u32[]{:S(2)}, u32[]{:S(2)}) collective-permute-start(bf16[1,128,16,64]{1,3,2,0:T(8,128)(2,1)S(1)} %pad_maximum_fusion.8), channel_id=1, source_target_pairs={{0,4},{1,5},{2,6},{3,7},{4,8},{5,9},{6,10},{7,11},{8,12},{9,13},{1... | collective-permute-start | bytes 786440 | tf_op jit(solution)/shard_map/ppermute | solution.py:38
  150.6 1.9 collective-permute-start.17
  153.3 11.0 %collective-permute-done.14 = bf16[1,128,16,64]{1,3,2,0:T(8,128)(2,1)S(1)} collective-permute-done((bf16[1,128,16,64]{1,3,2,0:T(8,128)(2,1)S(1)}, bf16[1,128,16,64]{1,3,2,0:T(8,128)(2,1)S(1)}, u32[]{:S(2)}, u32[]{:S(2)}) %collective-permute-start.14) | collective-permute-done | bytes 262176 | tf_op jit(solution)/shard_map/ppermute | solution.py:38
  165.3 0.9 multiply_reduce_fusion
  167.1 0.7 fusion.118
  167.8 0.9 fusion.70
  169.0 1.3 convolution_bitcast_fusion.3
  170.3 0.7 copy.46
  171.8 3.6 %collective-permute-start.19 = (bf16[1,64,1]{2,1,0:T(8,128)(2,1)}, bf16[1,64,1]{2,1,0:T(8,128)(2,1)S(1)}, u32[]{:S(2)}, u32[]{:S(2)}) collective-permute-start(bf16[1,64,1]{2,1,0:T(8,128)(2,1)} %get-tuple-element.37), channel_id=1, source_target_pairs={{0,1},{1,2},{2,3},{3,4},{4,5},{5,6},{6,7},{7,8},{8,9},{9,10},{10,1... | collective-permute-start | bytes 392 | tf_op jit(solution)/shard_map/ppermute | solution.py:26
  175.5 5.4 %collective-permute-start.18 = (bf16[1,64,1]{2,1,0:T(8,128)(2,1)}, bf16[1,64,1]{2,1,0:T(8,128)(2,1)S(1)}, u32[]{:S(2)}, u32[]{:S(2)}) collective-permute-start(bf16[1,64,1]{2,1,0:T(8,128)(2,1)} %get-tuple-element.36), channel_id=1, source_target_pairs={{1,0},{2,1},{3,2},{4,3},{5,4},{6,5},{7,6},{8,7},{9,8},{10,9},{11,1... | collective-permute-start | bytes 392 | tf_op jit(solution)/shard_map/ppermute | solution.py:28
  180.9 3.8 %pad_maximum_fusion = f32[4,512,512]{2,1,0:T(8,128)} fusion(f32[1,512,512]{2,1,0:T(8,128)S(1)} %convolution_bitcast_fusion.2, f32[1,512,512]{2,1,0:T(8,128)} %convolution_bitcast_fusion.3, f32[1,512,512]{2,1,0:T(8,128)S(1)} %convolution_bitcast_fusion.4, f32[1,512,512]{2,1,0:T(8,128)S(1)} %convolution_bitcast_fusion.5), kind=kLoop, calls=%fused_computation.10 | loop fusion | flops 3145728 | bytes 8388608 | tf_op jit(solution)/shard_map/stack | solution.py:311
  184.7 5.0 %reshape_reshape.3 = f32[2,2,2,2,2,2,2,2,2,8,256]{10,9,8,7,6,5,4,3,2,1,0:T(8,128)} reshape(f32[4,512,512]{2,1,0:T(8,128)} %pad_maximum_fusion) | data formatting | bytes 8388608 | tf_op jit(solution)/shard_map/reshape;reshape | solution.py:96
  189.8 4.9 %copy.35 = f32[2,2,2,2,2,2,2,2,2,8,256]{10,9,7,8,1,5,2,6,3,0,4:T(8,128)} copy(f32[2,2,2,2,2,2,2,2,2,8,256]{10,9,8,7,6,5,4,3,2,1,0:T(8,128)} %reshape_reshape.3) | data formatting | bytes 8388608 | tf_op jit(solution)/shard_map/reshape;reshape | solution.py:96
  195.1 1.0 fusion.33
  196.1 2.4 fusion.30
  198.9 2.2 copy-done.1
  201.0 101.9 %shard_map.145 = (f32[8,256]{1,0:T(8,128)S(1)}, f32[184,256]{1,0:T(8,128)S(1)}) custom-call(f32[4096,256]{1,0:T(8,128)S(1)} %bitcast.247, f32[184,256]{1,0:T(8,128)S(1)} %reshape.612.small_ref), custom_call_target="tpu_custom_call" | custom-call | tf_op jit(solution)/shard_map/pallas_call | solution.py:170
  303.3 0.7 slice.312
  303.9 0.5 slice.309
  304.4 0.7 reshape.616
  305.1 0.7 reshape.615
  305.8 0.6 copy.47
  306.4 0.7 slice.263
  (127 shorter events, 9.7 us)
Async XLA Ops:
  0.6 26.8 %copy-start = (f32[64,512]{1,0:T(8,128)S(1)}, f32[64,512]{1,0:T(8,128)}, u32[]{:S(2)}) copy-start(f32[64,512]{1,0:T(8,128)} %param.17) | copy-start | bytes 393220
  1.9 0.7 copy-start.10
  2.5 19.1 %copy-start.8 = (f32[3,64,64]{2,1,0:T(8,128)S(1)}, f32[3,64,64]{2,1,0:T(8,128)}, u32[]{:S(2)}) copy-start(f32[3,64,64]{2,1,0:T(8,128)} %param.16) | copy-start | bytes 147460
  2.5 19.4 %copy-start.18 = (bf16[1,128]{1,0:T(2,128)(2,1)S(1)}, bf16[1,128]{1,0:T(2,128)(2,1)}, u32[]{:S(2)}) copy-start(bf16[1,128]{1,0:T(2,128)(2,1)} %param.11) | copy-start | bytes 772
  2.5 25.5 %copy-start.16 = (f32[512]{0:T(512)S(1)}, f32[512]{0:T(512)}, u32[]{:S(2)}) copy-start(f32[512]{0:T(512)} %param.18) | copy-start | bytes 6148
  2.5 25.6 %copy-start.2 = (bf16[4,512,512]{2,1,0:T(8,128)(2,1)S(1)}, bf16[4,512,512]{2,1,0:T(8,128)(2,1)}, u32[]{:S(2)}) copy-start(bf16[4,512,512]{2,1,0:T(8,128)(2,1)} %param.19) | copy-start | bytes 6291460
  7.1 24.8 %copy-start.5 = (bf16[1,128,512]{2,1,0:T(8,128)(2,1)S(1)}, bf16[1,128,512]{2,1,0:T(8,128)(2,1)}, u32[]{:S(2)}) copy-start(bf16[1,128,512]{2,1,0:T(8,128)(2,1)} %param.13) | copy-start | bytes 393220
  7.2 14.9 %collective-permute-start.1 = (f32[1,64,1]{2,1,0:T(8,128)S(1)}, f32[1,64,1]{2,1,0:T(8,128)S(1)}, u32[]{:S(2)}, u32[]{:S(2)}) collective-permute-start(f32[1,64,1]{2,1,0:T(8,128)S(1)} %get-tuple-element.35), channel_id=1, source_target_pairs={{1,0},{2,1},{3,2},{4,3},{5,4},{6,5},{7,6},{8,7},{9,8},{10,9},{11,1... | collective-permute-start | bytes 776 | tf_op jit(solution)/shard_map/ppermute | solution.py:28
  18.4 8.8 %collective-permute-start = (f32[1,64,1]{2,1,0:T(8,128)S(1)}, f32[1,64,1]{2,1,0:T(8,128)S(1)}, u32[]{:S(2)}, u32[]{:S(2)}) collective-permute-start(f32[1,64,1]{2,1,0:T(8,128)S(1)} %get-tuple-element.34), channel_id=1, source_target_pairs={{0,1},{1,2},{2,3},{3,4},{4,5},{5,6},{6,7},{7,8},{8,9},{9,10},{10,1... | collective-permute-start | bytes 776 | tf_op jit(solution)/shard_map/ppermute | solution.py:26
  22.1 0.6 copy-start.12
  27.2 21.2 %copy-start.14 = (f32[1,64,1]{2,1,0:T(8,128)}, f32[1,64,1]{2,1,0:T(8,128)S(1)}, u32[]{:S(2)}) copy-start(f32[1,64,1]{2,1,0:T(8,128)S(1)} %collective-permute-done) | copy-start | bytes 772
  29.5 19.3 %collective-permute-start.2 = (bf16[1,128,1025]{2,1,0:T(8,128)(2,1)}, bf16[1,128,1025]{2,1,0:T(8,128)(2,1)}, u32[]{:S(2)}, u32[]{:S(2)}) collective-permute-start(bf16[1,128,1025]{2,1,0:T(8,128)(2,1)} %get-tuple-element.32), channel_id=1, source_target_pairs={{0,15},{1,0},{2,1},{3,2},{4,3},{5,4},{6,5},{7,6},{8,7},{9,8},{10,9... | collective-permute-start | bytes 787208 | tf_op jit(solution)/shard_map/ppermute | solution.py:38
  32.3 26.9 %collective-permute-start.3 = (bf16[1,128,1025]{2,1,0:T(8,128)(2,1)}, bf16[1,128,1025]{2,1,0:T(8,128)(2,1)}, u32[]{:S(2)}, u32[]{:S(2)}) collective-permute-start(bf16[1,128,1025]{2,1,0:T(8,128)(2,1)} %get-tuple-element.32), channel_id=1, source_target_pairs={{0,1},{1,2},{2,3},{3,4},{4,5},{5,6},{6,7},{7,8},{8,9},{9,10},{10,1... | collective-permute-start | bytes 787208 | tf_op jit(solution)/shard_map/ppermute | solution.py:38
  36.6 49.5 %collective-permute-start.4 = (bf16[1,128,1025]{2,1,0:T(8,128)(2,1)}, bf16[1,128,1025]{2,1,0:T(8,128)(2,1)}, u32[]{:S(2)}, u32[]{:S(2)}) collective-permute-start(bf16[1,128,1025]{2,1,0:T(8,128)(2,1)} %get-tuple-element.32), channel_id=1, source_target_pairs={{0,14},{1,15},{2,0},{3,1},{4,2},{5,3},{6,4},{7,5},{8,6},{9,7},{10,... | collective-permute-start | bytes 787208 | tf_op jit(solution)/shard_map/ppermute | solution.py:38
  38.6 52.3 %collective-permute-start.5 = (bf16[1,128,1025]{2,1,0:T(8,128)(2,1)}, bf16[1,128,1025]{2,1,0:T(8,128)(2,1)}, u32[]{:S(2)}, u32[]{:S(2)}) collective-permute-start(bf16[1,128,1025]{2,1,0:T(8,128)(2,1)} %get-tuple-element.32), channel_id=1, source_target_pairs={{0,2},{1,3},{2,4},{3,5},{4,6},{5,7},{6,8},{7,9},{8,10},{9,11},{10,... | collective-permute-start | bytes 787208 | tf_op jit(solution)/shard_map/ppermute | solution.py:38
  46.4 46.2 %collective-permute-start.6 = (bf16[1,128,1025]{2,1,0:T(8,128)(2,1)}, bf16[1,128,1025]{2,1,0:T(8,128)(2,1)}, u32[]{:S(2)}, u32[]{:S(2)}) collective-permute-start(bf16[1,128,1025]{2,1,0:T(8,128)(2,1)} %get-tuple-element.32), channel_id=1, source_target_pairs={{0,13},{1,14},{2,15},{3,0},{4,1},{5,2},{6,3},{7,4},{8,5},{9,6},{10... | collective-permute-start | bytes 787208 | tf_op jit(solution)/shard_map/ppermute | solution.py:38
  48.7 45.6 %collective-permute-start.7 = (bf16[1,128,1025]{2,1,0:T(8,128)(2,1)}, bf16[1,128,1025]{2,1,0:T(8,128)(2,1)S(1)}, u32[]{:S(2)}, u32[]{:S(2)}) collective-permute-start(bf16[1,128,1025]{2,1,0:T(8,128)(2,1)} %get-tuple-element.32), channel_id=1, source_target_pairs={{0,3},{1,4},{2,5},{3,6},{4,7},{5,8},{6,9},{7,10},{8,11},{9,12},{10... | collective-permute-start | bytes 787208 | tf_op jit(solution)/shard_map/ppermute | solution.py:38
  59.3 35.8 %collective-permute-start.8 = (bf16[1,128,1025]{2,1,0:T(8,128)(2,1)}, bf16[1,128,1025]{2,1,0:T(8,128)(2,1)S(1)}, u32[]{:S(2)}, u32[]{:S(2)}) collective-permute-start(bf16[1,128,1025]{2,1,0:T(8,128)(2,1)} %get-tuple-element.32), channel_id=1, source_target_pairs={{0,12},{1,13},{2,14},{3,15},{4,0},{5,1},{6,2},{7,3},{8,4},{9,5},{1... | collective-permute-start | bytes 787208 | tf_op jit(solution)/shard_map/ppermute | solution.py:38
  86.1 9.7 %collective-permute-start.9 = (bf16[1,128,1025]{2,1,0:T(8,128)(2,1)}, bf16[1,128,1025]{2,1,0:T(8,128)(2,1)S(1)}, u32[]{:S(2)}, u32[]{:S(2)}) collective-permute-start(bf16[1,128,1025]{2,1,0:T(8,128)(2,1)} %get-tuple-element.32), channel_id=1, source_target_pairs={{0,4},{1,5},{2,6},{3,7},{4,8},{5,9},{6,10},{7,11},{8,12},{9,13},{1... | collective-permute-start | bytes 787208 | tf_op jit(solution)/shard_map/ppermute | solution.py:38
  110.9 23.3 %collective-permute-start.10 = (bf16[1,128,16,64]{1,3,2,0:T(8,128)(2,1)S(1)}, bf16[1,128,16,64]{1,3,2,0:T(8,128)(2,1)S(1)}, u32[]{:S(2)}, u32[]{:S(2)}) collective-permute-start(bf16[1,128,16,64]{1,3,2,0:T(8,128)(2,1)S(1)} %pad_maximum_fusion.2), channel_id=1, source_target_pairs={{0,1},{1,2},{2,3},{3,4},{4,5},{5,6},{6,7},{7,8},{8,9},{9,10},{10,1... | collective-permute-start | bytes 786440 | tf_op jit(solution)/shard_map/ppermute | solution.py:38
  118.5 34.0 %copy-start.6 = (bf16[1,128,512]{2,1,0:T(8,128)(2,1)S(1)}, bf16[1,128,512]{2,1,0:T(8,128)(2,1)}, u32[]{:S(2)}) copy-start(bf16[1,128,512]{2,1,0:T(8,128)(2,1)} %param.13) | copy-start | bytes 393220
  118.5 21.1 %collective-permute-start.11 = (bf16[1,128,16,64]{1,3,2,0:T(8,128)(2,1)S(1)}, bf16[1,128,16,64]{1,3,2,0:T(8,128)(2,1)S(1)}, u32[]{:S(2)}, u32[]{:S(2)}) collective-permute-start(bf16[1,128,16,64]{1,3,2,0:T(8,128)(2,1)S(1)} %pad_maximum_fusion.3), channel_id=1, source_target_pairs={{0,15},{1,0},{2,1},{3,2},{4,3},{5,4},{6,5},{7,6},{8,7},{9,8},{10,9... | collective-permute-start | bytes 786440 | tf_op jit(solution)/shard_map/ppermute | solution.py:38
  120.6 30.0 %collective-permute-start.12 = (bf16[1,128,16,64]{1,3,2,0:T(8,128)(2,1)S(1)}, bf16[1,128,16,64]{1,3,2,0:T(8,128)(2,1)S(1)}, u32[]{:S(2)}, u32[]{:S(2)}) collective-permute-start(bf16[1,128,16,64]{1,3,2,0:T(8,128)(2,1)S(1)} %pad_maximum_fusion.4), channel_id=1, source_target_pairs={{0,2},{1,3},{2,4},{3,5},{4,6},{5,7},{6,8},{7,9},{8,10},{9,11},{10,... | collective-permute-start | bytes 786440 | tf_op jit(solution)/shard_map/ppermute | solution.py:38
  126.1 27.1 %collective-permute-start.13 = (bf16[1,128,16,64]{1,3,2,0:T(8,128)(2,1)S(1)}, bf16[1,128,16,64]{1,3,2,0:T(8,128)(2,1)S(1)}, u32[]{:S(2)}, u32[]{:S(2)}) collective-permute-start(bf16[1,128,16,64]{1,3,2,0:T(8,128)(2,1)S(1)} %pad_maximum_fusion.5), channel_id=1, source_target_pairs={{0,14},{1,15},{2,0},{3,1},{4,2},{5,3},{6,4},{7,5},{8,6},{9,7},{10,... | collective-permute-start | bytes 786440 | tf_op jit(solution)/shard_map/ppermute | solution.py:38
  131.3 21.5 %copy-start.3 = (bf16[4,512,512]{2,1,0:T(8,128)(2,1)S(1)}, bf16[4,512,512]{2,1,0:T(8,128)(2,1)}, u32[]{:S(2)}) copy-start(bf16[4,512,512]{2,1,0:T(8,128)(2,1)} %param.19) | copy-start | bytes 6291460
  131.3 32.9 %collective-permute-start.14 = (bf16[1,128,16,64]{1,3,2,0:T(8,128)(2,1)S(1)}, bf16[1,128,16,64]{1,3,2,0:T(8,128)(2,1)S(1)}, u32[]{:S(2)}, u32[]{:S(2)}) collective-permute-start(bf16[1,128,16,64]{1,3,2,0:T(8,128)(2,1)S(1)} %pad_maximum_fusion.6), channel_id=1, source_target_pairs={{0,3},{1,4},{2,5},{3,6},{4,7},{5,8},{6,9},{7,10},{8,11},{9,12},{10... | collective-permute-start | bytes 786440 | tf_op jit(solution)/shard_map/ppermute | solution.py:38
  134.3 30.1 %collective-permute-start.15 = (bf16[1,128,16,64]{1,3,2,0:T(8,128)(2,1)S(1)}, bf16[1,128,16,64]{1,3,2,0:T(8,128)(2,1)S(1)}, u32[]{:S(2)}, u32[]{:S(2)}) collective-permute-start(bf16[1,128,16,64]{1,3,2,0:T(8,128)(2,1)S(1)} %pad_maximum_fusion.7), channel_id=1, source_target_pairs={{0,13},{1,14},{2,15},{3,0},{4,1},{5,2},{6,3},{7,4},{8,5},{9,6},{10... | collective-permute-start | bytes 786440 | tf_op jit(solution)/shard_map/ppermute | solution.py:38
  139.6 24.8 %collective-permute-start.16 = (bf16[1,128,16,64]{1,3,2,0:T(8,128)(2,1)S(1)}, bf16[1,128,16,64]{1,3,2,0:T(8,128)(2,1)S(1)}, u32[]{:S(2)}, u32[]{:S(2)}) collective-permute-start(bf16[1,128,16,64]{1,3,2,0:T(8,128)(2,1)S(1)} %pad_maximum_fusion.8), channel_id=1, source_target_pairs={{0,4},{1,5},{2,6},{3,7},{4,8},{5,9},{6,10},{7,11},{8,12},{9,13},{1... | collective-permute-start | bytes 786440 | tf_op jit(solution)/shard_map/ppermute | solution.py:38
  150.6 13.9 %collective-permute-start.17 = (bf16[1,128,16,64]{1,3,2,0:T(8,128)(2,1)S(1)}, bf16[1,128,16,64]{1,3,2,0:T(8,128)(2,1)S(1)}, u32[]{:S(2)}, u32[]{:S(2)}) collective-permute-start(bf16[1,128,16,64]{1,3,2,0:T(8,128)(2,1)S(1)} %pad_maximum_fusion.9), channel_id=1, source_target_pairs={{0,12},{1,13},{2,14},{3,15},{4,0},{5,1},{6,2},{7,3},{8,4},{9,5},{1... | collective-permute-start | bytes 786440 | tf_op jit(solution)/shard_map/ppermute | solution.py:38
  166.2 5.0 %copy-start.15 = (f32[1,64,1]{2,1,0:T(8,128)S(1)}, f32[1,64,1]{2,1,0:T(8,128)}, u32[]{:S(2)}) copy-start(f32[1,64,1]{2,1,0:T(8,128)} %copy-done.14) | copy-start | bytes 772
  166.2 5.2 %copy-start.13 = (f32[1,64,1]{2,1,0:T(8,128)S(1)}, f32[1,64,1]{2,1,0:T(8,128)}, u32[]{:S(2)}) copy-start(f32[1,64,1]{2,1,0:T(8,128)} %copy-done.12) | copy-start | bytes 772
  171.8 22.8 %collective-permute-start.19 = (bf16[1,64,1]{2,1,0:T(8,128)(2,1)}, bf16[1,64,1]{2,1,0:T(8,128)(2,1)S(1)}, u32[]{:S(2)}, u32[]{:S(2)}) collective-permute-start(bf16[1,64,1]{2,1,0:T(8,128)(2,1)} %get-tuple-element.37), channel_id=1, source_target_pairs={{0,1},{1,2},{2,3},{3,4},{4,5},{5,6},{6,7},{7,8},{8,9},{9,10},{10,1... | collective-permute-start | bytes 392 | tf_op jit(solution)/shard_map/ppermute | solution.py:26
  175.5 19.4 %collective-permute-start.18 = (bf16[1,64,1]{2,1,0:T(8,128)(2,1)}, bf16[1,64,1]{2,1,0:T(8,128)(2,1)S(1)}, u32[]{:S(2)}, u32[]{:S(2)}) collective-permute-start(bf16[1,64,1]{2,1,0:T(8,128)(2,1)} %get-tuple-element.36), channel_id=1, source_target_pairs={{1,0},{2,1},{3,2},{4,3},{5,4},{6,5},{7,6},{8,7},{9,8},{10,9},{11,1... | collective-permute-start | bytes 392 | tf_op jit(solution)/shard_map/ppermute | solution.py:28
  189.7 4.9 %copy-start.9 = (f32[3,64,64]{2,1,0:T(8,128)S(1)}, f32[3,64,64]{2,1,0:T(8,128)}, u32[]{:S(2)}) copy-start(f32[3,64,64]{2,1,0:T(8,128)} %param.16) | copy-start | bytes 147460
  189.7 5.4 %copy-start.4 = (f32[64,64,128]{2,0,1:T(8,128)S(1)}, f32[64,64,128]{2,0,1:T(8,128)}, u32[]{:S(2)}) copy-start(f32[64,64,128]{2,0,1:T(8,128)} %get-tuple-element.41) | copy-start | bytes 6291460
  189.7 5.4 %copy-start.19 = (f32[64]{0:T(128)S(1)}, f32[64]{0:T(128)}, u32[]{:S(2)}) copy-start(f32[64]{0:T(128)} %param.15) | copy-start | bytes 772
  194.6 1.5 copy-start.11
  196.1 2.5 copy-start.7
  196.1 2.5 copy-start.17
  198.8 2.2 copy-start.1

commit v6 on v5

--- a/solution.py
+++ b/solution.py
@@ -191,6 +191,53 @@
     )(current, small_grid)
     return out.reshape(chunk), small_out.reshape(-1)[:size]
 
+def exchange_body(shifts, per_slot, src_ref, out_ref, held, send_sems, recv_sems):
+    place = lax.axis_index("sites")
+    row = lax.axis_index("sims")
+    count = lax.axis_size("sites")
+    targets = [(row, lax.rem(place + shift + count, count)) for shift in shifts]
+    barrier = pltpu.get_barrier_semaphore()
+    for device in targets:
+        pl.semaphore_signal(barrier, inc=1, device_id=device, device_id_type=pl.DeviceIdType.MESH)
+    pl.semaphore_wait(barrier, len(targets))
+    copies = []
+    for slot, device in enumerate(targets):
+        copy = pltpu.make_async_remote_copy(
+            src_ref=src_ref.at[slot] if per_slot else src_ref,
+            dst_ref=held.at[slot],
+            send_sem=send_sems.at[slot],
+            recv_sem=recv_sems.at[slot],
+            device_id=device,
+            device_id_type=pl.DeviceIdType.MESH,
+        )
+        copy.start()
+        copies.append(copy)
+    for copy in copies:
+        copy.wait_send()
+    for copy in copies:
+        copy.wait_recv()
+    out_ref[...] = held[...]
+
+
+def exchange(block, shifts, per_slot, collective):
+    slots = len(shifts)
+    shape = block.shape[1:] if per_slot else block.shape
+    return pl.pallas_call(
+        functools.partial(exchange_body, shifts, per_slot),
+        out_shape=jax.ShapeDtypeStruct((slots,) + shape, block.dtype),
+        in_specs=[pl.BlockSpec(memory_space=pltpu.VMEM)],
+        out_specs=pl.BlockSpec(memory_space=pltpu.VMEM),
+        scratch_shapes=[
+            pltpu.VMEM((slots,) + shape, block.dtype),
+            pltpu.SemaphoreType.DMA((slots,)),
+            pltpu.SemaphoreType.DMA((slots,)),
+        ],
+        compiler_params=pltpu.CompilerParams(
+            collective_id=collective, has_side_effects=True, vmem_limit_bytes=32 * 1024 * 1024
+        ),
+    )(block)
+
+
 def per_device(
     genotypes,
     key_prior,
@@ -252,10 +299,12 @@
     packed = jnp.concatenate(
         [keys, values, key_prior[:, :, None]], axis=2
     )
-    gathered = {0: packed}
-    for offset in offsets[1:]:
-        gathered[offset] = from_behind(packed, "sites", -offset)
-    packed_cat = jnp.concatenate([gathered[offset] for offset in offsets], axis=1)
+    lane_pad = -packed.shape[2] % 128
+    packed = jnp.pad(packed, ((0, 0), (0, 0), (0, lane_pad)))
+    arrived = exchange(packed[0], [-offset for offset in offsets[1:]], False, 1)
+    packed_cat = jnp.concatenate([packed[0][None], arrived], axis=0).reshape(
+        1, len(offsets) * local, packed.shape[2]
+    )
     key_cat = split_heads(packed_cat[:, :, :width], heads)
     value_cat = split_heads(packed_cat[:, :, width : 2 * width], heads)
     prior_cat = packed_cat[:, :, 2 * width]
@@ -294,14 +343,13 @@
     )
     key_sum = key_part[:, 0:local]
     value_sum = value_part[:, 0:local]
-    for position, offset in enumerate(offsets[1:], start=1):
-        lower = position * local
-        both = jnp.concatenate(
-            [key_part[:, lower : lower + local], value_part[:, lower : lower + local]], axis=2
-        ).astype(jnp.bfloat16)
-        back = from_behind(both, "sites", offset).astype(jnp.float32)
-        key_sum = key_sum + back[:, :, :heads]
-        value_sum = value_sum + back[:, :, heads:]
+    parts = jnp.concatenate(
+        [key_part[0, local:], value_part[0, local:]], axis=1
+    ).astype(jnp.bfloat16).reshape(len(offsets) - 1, local, 2 * width)
+    back = exchange(parts, list(offsets[1:]), True, 2).astype(jnp.float32)
+    for position in range(len(offsets) - 1):
+        key_sum = key_sum + back[position][None, :, :width].reshape(key_sum.shape)
+        value_sum = value_sum + back[position][None, :, width:].reshape(value_sum.shape)
     grad_keys = key_sum.astype(jnp.bfloat16).reshape(sims, local, width)
     grad_values = value_sum.astype(jnp.bfloat16).reshape(sims, local, width)
     term_query = jnp.einsum("std,ste->de", normed, grad_query, preferred_element_type=jnp.float32)

time: 311 us -> 329 us (1.058)
  Pallas kernels: 102 us -> 195 us
  starting transfers between devices: 118 us -> 25.6 us
  local copies, waits for them, and re-layouts: 36.1 us -> 60.1 us
  waiting for transfers between devices: 15.5 us -> 0.01 us
  matrix products: 20.8 us -> 25.9 us
    ppermute x16 -> x0, starting transfers between devices: 96.3 us -> none  [from_behind(): return lax.ppermute(value, axis, pairs)]
    pallas_call x0 -> x2, Pallas kernels: none -> 85.4 us  [exchange(): pl.pallas_call(functools.partial(exchange_body, shifts, per_slot), out_sh...]
    slice x2 -> x25, local copies, waits for them, and re-layouts: 0.46 us -> 28.8 us  [the longest x16 17.2 us: per_device(): key_sum = key_sum + back[position][None, :, :width].reshape(key_sum.shape)]
    ppermute x16 -> x0, waiting for transfers between devices: 11 us -> none  [from_behind(): return lax.ppermute(value, axis, pairs)]
    pallas_call x1, Pallas kernels: 102 us -> 110 us  [butterfly_kernel(): pl.pallas_call(functools.partial(butterfly_body, order, small_order, step...]
    unnamed x50 -> x75, local copies, waits for them, and re-layouts: 14.6 us -> 7.19 us
    ppermute x2, waiting for transfers between devices: 4.5 us -> 0.01 us  [extended(): lax.ppermute(tail, axis, [(i, (i + 1) % count) for i in range(count)])]
    convert_element_type x0 -> x1, local copies, waits for them, and re-layouts: none -> 3.46 us  [per_device(): parts = jnp.concatenate([key_part[0, local:], value_part[0, local:]], axi...]
  transfers between devices with their start and end apart: 20 -> 4, of which waited for: 2 -> 0; matrix products, arithmetic and copies ran while one was open for 9% -> 5% of each run, Pallas kernels for 0% -> 0%
where the time goes in v6:
time: 329 us; the launch traced here: 322 us
  Pallas kernels  195 us (59%)
  local copies, waits for them, and re-layouts  60.1 us (18%)
  matrix products  25.9 us (8%)
  starting transfers between devices  25.6 us (8%)
  other arithmetic  13.6 us (4%)
    pallas_call x1, Pallas kernels, butterfly_kernel(): pl.pallas_call(functools.partial(butterfly_body, order, small_order, step...  110 us
    pallas_call x2, Pallas kernels, exchange(): pl.pallas_call(functools.partial(exchange_body, shifts, per_slot), out_sh...  85.4 us
    slice x16, local copies, waits for them, and re-layouts, per_device(): key_sum = key_sum + back[position][None, :, :width].reshape(key_sum.shape)  17.2 us
    ppermute x2, starting transfers between devices, extended(): lax.ppermute(head, axis, [((i + 1) % count, i) for i in range(count)])  17 us
    slice x8, local copies, waits for them, and re-layouts, per_device(): back[position][None, :, width:].reshape(value_sum.shape)  11.6 us
    another operation x2, local copies, waits for them, and re-layouts, butterfly_sum(): cells = flat.reshape((2,) * total_bits + (chunk // LANES, LANES))  9.91 us
    ppermute x2, starting transfers between devices, extended(): lax.ppermute(tail, axis, [(i, (i + 1) % count) for i in range(count)])  8.63 us
    unnamed x75, local copies, waits for them, and re-layouts  7.19 us
  transfers between devices with their start and end apart: 4, of which 0 were waited for; matrix products, arithmetic and copies ran while one was open for 5% of the time, Pallas kernels for 0%

profile of v6, /device:TPU:6, one launch (start us, length us, event | category | flops | bytes accessed | tf_op | source)
XLA Modules:
  0.0 322.4 jit_solution(16984199837033265519)
XLA Ops:
  0.6 1.0 convert_element_type.93
  1.9 4.5 %fusion.16 = (f32[64,128]{1,0:T(8,128)S(1)}, f32[64,64,128]{2,0,1:T(8,128)}) fusion(f32[64]{0:T(128)} %param.15, f32[64,128,4]{1,2,0:T(4,128)S(1)} %copy.44, f32[4,64]{1,0:T(4,128)} %param.14), kind=kOutput, calls=%fused_computation.29 | convolution fusion | flops 28303360 | bytes 2262272 | tf_op jit(solution)/shard_map/shtk,kc->shct/dot_general | solution.py:265
  6.5 6.1 %collective-permute-start = (f32[1,64,1]{2,1,0:T(8,128)S(1)}, f32[1,64,1]{2,1,0:T(8,128)S(1)}, u32[]{:S(2)}, u32[]{:S(2)}) collective-permute-start(f32[1,64,1]{2,1,0:T(8,128)S(1)} %get-tuple-element.38), channel_id=1, source_target_pairs={{0,1},{1,2},{2,3},{3,4},{4,5},{5,6},{6,7},{7,8},{8,9},{9,10},{10,1... | collective-permute-start | bytes 776 | tf_op jit(solution)/shard_map/ppermute | solution.py:26
  12.6 7.2 %collective-permute-start.1 = (f32[1,64,1]{2,1,0:T(8,128)S(1)}, f32[1,64,1]{2,1,0:T(8,128)S(1)}, u32[]{:S(2)}, u32[]{:S(2)}) collective-permute-start(f32[1,64,1]{2,1,0:T(8,128)S(1)} %get-tuple-element.39), channel_id=1, source_target_pairs={{1,0},{2,1},{3,2},{4,3},{5,4},{6,5},{7,6},{8,7},{9,8},{10,9},{11,1... | collective-permute-start | bytes 776 | tf_op jit(solution)/shard_map/ppermute | solution.py:28
  21.2 1.1 fusion.37
  24.8 0.9 convolution_convert_fusion.1
  25.8 45.6 %shard_map.145 = bf16[8,128,1152]{2,1,0:T(8,128)(2,1)S(1)} custom-call(bf16[128,1152]{1,0:T(8,128)(2,1)S(1)} %fusion.177.src_ref), custom_call_target="tpu_custom_call" | custom-call | tf_op jit(solution)/shard_map/pallas_call | solution.py:225
  71.7 1.2 fusion.135
  73.2 0.7 copy.46
  73.9 1.7 copy.50
  75.6 0.8 fusion.5
  76.5 1.8 fusion.146
  78.9 1.7 bitcast_convert_fusion
  81.1 1.3 fusion.8
  82.4 1.0 convolution_convert_fusion.5
  83.9 2.5 fusion.43
  86.3 1.3 convolution_bitcast_fusion.5
  88.2 2.0 copy.80
  90.2 3.5 %copy.51.src_ref = bf16[8,128,1024]{2,1,0:T(8,128)(2,1)S(1)} copy(bf16[8,128,1024]{1,0,2:T(8,128)(2,1)} %bitcast.299) | data formatting | bytes 4194304 | tf_op jit(solution)/shard_map/convert_element_type | solution.py:348
  93.6 39.8 %shard_map.146 = bf16[8,128,1024]{2,1,0:T(8,128)(2,1)S(1)} custom-call(bf16[8,128,1024]{2,1,0:T(8,128)(2,1)S(1)} %copy.51.src_ref), custom_call_target="tpu_custom_call" | custom-call | tf_op jit(solution)/shard_map/pallas_call | solution.py:225
  133.9 1.6 slice_bitcast_fusion.7
  135.5 0.8 fusion.136
  136.4 1.1 copy.52
  137.4 1.8 copy.60
  139.2 1.9 fusion.143
  141.1 1.8 copy.59
  142.9 1.8 copy.67
  144.7 1.9 fusion.142
  146.6 1.8 copy.58
  148.4 1.8 copy.66
  150.2 0.9 fusion.141
  151.1 1.8 copy.57
  152.9 1.8 copy.65
  154.7 0.8 copy.56
  155.6 0.9 copy.64
  156.5 0.8 copy.55
  157.3 0.8 copy.63
  158.2 0.8 copy.54
  159.0 0.8 copy.62
  159.8 0.9 fusion.137
  160.7 1.8 copy.53
  162.5 1.9 copy.61
  164.4 1.8 fusion.74
  166.7 1.1 fusion.66
  167.8 0.9 multiply_reduce_fusion
  169.3 1.0 convolution_bitcast_fusion.6
  170.3 0.9 fusion.91
  171.2 0.7 fusion.145
  172.5 1.3 convolution_bitcast_fusion.2
  174.6 1.6 copy.81
  176.2 9.8 %collective-permute-start.2 = (bf16[1,64,1]{2,1,0:T(8,128)(2,1)}, bf16[1,64,1]{2,1,0:T(8,128)(2,1)S(1)}, u32[]{:S(2)}, u32[]{:S(2)}) collective-permute-start(bf16[1,64,1]{2,1,0:T(8,128)(2,1)} %get-tuple-element.40), channel_id=1, source_target_pairs={{1,0},{2,1},{3,2},{4,3},{5,4},{6,5},{7,6},{8,7},{9,8},{10,9},{11,1... | collective-permute-start | bytes 392 | tf_op jit(solution)/shard_map/ppermute | solution.py:28
  186.0 2.5 collective-permute-start.3
  188.5 3.9 %pad_maximum_fusion = f32[4,512,512]{2,1,0:T(8,128)} fusion(f32[1,512,512]{2,1,0:T(8,128)} %convolution_bitcast_fusion.2, f32[1,512,512]{2,1,0:T(8,128)S(1)} %convolution_bitcast_fusion.3, f32[1,512,512]{2,1,0:T(8,128)S(1)} %convolution_bitcast_fusion.4, f32[1,512,512]{2,1,0:T(8,128)S(1)} %copy-done.4), kind=kLoop, calls=%fused_computation.10 | loop fusion | flops 3145728 | bytes 8388608 | tf_op jit(solution)/shard_map/stack | solution.py:359
  192.4 5.0 %reshape_reshape.3 = f32[2,2,2,2,2,2,2,2,2,8,256]{10,9,8,7,6,5,4,3,2,1,0:T(8,128)} reshape(f32[4,512,512]{2,1,0:T(8,128)} %pad_maximum_fusion) | data formatting | bytes 8388608 | tf_op jit(solution)/shard_map/reshape;reshape | solution.py:96
  197.4 4.9 %copy.68 = f32[2,2,2,2,2,2,2,2,2,8,256]{10,9,7,8,1,5,2,6,3,0,4:T(8,128)} copy(f32[2,2,2,2,2,2,2,2,2,8,256]{10,9,8,7,6,5,4,3,2,1,0:T(8,128)} %reshape_reshape.3) | data formatting | bytes 8388608 | tf_op jit(solution)/shard_map/reshape;reshape | solution.py:96
  202.8 2.4 fusion.30
  205.2 1.0 fusion.35
  206.5 2.2 copy-done.1
  208.7 109.5 %shard_map.147 = (f32[8,256]{1,0:T(8,128)S(1)}, f32[184,256]{1,0:T(8,128)S(1)}) custom-call(f32[4096,256]{1,0:T(8,128)S(1)} %bitcast.291, f32[184,256]{1,0:T(8,128)S(1)} %reshape.395.small_ref), custom_call_target="tpu_custom_call" | custom-call | tf_op jit(solution)/shard_map/pallas_call | solution.py:170
  318.9 0.6 slice.276
  319.7 0.6 copy.82
  320.3 0.7 slice.233
  321.0 0.7 reshape.399
  321.7 0.7 reshape.398
  (137 shorter events, 10.4 us)
Async XLA Ops:
  0.6 23.1 %copy-start = (f32[64,512]{1,0:T(8,128)S(1)}, f32[64,512]{1,0:T(8,128)}, u32[]{:S(2)}) copy-start(f32[64,512]{1,0:T(8,128)} %param.17) | copy-start | bytes 393220
  1.9 4.6 %copy-start.24 = (f32[64,128,4]{1,2,0:T(4,128)}, f32[64,128,4]{1,2,0:T(4,128)S(1)}, u32[]{:S(2)}) copy-start(f32[64,128,4]{1,2,0:T(4,128)S(1)} %copy.44) | copy-start | bytes 393220
  1.9 18.9 %copy-start.5 = (bf16[4,512,512]{2,1,0:T(8,128)(2,1)S(1)}, bf16[4,512,512]{2,1,0:T(8,128)(2,1)}, u32[]{:S(2)}) copy-start(bf16[4,512,512]{2,1,0:T(8,128)(2,1)} %param.19) | copy-start | bytes 6291460
  1.9 18.9 %copy-start.19 = (bf16[1,128,512]{2,1,0:T(8,128)(2,1)S(1)}, bf16[1,128,512]{2,1,0:T(8,128)(2,1)}, u32[]{:S(2)}) copy-start(bf16[1,128,512]{2,1,0:T(8,128)(2,1)} %param.13) | copy-start | bytes 393220
  1.9 20.4 %copy-start.22 = (f32[3,64,64]{2,1,0:T(8,128)S(1)}, f32[3,64,64]{2,1,0:T(8,128)}, u32[]{:S(2)}) copy-start(f32[3,64,64]{2,1,0:T(8,128)} %param.16) | copy-start | bytes 147460
  1.9 20.6 %copy-start.33 = (bf16[1,128]{1,0:T(2,128)(2,1)S(1)}, bf16[1,128]{1,0:T(2,128)(2,1)}, u32[]{:S(2)}) copy-start(bf16[1,128]{1,0:T(2,128)(2,1)} %param.11) | copy-start | bytes 772
  6.5 17.8 %copy-start.31 = (f32[512]{0:T(512)S(1)}, f32[512]{0:T(512)}, u32[]{:S(2)}) copy-start(f32[512]{0:T(512)} %param.18) | copy-start | bytes 6148
  6.5 16.9 %collective-permute-start = (f32[1,64,1]{2,1,0:T(8,128)S(1)}, f32[1,64,1]{2,1,0:T(8,128)S(1)}, u32[]{:S(2)}, u32[]{:S(2)}) collective-permute-start(f32[1,64,1]{2,1,0:T(8,128)S(1)} %get-tuple-element.38), channel_id=1, source_target_pairs={{0,1},{1,2},{2,3},{3,4},{4,5},{5,6},{6,7},{7,8},{8,9},{9,10},{10,1... | collective-permute-start | bytes 776 | tf_op jit(solution)/shard_map/ppermute | solution.py:26
  12.6 10.2 %collective-permute-start.1 = (f32[1,64,1]{2,1,0:T(8,128)S(1)}, f32[1,64,1]{2,1,0:T(8,128)S(1)}, u32[]{:S(2)}, u32[]{:S(2)}) collective-permute-start(f32[1,64,1]{2,1,0:T(8,128)S(1)} %get-tuple-element.39), channel_id=1, source_target_pairs={{1,0},{2,1},{3,2},{4,3},{5,4},{6,5},{7,6},{8,7},{9,8},{10,9},{11,1... | collective-permute-start | bytes 776 | tf_op jit(solution)/shard_map/ppermute | solution.py:28
  22.8 0.6 copy-start.29
  23.4 2.3 copy-start.27
  71.7 1.2 copy-start.26
  75.6 0.9 copy-start.17
  81.0 6.8 %copy-start.2 = (f32[1,1152,8,64]{1,3,2,0:T(8,128)}, f32[1,1152,8,64]{1,3,2,0:T(8,128)S(1)}, u32[]{:S(2)}) copy-start(f32[1,1152,8,64]{1,3,2,0:T(8,128)S(1)} %convolution_bitcast_fusion) | copy-start | bytes 7077892
  83.9 3.9 %copy-start.3 = (f32[1,1152,8,64]{1,3,2,0:T(8,128)}, f32[1,1152,8,64]{1,3,2,0:T(8,128)S(1)}, u32[]{:S(2)}) copy-start(f32[1,1152,8,64]{1,3,2,0:T(8,128)S(1)} %convolution_bitcast_fusion.1) | copy-start | bytes 7077892
  159.8 6.4 %copy-start.6 = (bf16[4,512,512]{2,1,0:T(8,128)(2,1)S(1)}, bf16[4,512,512]{2,1,0:T(8,128)(2,1)}, u32[]{:S(2)}) copy-start(bf16[4,512,512]{2,1,0:T(8,128)(2,1)} %param.19) | copy-start | bytes 6291460
  162.5 4.1 %copy-start.8 = (f32[128,512]{0,1:T(8,128)S(1)}, f32[128,512]{0,1:T(8,128)}, u32[]{:S(2)}) copy-start(f32[128,512]{0,1:T(8,128)} %copy.60) | copy-start | bytes 786436
  162.5 4.1 %copy-start.9 = (f32[128,512]{0,1:T(8,128)S(1)}, f32[128,512]{0,1:T(8,128)}, u32[]{:S(2)}) copy-start(f32[128,512]{0,1:T(8,128)} %copy.67) | copy-start | bytes 786436
  164.4 1.9 copy-start.16
  164.4 2.2 copy-start.10
  164.4 2.2 copy-start.11
  164.4 2.2 copy-start.12
  164.4 2.2 copy-start.13
  164.4 2.2 copy-start.14
  164.4 2.2 copy-start.15
  166.6 2.2 copy-start.20
  168.7 3.8 %copy-start.18 = (bf16[1,128,8,64]{1,3,2,0:T(8,128)(2,1)S(1)}, bf16[1,128,8,64]{1,3,2,0:T(8,128)(2,1)}, u32[]{:S(2)}) copy-start(bf16[1,128,8,64]{1,3,2,0:T(8,128)(2,1)} %get-tuple-element.50) | copy-start | bytes 393220
  170.2 3.7 %copy-start.30 = (f32[1,64,1]{2,1,0:T(8,128)S(1)}, f32[1,64,1]{2,1,0:T(8,128)}, u32[]{:S(2)}) copy-start(f32[1,64,1]{2,1,0:T(8,128)} %copy-done.29) | copy-start | bytes 772
  171.8 2.4 copy-start.28
  172.2 16.3 %copy-start.4 = (f32[1,512,512]{2,1,0:T(8,128)S(1)}, f32[1,512,512]{2,1,0:T(8,128)}, u32[]{:S(2)}) copy-start(f32[1,512,512]{2,1,0:T(8,128)} %convolution_bitcast_fusion.5) | copy-start | bytes 3145732
  176.2 26.4 %collective-permute-start.2 = (bf16[1,64,1]{2,1,0:T(8,128)(2,1)}, bf16[1,64,1]{2,1,0:T(8,128)(2,1)S(1)}, u32[]{:S(2)}, u32[]{:S(2)}) collective-permute-start(bf16[1,64,1]{2,1,0:T(8,128)(2,1)} %get-tuple-element.40), channel_id=1, source_target_pairs={{1,0},{2,1},{3,2},{4,3},{5,4},{6,5},{7,6},{8,7},{9,8},{10,9},{11,1... | collective-permute-start | bytes 392 | tf_op jit(solution)/shard_map/ppermute | solution.py:28
  186.0 16.4 %collective-permute-start.3 = (bf16[1,64,1]{2,1,0:T(8,128)(2,1)}, bf16[1,64,1]{2,1,0:T(8,128)(2,1)S(1)}, u32[]{:S(2)}, u32[]{:S(2)}) collective-permute-start(bf16[1,64,1]{2,1,0:T(8,128)(2,1)} %get-tuple-element.41), channel_id=1, source_target_pairs={{0,1},{1,2},{2,3},{3,4},{4,5},{5,6},{6,7},{7,8},{8,9},{9,10},{10,1... | collective-permute-start | bytes 392 | tf_op jit(solution)/shard_map/ppermute | solution.py:26
  197.4 4.9 %copy-start.23 = (f32[3,64,64]{2,1,0:T(8,128)S(1)}, f32[3,64,64]{2,1,0:T(8,128)}, u32[]{:S(2)}) copy-start(f32[3,64,64]{2,1,0:T(8,128)} %param.16) | copy-start | bytes 147460
  197.4 5.4 %copy-start.7 = (f32[64,64,128]{2,0,1:T(8,128)S(1)}, f32[64,64,128]{2,0,1:T(8,128)}, u32[]{:S(2)}) copy-start(f32[64,64,128]{2,0,1:T(8,128)} %get-tuple-element.45) | copy-start | bytes 6291460
  197.4 5.4 %copy-start.25 = (f32[64,128,4]{1,2,0:T(4,128)S(1)}, f32[64,128,4]{1,2,0:T(4,128)}, u32[]{:S(2)}) copy-start(f32[64,128,4]{1,2,0:T(4,128)} %copy-done.24) | copy-start | bytes 393220
  197.4 5.4 %copy-start.34 = (f32[64]{0:T(128)S(1)}, f32[64]{0:T(128)}, u32[]{:S(2)}) copy-start(f32[64]{0:T(128)} %param.15) | copy-start | bytes 772
  205.2 1.1 copy-start.21
  205.2 1.1 copy-start.32
  206.5 2.2 copy-start.1

commit v7 on v6

--- a/solution.py
+++ b/solution.py
@@ -346,10 +346,9 @@
     parts = jnp.concatenate(
         [key_part[0, local:], value_part[0, local:]], axis=1
     ).astype(jnp.bfloat16).reshape(len(offsets) - 1, local, 2 * width)
-    back = exchange(parts, list(offsets[1:]), True, 2).astype(jnp.float32)
-    for position in range(len(offsets) - 1):
-        key_sum = key_sum + back[position][None, :, :width].reshape(key_sum.shape)
-        value_sum = value_sum + back[position][None, :, width:].reshape(value_sum.shape)
+    back = jnp.sum(exchange(parts, list(offsets[1:]), True, 2).astype(jnp.float32), axis=0)
+    key_sum = key_part[0, :local].reshape(local, width) + back[:, :width]
+    value_sum = value_part[0, :local].reshape(local, width) + back[:, width:]
     grad_keys = key_sum.astype(jnp.bfloat16).reshape(sims, local, width)
     grad_values = value_sum.astype(jnp.bfloat16).reshape(sims, local, width)
     term_query = jnp.einsum("std,ste->de", normed, grad_query, preferred_element_type=jnp.float32)

time: 329 us -> 295 us (0.90); the launches traced: 322 us -> 294 us
  local copies, waits for them, and re-layouts: 60.1 us -> 30.7 us
  Pallas kernels: 195 us -> 200 us
  other arithmetic: 13.6 us -> 9.12 us
    slice x24 -> x3, local copies, waits for them, and re-layouts: 28.8 us -> 0.6 us  [the longest x2 0.58 us: per_device(): value_sum = value_part[0, :local].reshape(local, width) + back[:, width:]]
    ppermute x2, starting transfers between devices: 17 us -> 10.6 us  [extended(): lax.ppermute(head, axis, [((i + 1) % count, i) for i in range(count)])]
    ppermute x2, starting transfers between devices: 8.63 us -> 14.9 us  [extended(): lax.ppermute(tail, axis, [(i, (i + 1) % count) for i in range(count)])]
    pallas_call x1, Pallas kernels: 110 us -> 115 us  [butterfly_kernel(): pl.pallas_call(functools.partial(butterfly_body, order, small_order, step...]
    unnamed x75 -> x67, local copies, waits for them, and re-layouts: 7.19 us -> 6.82 us
  transfers between devices with their start and end apart: 4 -> 4, of which waited for: 0 -> 0; matrix products, arithmetic and copies ran while one was open for 5% -> 6% of each run, Pallas kernels for 0% -> 0%
where the time goes in v7:
time: 295 us; the launch traced here: 294 us
  Pallas kernels  200 us (68%)
  local copies, waits for them, and re-layouts  30.7 us (10%)
  matrix products  26.5 us (9%)
  starting transfers between devices  25.5 us (9%)
  other arithmetic  9.12 us (3%)
    pallas_call x1, Pallas kernels, butterfly_kernel(): pl.pallas_call(functools.partial(butterfly_body, order, small_order, step...  115 us
    pallas_call x2, Pallas kernels, exchange(): pl.pallas_call(functools.partial(exchange_body, shifts, per_slot), out_sh...  85.1 us
    ppermute x2, starting transfers between devices, extended(): lax.ppermute(tail, axis, [(i, (i + 1) % count) for i in range(count)])  14.9 us
    ppermute x2, starting transfers between devices, extended(): lax.ppermute(head, axis, [((i + 1) % count, i) for i in range(count)])  10.6 us
    another operation x2, local copies, waits for them, and re-layouts, butterfly_sum(): cells = flat.reshape((2,) * total_bits + (chunk // LANES, LANES))  9.87 us
    unnamed x67, local copies, waits for them, and re-layouts  6.82 us
  transfers between devices with their start and end apart: 4, of which 0 were waited for; matrix products, arithmetic and copies ran while one was open for 6% of the time, Pallas kernels for 0%

profile of v7, /device:TPU:6, one launch (start us, length us, event | category | flops | bytes accessed | tf_op | source)
XLA Modules:
  0.0 294.4 jit_solution(12369915076942388178)
XLA Ops:
  0.6 1.0 convert_element_type.93
  1.9 4.5 %fusion.16 = (f32[64,128]{1,0:T(8,128)S(1)}, f32[64,64,128]{2,0,1:T(8,128)}) fusion(f32[64]{0:T(128)} %param.15, f32[64,128,4]{1,2,0:T(4,128)S(1)} %copy.39, f32[4,64]{1,0:T(4,128)} %param.14), kind=kOutput, calls=%fused_computation.30 | convolution fusion | flops 28303360 | bytes 2262272 | tf_op jit(solution)/shard_map/shtk,kc->shct/dot_general | solution.py:265
  6.6 6.1 %collective-permute-start = (f32[1,64,1]{2,1,0:T(8,128)S(1)}, f32[1,64,1]{2,1,0:T(8,128)S(1)}, u32[]{:S(2)}, u32[]{:S(2)}) collective-permute-start(f32[1,64,1]{2,1,0:T(8,128)S(1)} %get-tuple-element.16), channel_id=1, source_target_pairs={{0,1},{1,2},{2,3},{3,4},{4,5},{5,6},{6,7},{7,8},{8,9},{9,10},{10,1... | collective-permute-start | bytes 776 | tf_op jit(solution)/shard_map/ppermute | solution.py:26
  12.7 7.0 %collective-permute-start.1 = (f32[1,64,1]{2,1,0:T(8,128)S(1)}, f32[1,64,1]{2,1,0:T(8,128)S(1)}, u32[]{:S(2)}, u32[]{:S(2)}) collective-permute-start(f32[1,64,1]{2,1,0:T(8,128)S(1)} %get-tuple-element.17), channel_id=1, source_target_pairs={{1,0},{2,1},{3,2},{4,3},{5,4},{6,5},{7,6},{8,7},{9,8},{10,9},{11,1... | collective-permute-start | bytes 776 | tf_op jit(solution)/shard_map/ppermute | solution.py:28
  20.7 0.3 convolution_convert_fusion
  21.0 1.1 fusion.37
  22.1 0.2 fusion.79
  22.5 0.8 copy.44
  23.3 0.3 fusion.75
  23.6 0.3 fusion.28
  23.8 0.5 multiply_reduce_fusion.2
  24.4 0.6 copy-done.3
  25.2 0.2 fusion.23
  25.4 0.2 fusion.22
  25.6 0.9 convolution_convert_fusion.1
  26.6 45.6 %shard_map.145 = bf16[8,128,1152]{2,1,0:T(8,128)(2,1)S(1)} custom-call(bf16[128,1152]{1,0:T(8,128)(2,1)S(1)} %fusion.155.src_ref), custom_call_target="tpu_custom_call" | custom-call | tf_op jit(solution)/shard_map/pallas_call | solution.py:225
  72.2 0.3 pad_maximum_fusion.1
  72.5 1.2 fusion.121
  74.0 0.9 copy.41
  74.9 1.7 copy.45
  76.6 0.8 fusion.5
  77.5 1.8 fusion.124
  79.3 0.6 fusion.20
  79.9 1.7 bitcast_convert_fusion
  81.6 0.5 convolution_bitcast_fusion
  82.1 1.3 fusion.8
  83.4 1.0 convolution_convert_fusion.5
  84.4 0.5 convolution_bitcast_fusion.1
  85.3 1.3 fusion.43
  87.0 1.9 copy.61
  88.9 3.2 %copy.46.src_ref = bf16[8,128,1024]{2,1,0:T(8,128)(2,1)S(1)} copy(bf16[8,128,1024]{1,0,2:T(8,128)(2,1)} %bitcast.267) | data formatting | bytes 4194304 | tf_op jit(solution)/shard_map/convert_element_type | solution.py:348
  92.2 39.5 %shard_map.146 = bf16[8,128,1024]{2,1,0:T(8,128)(2,1)S(1)} custom-call(bf16[8,128,1024]{2,1,0:T(8,128)(2,1)S(1)} %copy.46.src_ref), custom_call_target="tpu_custom_call" | custom-call | tf_op jit(solution)/shard_map/pallas_call | solution.py:225
  131.7 0.3 convert_reduce_fusion
  132.1 0.6 slice-done
  132.9 1.4 convolution_add_fusion.1
  134.3 2.0 multiply_reduce_fusion
  136.5 0.4 fusion.125
  136.9 1.0 convolution_bitcast_fusion.6
  137.9 1.5 fusion.77
  139.4 0.7 fusion.123
  140.1 0.3 convolution_bitcast_fusion.3
  140.4 0.3 convolution_bitcast_fusion.4
  140.7 0.3 convolution_bitcast_fusion.5
  141.3 0.2 convolution_bitcast_fusion.7
  141.5 0.2 convolution_bitcast_fusion.9
  141.9 0.9 copy.62
  142.8 3.5 %collective-permute-start.2 = (bf16[1,64,1]{2,1,0:T(8,128)(2,1)}, bf16[1,64,1]{2,1,0:T(8,128)(2,1)S(1)}, u32[]{:S(2)}, u32[]{:S(2)}) collective-permute-start(bf16[1,64,1]{2,1,0:T(8,128)(2,1)} %get-tuple-element.18), channel_id=1, source_target_pairs={{1,0},{2,1},{3,2},{4,3},{5,4},{6,5},{7,6},{8,7},{9,8},{10,9},{11,1... | collective-permute-start | bytes 392 | tf_op jit(solution)/shard_map/ppermute | solution.py:28
  146.4 8.9 %collective-permute-start.3 = (bf16[1,64,1]{2,1,0:T(8,128)(2,1)}, bf16[1,64,1]{2,1,0:T(8,128)(2,1)S(1)}, u32[]{:S(2)}, u32[]{:S(2)}) collective-permute-start(bf16[1,64,1]{2,1,0:T(8,128)(2,1)} %get-tuple-element.19), channel_id=1, source_target_pairs={{0,1},{1,2},{2,3},{3,4},{4,5},{5,6},{6,7},{7,8},{8,9},{9,10},{10,1... | collective-permute-start | bytes 392 | tf_op jit(solution)/shard_map/ppermute | solution.py:26
  155.2 1.2 convolution_bitcast_fusion.2
  156.5 2.4 pad_maximum_fusion
  158.9 5.0 %reshape_reshape.3 = f32[2,2,2,2,2,2,2,2,2,8,256]{10,9,8,7,6,5,4,3,2,1,0:T(8,128)} reshape(f32[4,512,512]{2,1,0:T(8,128)} %pad_maximum_fusion) | data formatting | bytes 8388608 | tf_op jit(solution)/shard_map/reshape;reshape | solution.py:96
  163.9 4.9 %copy.49 = f32[2,2,2,2,2,2,2,2,2,8,256]{10,9,7,8,1,5,2,6,3,0,4:T(8,128)} copy(f32[2,2,2,2,2,2,2,2,2,8,256]{10,9,8,7,6,5,4,3,2,1,0:T(8,128)} %reshape_reshape.3) | data formatting | bytes 8388608 | tf_op jit(solution)/shard_map/reshape;reshape | solution.py:96
  168.8 0.2 fusion.73
  169.0 0.2 fusion.26
  169.3 2.4 fusion.30
  171.7 1.0 fusion.35
  173.0 2.2 copy-done.1
  175.2 115.1 %shard_map.147 = (f32[8,256]{1,0:T(8,128)S(1)}, f32[184,256]{1,0:T(8,128)S(1)}) custom-call(f32[4096,256]{1,0:T(8,128)S(1)} %bitcast.259, f32[184,256]{1,0:T(8,128)S(1)} %reshape.389.small_ref), custom_call_target="tpu_custom_call" | custom-call | tf_op jit(solution)/shard_map/pallas_call | solution.py:170
  290.4 0.5 slice.155
  290.9 0.6 slice.158
  291.7 0.6 copy.63
  292.3 0.7 slice.137
  293.0 0.7 reshape.393
  293.6 0.7 reshape.392
  (108 shorter events, 3.2 us)
Async XLA Ops:
  0.6 23.2 %copy-start = (f32[64,512]{1,0:T(8,128)S(1)}, f32[64,512]{1,0:T(8,128)}, u32[]{:S(2)}) copy-start(f32[64,512]{1,0:T(8,128)} %param.17) | copy-start | bytes 393220
  1.9 4.6 %copy-start.19 = (f32[64,128,4]{1,2,0:T(4,128)}, f32[64,128,4]{1,2,0:T(4,128)S(1)}, u32[]{:S(2)}) copy-start(f32[64,128,4]{1,2,0:T(4,128)S(1)} %copy.39) | copy-start | bytes 393220
  1.9 18.8 %copy-start.5 = (bf16[4,512,512]{2,1,0:T(8,128)(2,1)S(1)}, bf16[4,512,512]{2,1,0:T(8,128)(2,1)}, u32[]{:S(2)}) copy-start(bf16[4,512,512]{2,1,0:T(8,128)(2,1)} %param.19) | copy-start | bytes 6291460
  1.9 18.8 %copy-start.11 = (bf16[1,128,512]{2,1,0:T(8,128)(2,1)S(1)}, bf16[1,128,512]{2,1,0:T(8,128)(2,1)}, u32[]{:S(2)}) copy-start(bf16[1,128,512]{2,1,0:T(8,128)(2,1)} %param.13) | copy-start | bytes 393220
  1.9 20.2 %copy-start.15 = (f32[3,64,64]{2,1,0:T(8,128)S(1)}, f32[3,64,64]{2,1,0:T(8,128)}, u32[]{:S(2)}) copy-start(f32[3,64,64]{2,1,0:T(8,128)} %param.16) | copy-start | bytes 147460
  1.9 20.4 %copy-start.29 = (bf16[1,128]{1,0:T(2,128)(2,1)S(1)}, bf16[1,128]{1,0:T(2,128)(2,1)}, u32[]{:S(2)}) copy-start(bf16[1,128]{1,0:T(2,128)(2,1)} %param.11) | copy-start | bytes 772
  6.5 19.2 %copy-start.17 = (f32[64,128]{1,0:T(8,128)}, f32[64,128]{1,0:T(8,128)S(1)}, u32[]{:S(2)}) copy-start(f32[64,128]{1,0:T(8,128)S(1)} %get-tuple-element.22) | copy-start | bytes 98308
  6.5 18.6 %copy-start.27 = (f32[512]{0:T(512)S(1)}, f32[512]{0:T(512)}, u32[]{:S(2)}) copy-start(f32[512]{0:T(512)} %param.18) | copy-start | bytes 6148
  6.5 17.9 %copy-start.7 = (f32[1,64,128]{2,1,0:T(8,128)}, f32[1,64,128]{2,1,0:T(8,128)S(1)}, u32[]{:S(2)}) copy-start(f32[1,64,128]{2,1,0:T(8,128)S(1)} %multiply_bitcast_fusion) | copy-start | bytes 98308
  6.6 17.0 %collective-permute-start = (f32[1,64,1]{2,1,0:T(8,128)S(1)}, f32[1,64,1]{2,1,0:T(8,128)S(1)}, u32[]{:S(2)}, u32[]{:S(2)}) collective-permute-start(f32[1,64,1]{2,1,0:T(8,128)S(1)} %get-tuple-element.16), channel_id=1, source_target_pairs={{0,1},{1,2},{2,3},{3,4},{4,5},{5,6},{6,7},{7,8},{8,9},{9,10},{10,1... | collective-permute-start | bytes 776 | tf_op jit(solution)/shard_map/ppermute | solution.py:26
  12.7 10.6 %collective-permute-start.1 = (f32[1,64,1]{2,1,0:T(8,128)S(1)}, f32[1,64,1]{2,1,0:T(8,128)S(1)}, u32[]{:S(2)}, u32[]{:S(2)}) collective-permute-start(f32[1,64,1]{2,1,0:T(8,128)S(1)} %get-tuple-element.17), channel_id=1, source_target_pairs={{1,0},{2,1},{3,2},{4,3},{5,4},{6,5},{7,6},{8,7},{9,8},{10,9},{11,1... | collective-permute-start | bytes 776 | tf_op jit(solution)/shard_map/ppermute | solution.py:28
  23.3 3.3 %copy-start.25 = (f32[1,64,1]{2,1,0:T(8,128)}, f32[1,64,1]{2,1,0:T(8,128)S(1)}, u32[]{:S(2)}) copy-start(f32[1,64,1]{2,1,0:T(8,128)S(1)} %collective-permute-done.1) | copy-start | bytes 772
  23.5 3.1 %copy-start.23 = (f32[1,64,1]{2,1,0:T(8,128)}, f32[1,64,1]{2,1,0:T(8,128)S(1)}, u32[]{:S(2)}) copy-start(f32[1,64,1]{2,1,0:T(8,128)S(1)} %collective-permute-done) | copy-start | bytes 772
  23.8 0.6 copy-start.13
  24.4 0.7 copy-start.3
  72.5 1.2 copy-start.22
  76.6 0.9 copy-start.10
  79.9 1.7 copy-start.9
  82.1 3.0 %copy-start.2 = (f32[1,1152,8,64]{1,3,2,0:T(8,128)}, f32[1,1152,8,64]{1,3,2,0:T(8,128)S(1)}, u32[]{:S(2)}) copy-start(f32[1,1152,8,64]{1,3,2,0:T(8,128)S(1)} %convolution_bitcast_fusion) | copy-start | bytes 7077892
  131.7 1.0 slice-start
  132.1 2.2 copy-start.4
  132.8 3.5 %copy-start.12 = (bf16[1,128,512]{2,1,0:T(8,128)(2,1)S(1)}, bf16[1,128,512]{2,1,0:T(8,128)(2,1)}, u32[]{:S(2)}) copy-start(bf16[1,128,512]{2,1,0:T(8,128)(2,1)} %param.13) | copy-start | bytes 393220
  132.9 3.6 %copy-start.14 = (f32[1,64,128]{2,1,0:T(8,128)S(1)}, f32[1,64,128]{2,1,0:T(8,128)}, u32[]{:S(2)}) copy-start(f32[1,64,128]{2,1,0:T(8,128)} %copy-done.13) | copy-start | bytes 98308
  137.9 3.2 %copy-start.18 = (f32[64,128]{1,0:T(8,128)S(1)}, f32[64,128]{1,0:T(8,128)}, u32[]{:S(2)}) copy-start(f32[64,128]{1,0:T(8,128)} %copy-done.17) | copy-start | bytes 98308
  137.9 3.4 %copy-start.8 = (f32[1,64,128]{2,1,0:T(8,128)S(1)}, f32[1,64,128]{2,1,0:T(8,128)}, u32[]{:S(2)}) copy-start(f32[1,64,128]{2,1,0:T(8,128)} %copy-done.7) | copy-start | bytes 98308
  137.9 3.4 %copy-start.26 = (f32[1,64,1]{2,1,0:T(8,128)S(1)}, f32[1,64,1]{2,1,0:T(8,128)}, u32[]{:S(2)}) copy-start(f32[1,64,1]{2,1,0:T(8,128)} %copy-done.25) | copy-start | bytes 772
  140.1 1.4 copy-start.24
  142.8 26.2 %collective-permute-start.2 = (bf16[1,64,1]{2,1,0:T(8,128)(2,1)}, bf16[1,64,1]{2,1,0:T(8,128)(2,1)S(1)}, u32[]{:S(2)}, u32[]{:S(2)}) collective-permute-start(bf16[1,64,1]{2,1,0:T(8,128)(2,1)} %get-tuple-element.18), channel_id=1, source_target_pairs={{1,0},{2,1},{3,2},{4,3},{5,4},{6,5},{7,6},{8,7},{9,8},{10,9},{11,1... | collective-permute-start | bytes 392 | tf_op jit(solution)/shard_map/ppermute | solution.py:28
  146.4 22.4 %collective-permute-start.3 = (bf16[1,64,1]{2,1,0:T(8,128)(2,1)}, bf16[1,64,1]{2,1,0:T(8,128)(2,1)S(1)}, u32[]{:S(2)}, u32[]{:S(2)}) collective-permute-start(bf16[1,64,1]{2,1,0:T(8,128)(2,1)} %get-tuple-element.19), channel_id=1, source_target_pairs={{0,1},{1,2},{2,3},{3,4},{4,5},{5,6},{6,7},{7,8},{8,9},{9,10},{10,1... | collective-permute-start | bytes 392 | tf_op jit(solution)/shard_map/ppermute | solution.py:26
  163.9 4.9 %copy-start.16 = (f32[3,64,64]{2,1,0:T(8,128)S(1)}, f32[3,64,64]{2,1,0:T(8,128)}, u32[]{:S(2)}) copy-start(f32[3,64,64]{2,1,0:T(8,128)} %param.16) | copy-start | bytes 147460
  163.9 5.2 %copy-start.21 = (f32[128,64]{0,1:T(8,128)S(1)}, f32[128,64]{0,1:T(8,128)}, u32[]{:S(2)}) copy-start(f32[128,64]{0,1:T(8,128)} %fusion.77) | copy-start | bytes 98308
  163.9 5.4 %copy-start.6 = (f32[64,64,128]{2,0,1:T(8,128)S(1)}, f32[64,64,128]{2,0,1:T(8,128)}, u32[]{:S(2)}) copy-start(f32[64,64,128]{2,0,1:T(8,128)} %get-tuple-element.23) | copy-start | bytes 6291460
  163.9 5.4 %copy-start.20 = (f32[64,128,4]{1,2,0:T(4,128)S(1)}, f32[64,128,4]{1,2,0:T(4,128)}, u32[]{:S(2)}) copy-start(f32[64,128,4]{1,2,0:T(4,128)} %copy-done.19) | copy-start | bytes 393220
  163.9 5.4 %copy-start.30 = (f32[64]{0:T(128)S(1)}, f32[64]{0:T(128)}, u32[]{:S(2)}) copy-start(f32[64]{0:T(128)} %param.15) | copy-start | bytes 772
  171.7 1.1 copy-start.28
  173.0 2.2 copy-start.1

commit v8 on v7

--- a/solution.py
+++ b/solution.py
@@ -285,29 +285,26 @@
     query = jnp.einsum(
         "std,de->ste", normed, attn_weight[0], preferred_element_type=jnp.float32
     ).astype(jnp.bfloat16)
-    keys = jnp.einsum(
-        "std,de->ste", normed, attn_weight[1], preferred_element_type=jnp.float32
-    ).astype(jnp.bfloat16)
-    values = jnp.einsum(
-        "std,de->ste", normed, attn_weight[2], preferred_element_type=jnp.float32
-    ).astype(jnp.bfloat16)
     query_heads = split_heads(query, heads)
-    key_heads = split_heads(keys, heads)
-    value_heads = split_heads(values, heads)
     reach_blocks = -(-BAND // local)
     offsets = block_offsets(count, reach_blocks)
-    packed = jnp.concatenate(
-        [keys, values, key_prior[:, :, None]], axis=2
-    )
+    packed = jnp.concatenate([normed, key_prior[:, :, None]], axis=2)
     lane_pad = -packed.shape[2] % 128
     packed = jnp.pad(packed, ((0, 0), (0, 0), (0, lane_pad)))
     arrived = exchange(packed[0], [-offset for offset in offsets[1:]], False, 1)
     packed_cat = jnp.concatenate([packed[0][None], arrived], axis=0).reshape(
         1, len(offsets) * local, packed.shape[2]
     )
-    key_cat = split_heads(packed_cat[:, :, :width], heads)
-    value_cat = split_heads(packed_cat[:, :, width : 2 * width], heads)
-    prior_cat = packed_cat[:, :, 2 * width]
+    normed_cat = packed_cat[:, :, :width]
+    keys_cat = jnp.einsum(
+        "std,de->ste", normed_cat, attn_weight[1], preferred_element_type=jnp.float32
+    ).astype(jnp.bfloat16)
+    values_cat = jnp.einsum(
+        "std,de->ste", normed_cat, attn_weight[2], preferred_element_type=jnp.float32
+    ).astype(jnp.bfloat16)
+    key_cat = split_heads(keys_cat, heads)
+    value_cat = split_heads(values_cat, heads)
+    prior_cat = packed_cat[:, :, width]
     key_places = jnp.concatenate([(place + offset) % count * local + ordinal for offset in offsets])
     query_places = place * local + ordinal
     scores, inside = band_scores(

time: 295 us -> 274 us (0.929)
  the two profiles are of different devices: /device:TPU:6 before, /device:TPU:59 now
where the time goes in v8:
time: 274 us; the launch traced here: 273 us
  Pallas kernels  188 us (69%)
  matrix products  28.5 us (10%)
  local copies, waits for them, and re-layouts  26.9 us (10%)
  starting transfers between devices  18.7 us (7%)
  other arithmetic  8.43 us (3%)
    pallas_call x1, Pallas kernels, butterfly_kernel(): pl.pallas_call(functools.partial(butterfly_body, order, small_order, step...  123 us
    pallas_call x2, Pallas kernels, exchange(): pl.pallas_call(functools.partial(exchange_body, shifts, per_slot), out_sh...  64.7 us
    another operation x2, local copies, waits for them, and re-layouts, butterfly_sum(): cells = flat.reshape((2,) * total_bits + (chunk // LANES, LANES))  9.84 us
    ppermute x2, starting transfers between devices, extended(): lax.ppermute(head, axis, [((i + 1) % count, i) for i in range(count)])  9.76 us
    ppermute x2, starting transfers between devices, extended(): lax.ppermute(tail, axis, [(i, (i + 1) % count) for i in range(count)])  8.96 us
    unnamed x55, local copies, waits for them, and re-layouts  6.71 us
  transfers between devices with their start and end apart: 4, of which 0 were waited for; matrix products, arithmetic and copies ran while one was open for 6% of the time, Pallas kernels for 0%

profile of v8, /device:TPU:59, one launch (start us, length us, event | category | flops | bytes accessed | tf_op | source)
XLA Modules:
  0.0 272.7 jit_solution(6150741257257863590)
XLA Ops:
  0.6 1.0 convert_element_type.91
  1.9 4.5 %fusion.16 = (f32[64,128]{1,0:T(8,128)S(1)}, f32[64,64,128]{2,0,1:T(8,128)}) fusion(f32[64]{0:T(128)} %param.15, f32[64,128,4]{1,2,0:T(4,128)S(1)} %copy.35, f32[4,64]{1,0:T(4,128)} %param.14), kind=kOutput, calls=%fused_computation.31 | convolution fusion | flops 28303360 | bytes 2262272 | tf_op jit(solution)/shard_map/shtk,kc->shct/dot_general | solution.py:265
  6.5 5.8 %collective-permute-start = (f32[1,64,1]{2,1,0:T(8,128)S(1)}, f32[1,64,1]{2,1,0:T(8,128)S(1)}, u32[]{:S(2)}, u32[]{:S(2)}) collective-permute-start(f32[1,64,1]{2,1,0:T(8,128)S(1)} %get-tuple-element.16), channel_id=1, source_target_pairs={{0,1},{1,2},{2,3},{3,4},{4,5},{5,6},{6,7},{7,8},{8,9},{9,10},{10,1... | collective-permute-start | bytes 776 | tf_op jit(solution)/shard_map/ppermute | solution.py:26
  12.3 6.7 %collective-permute-start.1 = (f32[1,64,1]{2,1,0:T(8,128)S(1)}, f32[1,64,1]{2,1,0:T(8,128)S(1)}, u32[]{:S(2)}, u32[]{:S(2)}) collective-permute-start(f32[1,64,1]{2,1,0:T(8,128)S(1)} %get-tuple-element.17), channel_id=1, source_target_pairs={{1,0},{2,1},{3,2},{4,3},{5,4},{6,5},{7,6},{8,7},{9,8},{10,9},{11,1... | collective-permute-start | bytes 776 | tf_op jit(solution)/shard_map/ppermute | solution.py:28
  20.1 0.3 convolution_convert_fusion.2
  20.4 0.4 fusion.35
  20.9 0.2 fusion.75
  21.4 0.3 fusion.71
  21.7 0.3 fusion.26
  22.0 0.5 multiply_reduce_fusion.2
  22.8 29.0 %shard_map.145 = bf16[8,128,640]{2,1,0:T(8,128)(2,1)S(1)} custom-call(bf16[128,640]{1,0:T(8,128)(2,1)S(1)} %get-tuple-element.15.src_ref), custom_call_target="tpu_custom_call" | custom-call | tf_op jit(solution)/shard_map/pallas_call | solution.py:225
  51.9 1.9 convolution_convert_fusion
  53.9 0.9 convolution_convert_fusion.1
  54.8 0.2 convolution_convert_fusion.3
  55.1 0.2 copy.54
  55.3 0.8 fusion.5
  56.2 1.8 fusion.120
  58.0 0.6 fusion.20
  58.6 0.7 copy-done.8
  59.2 1.6 bitcast_convert_fusion
  60.9 0.5 convolution_bitcast_fusion
  61.4 1.5 fusion.8
  62.9 1.0 convolution_convert_fusion.5
  63.9 0.5 convolution_bitcast_fusion.1
  64.5 0.2 fusion.31
  64.8 2.1 fusion.40
  66.9 0.8 copy.41
  67.7 0.2 pad_maximum_fusion.1
  67.9 1.9 copy.55
  69.8 3.2 %copy.40.src_ref = bf16[8,128,1024]{2,1,0:T(8,128)(2,1)S(1)} copy(bf16[8,128,1024]{1,0,2:T(8,128)(2,1)} %bitcast.263) | data formatting | bytes 4194304 | tf_op jit(solution)/shard_map/convert_element_type | solution.py:345
  73.1 35.7 %shard_map.146 = bf16[8,128,1024]{2,1,0:T(8,128)(2,1)S(1)} custom-call(bf16[8,128,1024]{2,1,0:T(8,128)(2,1)S(1)} %copy.40.src_ref), custom_call_target="tpu_custom_call" | custom-call | tf_op jit(solution)/shard_map/pallas_call | solution.py:225
  108.8 0.3 convert_reduce_fusion
  109.2 0.6 slice-done
  110.0 1.4 convolution_add_fusion.1
  111.4 2.0 multiply_reduce_fusion
  113.6 0.4 fusion.121
  114.0 0.9 convolution_bitcast_fusion.6
  114.9 0.9 fusion.73
  115.8 0.7 fusion.119
  116.5 0.3 convolution_bitcast_fusion.3
  116.8 0.3 convolution_bitcast_fusion.4
  117.1 0.3 convolution_bitcast_fusion.5
  117.5 0.2 convolution_bitcast_fusion.8
  117.7 0.2 convolution_bitcast_fusion.7
  117.9 0.2 convolution_bitcast_fusion.9
  118.3 0.9 copy.56
  119.2 3.0 %collective-permute-start.2 = (bf16[1,64,1]{2,1,0:T(8,128)(2,1)}, bf16[1,64,1]{2,1,0:T(8,128)(2,1)S(1)}, u32[]{:S(2)}, u32[]{:S(2)}) collective-permute-start(bf16[1,64,1]{2,1,0:T(8,128)(2,1)} %get-tuple-element.18), channel_id=1, source_target_pairs={{1,0},{2,1},{3,2},{4,3},{5,4},{6,5},{7,6},{8,7},{9,8},{10,9},{11,1... | collective-permute-start | bytes 392 | tf_op jit(solution)/shard_map/ppermute | solution.py:28
  122.2 3.2 %collective-permute-start.3 = (bf16[1,64,1]{2,1,0:T(8,128)(2,1)}, bf16[1,64,1]{2,1,0:T(8,128)(2,1)S(1)}, u32[]{:S(2)}, u32[]{:S(2)}) collective-permute-start(bf16[1,64,1]{2,1,0:T(8,128)(2,1)} %get-tuple-element.19), channel_id=1, source_target_pairs={{0,1},{1,2},{2,3},{3,4},{4,5},{5,6},{6,7},{7,8},{8,9},{9,10},{10,1... | collective-permute-start | bytes 392 | tf_op jit(solution)/shard_map/ppermute | solution.py:26
  125.4 1.2 convolution_bitcast_fusion.2
  126.7 2.4 pad_maximum_fusion
  129.1 4.9 %reshape_reshape.3 = f32[2,2,2,2,2,2,2,2,2,8,256]{10,9,8,7,6,5,4,3,2,1,0:T(8,128)} reshape(f32[4,512,512]{2,1,0:T(8,128)} %pad_maximum_fusion) | data formatting | bytes 8388608 | tf_op jit(solution)/shard_map/reshape;reshape | solution.py:96
  134.0 4.9 %copy.43 = f32[2,2,2,2,2,2,2,2,2,8,256]{10,9,7,8,1,5,2,6,3,0,4:T(8,128)} copy(f32[2,2,2,2,2,2,2,2,2,8,256]{10,9,8,7,6,5,4,3,2,1,0:T(8,128)} %reshape_reshape.3) | data formatting | bytes 8388608 | tf_op jit(solution)/shard_map/reshape;reshape | solution.py:96
  138.9 0.2 fusion.69
  139.1 0.2 fusion.24
  139.4 2.4 fusion.28
  141.8 1.0 fusion.33
  143.1 2.2 copy-done.1
  145.3 123.3 %shard_map.147 = (f32[8,256]{1,0:T(8,128)S(1)}, f32[184,256]{1,0:T(8,128)S(1)}) custom-call(f32[4096,256]{1,0:T(8,128)S(1)} %bitcast.259, f32[184,256]{1,0:T(8,128)S(1)} %reshape.392.small_ref), custom_call_target="tpu_custom_call" | custom-call | tf_op jit(solution)/shard_map/pallas_call | solution.py:170
  268.7 0.5 slice.150
  269.3 0.6 slice.153
  270.1 0.6 copy.57
  270.7 0.7 slice.133
  271.3 0.7 reshape.396
  272.0 0.7 reshape.395
  (93 shorter events, 2.6 us)
Async XLA Ops:
  0.6 21.3 %copy-start = (f32[64,512]{1,0:T(8,128)S(1)}, f32[64,512]{1,0:T(8,128)}, u32[]{:S(2)}) copy-start(f32[64,512]{1,0:T(8,128)} %param.17) | copy-start | bytes 393220
  1.9 4.6 %copy-start.15 = (f32[64,128,4]{1,2,0:T(4,128)}, f32[64,128,4]{1,2,0:T(4,128)S(1)}, u32[]{:S(2)}) copy-start(f32[64,128,4]{1,2,0:T(4,128)S(1)} %copy.35) | copy-start | bytes 393220
  1.9 18.2 %copy-start.6 = (bf16[4,512,512]{2,1,0:T(8,128)(2,1)S(1)}, bf16[4,512,512]{2,1,0:T(8,128)(2,1)}, u32[]{:S(2)}) copy-start(bf16[4,512,512]{2,1,0:T(8,128)(2,1)} %param.19) | copy-start | bytes 6291460
  1.9 18.2 %copy-start.11 = (bf16[1,128,512]{2,1,0:T(8,128)(2,1)S(1)}, bf16[1,128,512]{2,1,0:T(8,128)(2,1)}, u32[]{:S(2)}) copy-start(bf16[1,128,512]{2,1,0:T(8,128)(2,1)} %param.13) | copy-start | bytes 393220
  1.9 18.9 %copy-start.13 = (f32[3,64,64]{2,1,0:T(8,128)S(1)}, f32[3,64,64]{2,1,0:T(8,128)}, u32[]{:S(2)}) copy-start(f32[3,64,64]{2,1,0:T(8,128)} %param.16) | copy-start | bytes 147460
  1.9 19.2 %copy-start.23 = (bf16[1,128]{1,0:T(2,128)(2,1)S(1)}, bf16[1,128]{1,0:T(2,128)(2,1)}, u32[]{:S(2)}) copy-start(bf16[1,128]{1,0:T(2,128)(2,1)} %param.11) | copy-start | bytes 772
  6.5 16.1 %copy-start.21 = (f32[512]{0:T(512)S(1)}, f32[512]{0:T(512)}, u32[]{:S(2)}) copy-start(f32[512]{0:T(512)} %param.18) | copy-start | bytes 6148
  6.5 15.1 %collective-permute-start = (f32[1,64,1]{2,1,0:T(8,128)S(1)}, f32[1,64,1]{2,1,0:T(8,128)S(1)}, u32[]{:S(2)}, u32[]{:S(2)}) collective-permute-start(f32[1,64,1]{2,1,0:T(8,128)S(1)} %get-tuple-element.16), channel_id=1, source_target_pairs={{0,1},{1,2},{2,3},{3,4},{4,5},{5,6},{6,7},{7,8},{8,9},{9,10},{10,1... | collective-permute-start | bytes 776 | tf_op jit(solution)/shard_map/ppermute | solution.py:26
  12.3 9.0 %collective-permute-start.1 = (f32[1,64,1]{2,1,0:T(8,128)S(1)}, f32[1,64,1]{2,1,0:T(8,128)S(1)}, u32[]{:S(2)}, u32[]{:S(2)}) collective-permute-start(f32[1,64,1]{2,1,0:T(8,128)S(1)} %get-tuple-element.17), channel_id=1, source_target_pairs={{1,0},{2,1},{3,2},{4,3},{5,4},{6,5},{7,6},{8,7},{9,8},{10,9},{11,1... | collective-permute-start | bytes 776 | tf_op jit(solution)/shard_map/ppermute | solution.py:28
  21.4 1.1 copy-start.19
  21.7 0.8 copy-start.17
  51.9 2.0 copy-start.7
  58.0 1.3 copy-start.8
  61.4 3.2 %copy-start.2 = (f32[1,1152,8,64]{1,3,2,0:T(8,128)}, f32[1,1152,8,64]{1,3,2,0:T(8,128)S(1)}, u32[]{:S(2)}) copy-start(f32[1,1152,8,64]{1,3,2,0:T(8,128)S(1)} %convolution_bitcast_fusion) | copy-start | bytes 7077892
  63.9 0.9 copy-start.4
  108.8 1.0 slice-start
  108.8 1.1 copy-start.9
  108.8 1.2 copy-start.10
  109.9 3.5 %copy-start.12 = (bf16[1,128,512]{2,1,0:T(8,128)(2,1)S(1)}, bf16[1,128,512]{2,1,0:T(8,128)(2,1)}, u32[]{:S(2)}) copy-start(bf16[1,128,512]{2,1,0:T(8,128)(2,1)} %param.13) | copy-start | bytes 393220
  113.4 3.7 %copy-start.5 = (bf16[8,64,128]{2,1,0:T(8,128)(2,1)S(1)}, bf16[8,64,128]{2,1,0:T(8,128)(2,1)}, u32[]{:S(2)}) copy-start(bf16[8,64,128]{2,1,0:T(8,128)(2,1)} %copy-done.4) | copy-start | bytes 393220
  114.9 2.8 %copy-start.20 = (f32[1,64,1]{2,1,0:T(8,128)S(1)}, f32[1,64,1]{2,1,0:T(8,128)}, u32[]{:S(2)}) copy-start(f32[1,64,1]{2,1,0:T(8,128)} %copy-done.19) | copy-start | bytes 772
  116.5 1.4 copy-start.18
  119.2 19.9 %collective-permute-start.2 = (bf16[1,64,1]{2,1,0:T(8,128)(2,1)}, bf16[1,64,1]{2,1,0:T(8,128)(2,1)S(1)}, u32[]{:S(2)}, u32[]{:S(2)}) collective-permute-start(bf16[1,64,1]{2,1,0:T(8,128)(2,1)} %get-tuple-element.18), channel_id=1, source_target_pairs={{1,0},{2,1},{3,2},{4,3},{5,4},{6,5},{7,6},{8,7},{9,8},{10,9},{11,1... | collective-permute-start | bytes 392 | tf_op jit(solution)/shard_map/ppermute | solution.py:28
  122.2 16.7 %collective-permute-start.3 = (bf16[1,64,1]{2,1,0:T(8,128)(2,1)}, bf16[1,64,1]{2,1,0:T(8,128)(2,1)S(1)}, u32[]{:S(2)}, u32[]{:S(2)}) collective-permute-start(bf16[1,64,1]{2,1,0:T(8,128)(2,1)} %get-tuple-element.19), channel_id=1, source_target_pairs={{0,1},{1,2},{2,3},{3,4},{4,5},{5,6},{6,7},{7,8},{8,9},{9,10},{10,1... | collective-permute-start | bytes 392 | tf_op jit(solution)/shard_map/ppermute | solution.py:26
  134.0 4.9 %copy-start.14 = (f32[3,64,64]{2,1,0:T(8,128)S(1)}, f32[3,64,64]{2,1,0:T(8,128)}, u32[]{:S(2)}) copy-start(f32[3,64,64]{2,1,0:T(8,128)} %param.16) | copy-start | bytes 147460
  134.0 5.4 %copy-start.3 = (f32[64,64,128]{2,0,1:T(8,128)S(1)}, f32[64,64,128]{2,0,1:T(8,128)}, u32[]{:S(2)}) copy-start(f32[64,64,128]{2,0,1:T(8,128)} %get-tuple-element.23) | copy-start | bytes 6291460
  134.0 5.4 %copy-start.16 = (f32[64,128,4]{1,2,0:T(4,128)S(1)}, f32[64,128,4]{1,2,0:T(4,128)}, u32[]{:S(2)}) copy-start(f32[64,128,4]{1,2,0:T(4,128)} %copy-done.15) | copy-start | bytes 393220
  134.0 5.4 %copy-start.24 = (f32[64]{0:T(128)S(1)}, f32[64]{0:T(128)}, u32[]{:S(2)}) copy-start(f32[64]{0:T(128)} %param.15) | copy-start | bytes 772
  141.8 1.1 copy-start.22
  143.1 2.2 copy-start.1

commit v9 on v8

--- a/solution.py
+++ b/solution.py
@@ -340,28 +340,23 @@
     )
     key_sum = key_part[:, 0:local]
     value_sum = value_part[:, 0:local]
-    parts = jnp.concatenate(
-        [key_part[0, local:], value_part[0, local:]], axis=1
-    ).astype(jnp.bfloat16).reshape(len(offsets) - 1, local, 2 * width)
-    back = jnp.sum(exchange(parts, list(offsets[1:]), True, 2).astype(jnp.float32), axis=0)
-    key_sum = key_part[0, :local].reshape(local, width) + back[:, :width]
-    value_sum = value_part[0, :local].reshape(local, width) + back[:, width:]
-    grad_keys = key_sum.astype(jnp.bfloat16).reshape(sims, local, width)
-    grad_values = value_sum.astype(jnp.bfloat16).reshape(sims, local, width)
+    key_rows = key_part[0].reshape(len(offsets) * local, width).astype(jnp.bfloat16)
+    value_rows = value_part[0].reshape(len(offsets) * local, width).astype(jnp.bfloat16)
     term_query = jnp.einsum("std,ste->de", normed, grad_query, preferred_element_type=jnp.float32)
-    term_keys = jnp.einsum("std,ste->de", normed, grad_keys, preferred_element_type=jnp.float32)
-    term_values = jnp.einsum("std,ste->de", normed, grad_values, preferred_element_type=jnp.float32)
+    term_keys = jnp.einsum("td,te->de", normed_cat[0], key_rows, preferred_element_type=jnp.float32)
+    term_values = jnp.einsum("td,te->de", normed_cat[0], value_rows, preferred_element_type=jnp.float32)
     term_output = jnp.einsum("std,ste->de", attended, cotangent, preferred_element_type=jnp.float32)
     flat_terms = jnp.stack([term_query, term_keys, term_values, term_output]).reshape(-1)
+    contrib = jnp.einsum("te,de->td", key_rows, attn_weight[1], preferred_element_type=jnp.float32)
+    contrib = contrib + jnp.einsum(
+        "te,de->td", value_rows, attn_weight[2], preferred_element_type=jnp.float32
+    )
+    parts = contrib[local:].astype(jnp.bfloat16).reshape(len(offsets) - 1, local, width)
+    back = jnp.sum(exchange(parts, list(offsets[1:]), True, 2).astype(jnp.float32), axis=0)
     grad_normed = jnp.einsum(
         "ste,de->std", grad_query, attn_weight[0], preferred_element_type=jnp.float32
     )
-    grad_normed = grad_normed + jnp.einsum(
-        "ste,de->std", grad_keys, attn_weight[1], preferred_element_type=jnp.float32
-    )
-    grad_normed = grad_normed + jnp.einsum(
-        "ste,de->std", grad_values, attn_weight[2], preferred_element_type=jnp.float32
-    )
+    grad_normed = grad_normed + (contrib[:local] + back)[None]
     term_gain = jnp.sum(grad_normed * wide * inverse, axis=(0, 1))
     scaled = grad_normed * norm_gain
     grad_embedded = (

time: 274 us -> 250 us (0.912)
  the two profiles are of different devices: /device:TPU:59 before, /device:TPU:12 now
where the time goes in v9:
time: 250 us; the launch traced here: 249 us
  Pallas kernels  158 us (63%)
  matrix products  31.6 us (13%)
  local copies, waits for them, and re-layouts  22.9 us (9%)
  starting transfers between devices  21.7 us (9%)
  other arithmetic  9.69 us (4%)
  waiting for transfers between devices  2.67 us (1%)
    pallas_call x1, Pallas kernels, butterfly_kernel(): pl.pallas_call(functools.partial(butterfly_body, order, small_order, step...  106 us
    pallas_call x2, Pallas kernels, exchange(): pl.pallas_call(functools.partial(exchange_body, shifts, per_slot), out_sh...  52.5 us
    ppermute x2, starting transfers between devices, extended(): lax.ppermute(head, axis, [((i + 1) % count, i) for i in range(count)])  15.6 us
    another operation x2, local copies, waits for them, and re-layouts, butterfly_sum(): cells = flat.reshape((2,) * total_bits + (chunk // LANES, LANES))  9.88 us
    ppermute x2, starting transfers between devices, extended(): lax.ppermute(tail, axis, [(i, (i + 1) % count) for i in range(count)])  6.09 us
    unnamed x70, local copies, waits for them, and re-layouts  5.26 us
  transfers between devices with their start and end apart: 4, of which 1 were waited for; matrix products, arithmetic and copies ran while one was open for 7% of the time, Pallas kernels for 0%

profile of v9, /device:TPU:12, one launch (start us, length us, event | category | flops | bytes accessed | tf_op | source)
XLA Modules:
  0.0 249.1 jit_solution(12981698119659774008)
XLA Ops:
  0.6 1.0 convert_element_type.107
  1.9 4.5 %fusion.16 = (f32[64,128]{1,0:T(8,128)S(1)}, f32[64,64,128]{2,0,1:T(8,128)}) fusion(f32[64]{0:T(128)} %param.15, f32[64,128,4]{1,2,0:T(4,128)S(1)} %copy.25, f32[4,64]{1,0:T(4,128)} %param.14), kind=kOutput, calls=%fused_computation.29 | convolution fusion | flops 28303360 | bytes 2262272 | tf_op jit(solution)/shard_map/shtk,kc->shct/dot_general | solution.py:265
  6.5 10.9 %collective-permute-start.1 = (f32[1,64,1]{2,1,0:T(8,128)S(1)}, f32[1,64,1]{2,1,0:T(8,128)S(1)}, u32[]{:S(2)}, u32[]{:S(2)}) collective-permute-start(f32[1,64,1]{2,1,0:T(8,128)S(1)} %get-tuple-element.15), channel_id=1, source_target_pairs={{1,0},{2,1},{3,2},{4,3},{5,4},{6,5},{7,6},{8,7},{9,8},{10,9},{11,1... | collective-permute-start | bytes 776 | tf_op jit(solution)/shard_map/ppermute | solution.py:28
  17.4 1.9 collective-permute-start
  20.2 1.4 convolution_convert_fusion.4
  21.6 1.1 fusion.33
  22.7 0.2 fusion.71
  23.3 0.3 fusion.67
  23.5 2.7 %collective-permute-done = f32[1,64,1]{2,1,0:T(8,128)S(1)} collective-permute-done((f32[1,64,1]{2,1,0:T(8,128)S(1)}, f32[1,64,1]{2,1,0:T(8,128)S(1)}, u32[]{:S(2)}, u32[]{:S(2)}) %collective-permute-start) | collective-permute-done | bytes 288 | tf_op jit(solution)/shard_map/ppermute | solution.py:26
  26.2 0.3 fusion.26
  26.5 0.5 multiply_reduce_fusion.2
  27.0 0.5 multiply_multiply_fusion
  27.7 27.2 %shard_map.145 = bf16[8,128,640]{2,1,0:T(8,128)(2,1)S(1)} custom-call(bf16[128,640]{1,0:T(8,128)(2,1)S(1)} %get-tuple-element.13.src_ref), custom_call_target="tpu_custom_call" | custom-call | tf_op jit(solution)/shard_map/pallas_call | solution.py:225
  54.8 0.2 pad_maximum_fusion.1
  55.0 0.9 convolution_convert_fusion.3
  56.0 0.9 convolution_convert_fusion.5
  56.9 1.9 convolution_convert_fusion.2
  58.8 0.2 copy.41
  59.0 1.0 copy.27
  60.0 0.8 fusion.5
  61.0 1.8 fusion.116
  62.8 0.6 fusion.20
  63.3 0.7 copy-done.5
  64.0 1.6 bitcast_convert_fusion
  65.7 0.5 convolution_convert_fusion
  66.2 1.5 fusion.8
  67.7 0.5 convolution_convert_fusion.1
  68.2 1.0 convolution_convert_fusion.7
  69.2 0.6 copy-done.3
  69.8 0.8 fusion.40
  70.6 0.8 convolution_add_fusion
  71.6 25.3 %shard_map.146 = bf16[8,128,512]{2,1,0:T(8,128)(2,1)S(1)} custom-call(bf16[8,128,512]{2,1,0:T(8,128)(2,1)S(1)} %bitcast.252), custom_call_target="tpu_custom_call" | custom-call | tf_op jit(solution)/shard_map/pallas_call | solution.py:225
  97.1 0.9 multiply_reduce_fusion
  98.2 0.3 convolution_bitcast_fusion.4
  98.5 0.4 fusion.117
  98.9 0.7 fusion.115
  99.6 1.5 fusion.69
  101.1 1.0 convolution_bitcast_fusion.3
  102.2 1.9 convolution_bitcast_fusion.1
  104.1 1.9 convolution_bitcast_fusion
  105.9 0.7 copy.42
  106.7 0.2 convolution_bitcast_fusion.6
  106.8 0.2 convolution_bitcast_fusion.7
  107.1 0.2 convolution_bitcast_fusion.5
  107.4 0.7 pad_maximum_fusion.2
  108.0 1.6 reshape.380
  109.6 4.2 %collective-permute-start.3 = (bf16[1,64,1]{2,1,0:T(8,128)(2,1)}, bf16[1,64,1]{2,1,0:T(8,128)(2,1)}, u32[]{:S(2)}, u32[]{:S(2)}) collective-permute-start(bf16[1,64,1]{2,1,0:T(8,128)(2,1)} %get-tuple-element.17), channel_id=1, source_target_pairs={{0,1},{1,2},{2,3},{3,4},{4,5},{5,6},{6,7},{7,8},{8,9},{9,10},{10,1... | collective-permute-start | bytes 392 | tf_op jit(solution)/shard_map/ppermute | solution.py:26
  113.8 4.7 %collective-permute-start.2 = (bf16[1,64,1]{2,1,0:T(8,128)(2,1)}, bf16[1,64,1]{2,1,0:T(8,128)(2,1)}, u32[]{:S(2)}, u32[]{:S(2)}) collective-permute-start(bf16[1,64,1]{2,1,0:T(8,128)(2,1)} %get-tuple-element.16), channel_id=1, source_target_pairs={{1,0},{2,1},{3,2},{4,3},{5,4},{6,5},{7,6},{8,7},{9,8},{10,9},{11,1... | collective-permute-start | bytes 392 | tf_op jit(solution)/shard_map/ppermute | solution.py:28
  118.5 0.3 convolution_bitcast_fusion.2
  118.8 2.4 pad_maximum_fusion
  121.2 5.0 %reshape_reshape.3 = f32[2,2,2,2,2,2,2,2,2,8,256]{10,9,8,7,6,5,4,3,2,1,0:T(8,128)} reshape(f32[4,512,512]{2,1,0:T(8,128)} %pad_maximum_fusion) | data formatting | bytes 8388608 | tf_op jit(solution)/shard_map/reshape;reshape | solution.py:96
  126.2 4.9 %copy.30 = f32[2,2,2,2,2,2,2,2,2,8,256]{10,9,7,8,1,5,2,6,3,0,4:T(8,128)} copy(f32[2,2,2,2,2,2,2,2,2,8,256]{10,9,8,7,6,5,4,3,2,1,0:T(8,128)} %reshape_reshape.3) | data formatting | bytes 8388608 | tf_op jit(solution)/shard_map/reshape;reshape | solution.py:96
  131.1 1.0 fusion.65
  132.1 0.9 fusion.24
  133.0 1.0 fusion.31
  134.0 2.4 fusion.28
  136.8 2.2 copy-done.1
  139.0 106.0 %shard_map.147 = (f32[8,256]{1,0:T(8,128)S(1)}, f32[184,256]{1,0:T(8,128)S(1)}) custom-call(f32[4096,256]{1,0:T(8,128)S(1)} %bitcast.251, f32[184,256]{1,0:T(8,128)S(1)} %reshape.382.small_ref), custom_call_target="tpu_custom_call" | custom-call | tf_op jit(solution)/shard_map/pallas_call | solution.py:170
  245.3 0.7 slice.132
  245.9 0.5 slice.129
  246.5 0.7 reshape.386
  247.1 0.7 reshape.385
  247.9 0.6 copy.43
  248.5 0.7 slice.116
  (98 shorter events, 2.1 us)
Async XLA Ops:
  0.6 25.8 %copy-start = (f32[64,512]{1,0:T(8,128)S(1)}, f32[64,512]{1,0:T(8,128)}, u32[]{:S(2)}) copy-start(f32[64,512]{1,0:T(8,128)} %param.17) | copy-start | bytes 393220
  1.9 4.5 %copy-start.19 = (f32[64,128,4]{1,2,0:T(4,128)}, f32[64,128,4]{1,2,0:T(4,128)S(1)}, u32[]{:S(2)}) copy-start(f32[64,128,4]{1,2,0:T(4,128)S(1)} %copy.25) | copy-start | bytes 393220
  1.9 18.4 %copy-start.10 = (bf16[1,128,512]{2,1,0:T(8,128)(2,1)S(1)}, bf16[1,128,512]{2,1,0:T(8,128)(2,1)}, u32[]{:S(2)}) copy-start(bf16[1,128,512]{2,1,0:T(8,128)(2,1)} %param.13) | copy-start | bytes 393220
  1.9 20.8 %copy-start.14 = (f32[3,64,64]{2,1,0:T(8,128)S(1)}, f32[3,64,64]{2,1,0:T(8,128)}, u32[]{:S(2)}) copy-start(f32[3,64,64]{2,1,0:T(8,128)} %param.16) | copy-start | bytes 147460
  1.9 21.1 %copy-start.30 = (bf16[1,128]{1,0:T(2,128)(2,1)S(1)}, bf16[1,128]{1,0:T(2,128)(2,1)}, u32[]{:S(2)}) copy-start(bf16[1,128]{1,0:T(2,128)(2,1)} %param.11) | copy-start | bytes 772
  6.4 16.6 %copy-start.16 = (f32[64,128]{1,0:T(8,128)}, f32[64,128]{1,0:T(8,128)S(1)}, u32[]{:S(2)}) copy-start(f32[64,128]{1,0:T(8,128)S(1)} %get-tuple-element.20) | copy-start | bytes 98308
  6.4 21.1 %copy-start.26 = (f32[512]{0:T(512)S(1)}, f32[512]{0:T(512)}, u32[]{:S(2)}) copy-start(f32[512]{0:T(512)} %param.18) | copy-start | bytes 6148
  6.5 16.8 %collective-permute-start.1 = (f32[1,64,1]{2,1,0:T(8,128)S(1)}, f32[1,64,1]{2,1,0:T(8,128)S(1)}, u32[]{:S(2)}, u32[]{:S(2)}) collective-permute-start(f32[1,64,1]{2,1,0:T(8,128)S(1)} %get-tuple-element.15), channel_id=1, source_target_pairs={{1,0},{2,1},{3,2},{4,3},{5,4},{6,5},{7,6},{8,7},{9,8},{10,9},{11,1... | collective-permute-start | bytes 776 | tf_op jit(solution)/shard_map/ppermute | solution.py:28
  17.4 8.8 %collective-permute-start = (f32[1,64,1]{2,1,0:T(8,128)S(1)}, f32[1,64,1]{2,1,0:T(8,128)S(1)}, u32[]{:S(2)}, u32[]{:S(2)}) collective-permute-start(f32[1,64,1]{2,1,0:T(8,128)S(1)} %get-tuple-element.14), channel_id=1, source_target_pairs={{0,1},{1,2},{2,3},{3,4},{4,5},{5,6},{6,7},{7,8},{8,9},{9,10},{10,1... | collective-permute-start | bytes 776 | tf_op jit(solution)/shard_map/ppermute | solution.py:26
  23.3 4.3 %copy-start.22 = (f32[1,64,1]{2,1,0:T(8,128)}, f32[1,64,1]{2,1,0:T(8,128)S(1)}, u32[]{:S(2)}) copy-start(f32[1,64,1]{2,1,0:T(8,128)S(1)} %collective-permute-done.1) | copy-start | bytes 772
  26.2 28.8 %copy-start.24 = (f32[1,64,1]{2,1,0:T(8,128)}, f32[1,64,1]{2,1,0:T(8,128)S(1)}, u32[]{:S(2)}) copy-start(f32[1,64,1]{2,1,0:T(8,128)S(1)} %collective-permute-done) | copy-start | bytes 772
  27.5 70.5 %copy-start.28 = (f32[128]{0:T(128)}, f32[128]{0:T(128)S(1)}, u32[]{:S(2)}) copy-start(f32[128]{0:T(128)S(1)} %get-tuple-element.19) | copy-start | bytes 1540
  27.7 27.3 %copy-start.2 = (bf16[4,512,512]{2,1,0:T(8,128)(2,1)S(1)}, bf16[4,512,512]{2,1,0:T(8,128)(2,1)}, u32[]{:S(2)}) copy-start(bf16[4,512,512]{2,1,0:T(8,128)(2,1)} %param.19) | copy-start | bytes 6291460
  60.0 0.9 copy-start.8
  62.7 1.3 copy-start.5
  68.2 1.6 copy-start.3
  71.6 26.4 %copy-start.11 = (bf16[1,128,512]{2,1,0:T(8,128)(2,1)S(1)}, bf16[1,128,512]{2,1,0:T(8,128)(2,1)}, u32[]{:S(2)}) copy-start(bf16[1,128,512]{2,1,0:T(8,128)(2,1)} %param.13) | copy-start | bytes 393220
  71.6 26.4 %copy-start.31 = (f32[128]{0:T(128)S(1)}, f32[128]{0:T(128)}, u32[]{:S(2)}) copy-start(f32[128]{0:T(128)} %get-tuple-element.18) | copy-start | bytes 1540
  97.1 4.0 %copy-start.27 = (f32[512]{0:T(512)S(1)}, f32[512]{0:T(512)}, u32[]{:S(2)}) copy-start(f32[512]{0:T(512)} %param.18) | copy-start | bytes 6148
  104.0 2.6 %copy-start.17 = (f32[64,128]{1,0:T(8,128)S(1)}, f32[64,128]{1,0:T(8,128)}, u32[]{:S(2)}) copy-start(f32[64,128]{1,0:T(8,128)} %copy-done.16) | copy-start | bytes 98308
  104.0 2.8 %copy-start.25 = (f32[1,64,1]{2,1,0:T(8,128)S(1)}, f32[1,64,1]{2,1,0:T(8,128)}, u32[]{:S(2)}) copy-start(f32[1,64,1]{2,1,0:T(8,128)} %copy-done.24) | copy-start | bytes 772
  104.0 3.1 %copy-start.23 = (f32[1,64,1]{2,1,0:T(8,128)S(1)}, f32[1,64,1]{2,1,0:T(8,128)}, u32[]{:S(2)}) copy-start(f32[1,64,1]{2,1,0:T(8,128)} %copy-done.22) | copy-start | bytes 772
  104.0 14.4 %copy-start.9 = (bf16[1,128,8,64]{1,3,2,0:T(8,128)(2,1)S(1)}, bf16[1,128,8,64]{1,3,2,0:T(8,128)(2,1)}, u32[]{:S(2)}) copy-start(bf16[1,128,8,64]{1,3,2,0:T(8,128)(2,1)} %get-tuple-element.26) | copy-start | bytes 393220
  104.0 14.4 %copy-start.12 = (bf16[1,128,512]{2,1,0:T(8,128)(2,1)S(1)}, bf16[1,128,512]{2,1,0:T(8,128)(2,1)}, u32[]{:S(2)}) copy-start(bf16[1,128,512]{2,1,0:T(8,128)(2,1)} %param.13) | copy-start | bytes 393220
  105.9 12.8 %copy-start.6 = (f32[1,512,512]{2,1,0:T(8,128)S(1)}, f32[1,512,512]{2,1,0:T(8,128)}, u32[]{:S(2)}) copy-start(f32[1,512,512]{2,1,0:T(8,128)} %convolution_bitcast_fusion.1) | copy-start | bytes 3145732
  107.3 11.4 %copy-start.7 = (f32[1,512,512]{2,1,0:T(8,128)S(1)}, f32[1,512,512]{2,1,0:T(8,128)}, u32[]{:S(2)}) copy-start(f32[1,512,512]{2,1,0:T(8,128)} %convolution_bitcast_fusion) | copy-start | bytes 3145732
  109.6 21.5 %collective-permute-start.3 = (bf16[1,64,1]{2,1,0:T(8,128)(2,1)}, bf16[1,64,1]{2,1,0:T(8,128)(2,1)}, u32[]{:S(2)}, u32[]{:S(2)}) collective-permute-start(bf16[1,64,1]{2,1,0:T(8,128)(2,1)} %get-tuple-element.17), channel_id=1, source_target_pairs={{0,1},{1,2},{2,3},{3,4},{4,5},{5,6},{6,7},{7,8},{8,9},{9,10},{10,1... | collective-permute-start | bytes 392 | tf_op jit(solution)/shard_map/ppermute | solution.py:26
  113.8 18.3 %collective-permute-start.2 = (bf16[1,64,1]{2,1,0:T(8,128)(2,1)}, bf16[1,64,1]{2,1,0:T(8,128)(2,1)}, u32[]{:S(2)}, u32[]{:S(2)}) collective-permute-start(bf16[1,64,1]{2,1,0:T(8,128)(2,1)} %get-tuple-element.16), channel_id=1, source_target_pairs={{1,0},{2,1},{3,2},{4,3},{5,4},{6,5},{7,6},{8,7},{9,8},{10,9},{11,1... | collective-permute-start | bytes 392 | tf_op jit(solution)/shard_map/ppermute | solution.py:28
  126.2 4.9 %copy-start.15 = (f32[3,64,64]{2,1,0:T(8,128)S(1)}, f32[3,64,64]{2,1,0:T(8,128)}, u32[]{:S(2)}) copy-start(f32[3,64,64]{2,1,0:T(8,128)} %param.16) | copy-start | bytes 147460
  126.2 5.9 %copy-start.21 = (f32[128,64]{0,1:T(8,128)S(1)}, f32[128,64]{0,1:T(8,128)}, u32[]{:S(2)}) copy-start(f32[128,64]{0,1:T(8,128)} %fusion.69) | copy-start | bytes 98308
  126.2 6.9 %copy-start.4 = (f32[64,64,128]{2,0,1:T(8,128)S(1)}, f32[64,64,128]{2,0,1:T(8,128)}, u32[]{:S(2)}) copy-start(f32[64,64,128]{2,0,1:T(8,128)} %get-tuple-element.21) | copy-start | bytes 6291460
  126.2 6.9 %copy-start.32 = (f32[64]{0:T(128)S(1)}, f32[64]{0:T(128)}, u32[]{:S(2)}) copy-start(f32[64]{0:T(128)} %param.15) | copy-start | bytes 772
  131.1 2.9 %copy-start.20 = (f32[64,128,4]{1,2,0:T(4,128)S(1)}, f32[64,128,4]{1,2,0:T(4,128)}, u32[]{:S(2)}) copy-start(f32[64,128,4]{1,2,0:T(4,128)} %copy-done.19) | copy-start | bytes 393220
  134.0 2.5 %copy-start.13 = (f32[8,4,8,128]{3,1,2,0:T(4,128)S(1)}, f32[8,4,8,128]{3,1,2,0:T(4,128)}, u32[]{:S(2)}) copy-start(f32[8,4,8,128]{3,1,2,0:T(4,128)} %copy.42) | copy-start | bytes 393220
  134.0 2.5 %copy-start.18 = (f32[12288]{0:T(1024)S(1)}, f32[12288]{0:T(1024)}, u32[]{:S(2)}) copy-start(f32[12288]{0:T(1024)} %reshape.380) | copy-start | bytes 147460
  134.0 2.5 %copy-start.29 = (f32[512]{0:T(512)S(1)}, f32[512]{0:T(512)}, u32[]{:S(2)}) copy-start(f32[512]{0:T(512)} %get-tuple-element.10) | copy-start | bytes 6148
  136.8 2.2 copy-start.1
